TPU v7x, 32 devices: a whole 2x2x4 slice. The times are simulated.
32 devices in a mesh: dp: 4 (over z), row: 2 (over x), col: 4 (over y, core).
Axes of the slice: x: 2, y: 2, z: 4, core: 2. Of those that a mesh axis runs over, the one named last changes fastest.
Arguments:
- tokens: bfloat16 [2, 8192, 768], P(None, ('dp', 'row', 'col')), may hold values from -6 to 6
- cotangent: bfloat16 [2, 8192, 768], P(None, ('dp', 'row', 'col')), may hold values from -6 to 6
- doc_ids: int32 [2, 4, 2048], P(None, 'dp', ('row', 'col')), may hold values from 0 to 3, never falling along the last dimension, each value on 1 to 1024 neighbouring positions
- proj_weight: bfloat16 [5, 768, 384], P(None, 'row', 'col'), may hold values from -0.21875 to 0.21875
- out_weight: bfloat16 [768, 768], P('row', 'col'), may hold values from -0.625 to 0.625
- inner_weight: bfloat16 [2, 384, 1536], P('row', None, 'col'), may hold values from -0.3125 to 0.3125
- outer_weight: bfloat16 [2, 1536, 384], P('row', 'col'), may hold values from -0.15625 to 0.15625
- depth_weight: bfloat16 [9, 768], replicated, may hold values from -2 to 2
- proj_bias: bfloat16 [4, 384], replicated, may hold values from -3 to 3
- kernel_weight: bfloat16 [384, 54], replicated, may hold values from -0.3125 to 0.3125
- kernel_bias: bfloat16 [54], replicated, may hold values from -3 to 3
- out_bias: bfloat16 [768], replicated, may hold values from -2 to 2
- norm1_gain: bfloat16 [768], replicated, may hold values from 0.5 to 1.5
- norm1_shift: bfloat16 [768], replicated, may hold values from -2 to 2
- inner_bias: bfloat16 [3072], replicated, may hold values from -2 to 2
- outer_bias: bfloat16 [768], replicated, may hold values from -2 to 2
- norm2_gain: bfloat16 [768], replicated, may hold values from 0.5 to 1.5
- norm2_shift: bfloat16 [768], replicated, may hold values from -2 to 2
Outputs:
- output: bfloat16 [2, 8192, 768], P(None, ('dp', 'row', 'col'))
- tokens_grad: float32 [2, 8192, 768], P(None, ('dp', 'row', 'col'))
- proj_weight_grad: float32 [5, 768, 384], P(None, 'row', 'col')
- out_weight_grad: float32 [768, 768], P('row', 'col')
- inner_weight_grad: float32 [2, 384, 1536], P('row', None, 'col')
- outer_weight_grad: float32 [2, 1536, 384], P('row', 'col')
- depth_weight_grad: float32 [9, 768], replicated
- proj_bias_grad: float32 [4, 384], replicated
- kernel_weight_grad: float32 [384, 54], replicated
- kernel_bias_grad: float32 [54], replicated
- out_bias_grad: float32 [768], replicated
- norm1_gain_grad: float32 [768], replicated
- norm1_shift_grad: float32 [768], replicated
- inner_bias_grad: float32 [3072], replicated
- outer_bias_grad: float32 [768], replicated
- norm2_gain_grad: float32 [768], replicated
- norm2_shift_grad: float32 [768], replicated
Inputs may be any that keep to these rules, and one draw needn't show every extreme that they name: `doc_ids`: document numbers never fall along a sequence of 2048 tokens; each document has at most 1024 tokens, and one in every sequence has exactly that many.
All inputs are finite; a program needn't handle non-finite values.
Results may differ from a plain program's by a relative error of at most 0.018.
Values may be sent and summed in bfloat16 or wider, within the bound.
No kernel may reach another device: no remote copies, remote signals or barrier semaphores. Data moves between devices by JAX's collectives and lax.ppermute only.
A program may use at most 256 MiB of HBM per device.

v0:
```python
import jax
import jax.numpy as jnp
from jax import lax
from jax.sharding import PartitionSpec as P

HEADS = 6
HEAD = 64
KERNEL = 9
FF = 3072
ATT = 384


EPSILON = 1e-12
MASKED = -1e30


def padded(block, sides, width):
    for axis, dim in sides:
        count = lax.axis_size(axis)
        forward = [(i, i + 1) for i in range(count - 1)]
        backward = [(target, source) for source, target in forward]
        low = lax.ppermute(
            lax.slice_in_dim(block, block.shape[dim] - width, None, axis=dim), axis, forward
        )
        high = lax.ppermute(lax.slice_in_dim(block, 0, width, axis=dim), axis, backward)
        block = jnp.concatenate([low, block, high], axis=dim)
    return block


def norm_rows(values_in, norm_gain, norm_shift):
    row_mean = jnp.mean(values_in, axis=-1, keepdims=True)
    centred = values_in - row_mean
    row_var = jnp.mean(centred * centred, axis=-1, keepdims=True)
    return centred * lax.rsqrt(row_var + EPSILON) * norm_gain + norm_shift


def conv_softmax(logits, tap_mask):
    allowed = tap_mask[:, None, :]
    masked = jnp.where(allowed, logits, MASKED)
    row_top = jnp.max(masked, axis=-1, keepdims=True)
    exp_terms = jnp.where(allowed, jnp.exp(masked - row_top), 0.0)
    return exp_terms / jnp.sum(exp_terms, axis=-1, keepdims=True)


def gelu_exact(values_in):
    return jax.nn.gelu(values_in, approximate=False)


def fetch_weights(proj_weight, out_weight, inner_weight, outer_weight):
    gathered = (
        lax.all_gather(proj_weight[None], ("row", "col"), axis=0, tiled=True),
        lax.all_gather(out_weight[None], ("row", "col"), axis=0, tiled=True),
        lax.all_gather(inner_weight[None], ("row", "col"), axis=0, tiled=True),
        lax.all_gather(outer_weight[None], ("row", "col"), axis=0, tiled=True),
    )
    grid_rows = lax.axis_size("row")
    grid_cols = lax.axis_size("col")
    return tuple(
        (
            gathered_piece.reshape((grid_rows, grid_cols) + gathered_piece.shape[1:])
            for gathered_piece in gathered
        )
    )


def local(
    tokens,
    cotangent,
    doc_ids,
    proj_weight,
    out_weight,
    inner_weight,
    outer_weight,
    depth_weight,
    proj_bias,
    kernel_weight,
    kernel_bias,
    out_bias,
    norm1_gain,
    norm1_shift,
    inner_bias,
    outer_bias,
    norm2_gain,
    norm2_shift,
):
    micro_count, tokens_here, model_width = tokens.shape
    margin = KERNEL // 2
    grid_rows = lax.axis_size("row")
    grid_cols = lax.axis_size("col")
    score_scale = HEAD ** (-0.5)
    lowtype = jnp.bfloat16
    wide = jnp.float32
    depth_gain = depth_weight.astype(wide)
    bias_proj = proj_bias.astype(wide)
    bias_kernel = kernel_bias.astype(wide)
    bias_out = out_bias.astype(wide)
    gain_first = norm1_gain.astype(wide)
    shift_first = norm1_shift.astype(wide)
    bias_inner = inner_bias.astype(wide)
    bias_outer = outer_bias.astype(wide)
    gain_second = norm2_gain.astype(wide)
    shift_second = norm2_shift.astype(wide)
    doc_full = lax.all_gather(doc_ids[:, 0, :], ("row", "col"), axis=1, tiled=True)
    extended_all = padded(tokens, ((("row", "col"), 1),), margin)
    seq_start = lax.axis_index(("row", "col")) * tokens_here
    fetched = fetch_weights(proj_weight, out_weight, inner_weight, outer_weight)
    outputs = []
    token_grads = []
    grad_items = []
    for micro in range(micro_count):
        proj_full, out_full, inner_full, outer_full = fetched
        proj_tokens = proj_full[:, :, :4]
        proj_point = proj_full[:, :, 4]
        groups_here = inner_full.shape[2]
        own_rows = tokens[micro]
        extended = extended_all[micro]
        doc_seq = doc_full[micro]
        doc_padded = jnp.pad(doc_seq, (margin, margin), constant_values=-1)
        doc_ext = lax.dynamic_slice_in_dim(doc_padded, seq_start, tokens_here + 2 * margin)
        doc_own = doc_ext[margin : margin + tokens_here]
        tap_mask = jnp.stack(
            [doc_ext[offset : offset + tokens_here] == doc_own for offset in range(KERNEL)], axis=1
        )
        ext_wide = extended.astype(wide)
        shifted = [
            jnp.where(
                tap_mask[:, offset : offset + 1], ext_wide[offset : offset + tokens_here], 0.0
            )
            for offset in range(KERNEL)
        ]
        depthwise = sum((depth_gain[offset] * shifted[offset] for offset in range(KERNEL)))
        depth_low = depthwise.astype(lowtype)
        split_depth = depth_low.reshape(tokens_here, grid_rows, -1)
        split_tokens = own_rows.reshape(tokens_here, grid_rows, -1)
        mixed_proj = jnp.einsum(
            "tra,rcjab->jtcb", split_tokens, proj_tokens, preferred_element_type=wide
        ).reshape(4, tokens_here, ATT)
        query_low = (mixed_proj[0] + bias_proj[0]).astype(lowtype)
        key_low = mixed_proj[1].astype(lowtype)
        value_low = (mixed_proj[2] + bias_proj[1]).astype(lowtype)
        conv_value = (mixed_proj[3] + bias_proj[2]).astype(lowtype)
        rim_tokens = jnp.concatenate(
            [extended[:margin], extended[margin + tokens_here :]], axis=0
        ).reshape(2 * margin, grid_rows, -1)
        rim_value = (
            jnp.einsum(
                "tra,rcab->tcb", rim_tokens, proj_full[:, :, 3], preferred_element_type=wide
            ).reshape(2 * margin, ATT)
            + bias_proj[2]
        ).astype(lowtype)
        conv_ext = jnp.concatenate([rim_value[:margin], conv_value, rim_value[margin:]], axis=0)
        conv_heads = conv_ext.reshape(tokens_here + 2 * margin, HEADS, HEAD)
        key_conv = (
            jnp.einsum(
                "tra,rcab->tcb", split_depth, proj_point, preferred_element_type=wide
            ).reshape(tokens_here, ATT)
            + bias_proj[3]
        )
        conv_attn = (query_low.astype(wide) * key_conv).astype(lowtype)
        logits = (
            jnp.dot(conv_attn, kernel_weight, preferred_element_type=wide) + bias_kernel
        ).reshape(tokens_here, HEADS, KERNEL)
        conv_weights = conv_softmax(logits, tap_mask)
        conv_context = sum(
            (
                conv_weights[:, :, offset : offset + 1] * conv_heads[offset : offset + tokens_here]
                for offset in range(KERNEL)
            )
        )
        keys_all, values_all = (
            lax.all_gather(key_low, ("row", "col"), axis=0, tiled=True),
            lax.all_gather(value_low, ("row", "col"), axis=0, tiled=True),
        )
        same_doc = doc_own[:, None] == doc_seq[None, :]
        head_outs = []
        row_tops = []
        row_totals = []
        for head_index in range(HEADS):
            columns = slice(head_index * HEAD, (head_index + 1) * HEAD)
            raw_scores = (
                jnp.einsum(
                    "qd,kd->qk",
                    query_low[:, columns],
                    keys_all[:, columns],
                    preferred_element_type=wide,
                )
                * score_scale
            )
            masked = jnp.where(same_doc, raw_scores, MASKED)
            row_top = jnp.max(masked, axis=-1, keepdims=True)
            exp_terms = jnp.exp(masked - row_top)
            row_total = jnp.sum(exp_terms, axis=-1, keepdims=True)
            probs_low = (exp_terms / row_total).astype(lowtype)
            head_outs.append(
                jnp.dot(probs_low, values_all[:, columns], preferred_element_type=wide)
            )
            row_tops.append(row_top)
            row_totals.append(row_total)
        attended = jnp.concatenate(head_outs, axis=1)
        context = jnp.concatenate(
            [attended, conv_context.reshape(tokens_here, ATT)], axis=1
        ).astype(lowtype)
        split_context = context.reshape(tokens_here, grid_rows, -1)
        attn_out = (
            jnp.einsum(
                "tra,rcab->tcb", split_context, out_full, preferred_element_type=wide
            ).reshape(tokens_here, model_width)
            + bias_out
        )
        resid_first = own_rows.astype(wide) + attn_out
        hidden = norm_rows(resid_first, gain_first, shift_first)
        hidden_low = hidden.astype(lowtype).reshape(tokens_here, grid_rows, groups_here, -1)
        inner_pre = (
            jnp.einsum(
                "trga,rcgab->trgcb", hidden_low, inner_full, preferred_element_type=wide
            ).reshape(tokens_here, FF)
            + bias_inner
        )
        active = gelu_exact(inner_pre).astype(lowtype)
        split_active = active.reshape(tokens_here, grid_rows, groups_here, grid_cols, -1)
        ffn_out = (
            jnp.einsum(
                "trgca,rcgab->trgb", split_active, outer_full, preferred_element_type=wide
            ).reshape(tokens_here, model_width)
            + bias_outer
        )
        resid_second = hidden + ffn_out
        outputs.append(norm_rows(resid_second, gain_second, shift_second).astype(lowtype))
        proj_full, out_full, inner_full, outer_full = fetched
        proj_tokens = proj_full[:, :, :4]
        proj_point = proj_full[:, :, 4]
        cot_rows = cotangent[micro].astype(wide)
        norm2_back = jax.vjp(norm_rows, resid_second, gain_second, shift_second)[1]
        g_resid2, g_gain2, g_shift2 = norm2_back(cot_rows)
        g_ffn = g_resid2.astype(lowtype)
        split_gffn = g_ffn.reshape(tokens_here, grid_rows, groups_here, -1)
        d_outer_w = jnp.einsum(
            "trgca,trgb->rcgab", split_active, split_gffn, preferred_element_type=wide
        )
        g_active = jnp.einsum(
            "trgb,rcgab->trgca", split_gffn, outer_full, preferred_element_type=wide
        ).reshape(tokens_here, FF)
        gelu_back = jax.vjp(gelu_exact, inner_pre)[1]
        g_inner = gelu_back(g_active)[0].astype(lowtype)
        split_ginner = g_inner.reshape(tokens_here, grid_rows, groups_here, grid_cols, -1)
        d_inner_w = jnp.einsum(
            "trga,trgcb->rcgab", hidden_low, split_ginner, preferred_element_type=wide
        )
        g_hidden = g_resid2 + jnp.einsum(
            "trgcb,rcgab->trga", split_ginner, inner_full, preferred_element_type=wide
        ).reshape(tokens_here, model_width)
        norm1_back = jax.vjp(norm_rows, resid_first, gain_first, shift_first)[1]
        g_resid1, g_gain1, g_shift1 = norm1_back(g_hidden)
        g_attn = g_resid1.astype(lowtype)
        split_gattn = g_attn.reshape(tokens_here, grid_cols, -1)
        d_out_w = jnp.einsum(
            "tra,tcb->rcab", split_context, split_gattn, preferred_element_type=wide
        )
        g_context = (
            jnp.einsum("tcb,rcab->tra", split_gattn, out_full, preferred_element_type=wide)
            .reshape(tokens_here, model_width)
            .astype(lowtype)
        )
        g_attention = g_context[:, :ATT]
        g_conv = g_context[:, ATT:].astype(wide).reshape(tokens_here, HEADS, HEAD)
        g_conv_w = jnp.stack(
            [
                jnp.sum(g_conv * conv_heads[offset : offset + tokens_here], axis=-1)
                for offset in range(KERNEL)
            ],
            axis=-1,
        )
        softmax_back = jax.vjp(lambda logit_values: conv_softmax(logit_values, tap_mask), logits)[1]
        g_logits = softmax_back(g_conv_w)[0].reshape(tokens_here, HEADS * KERNEL).astype(lowtype)
        d_kernel_w = jnp.dot(conv_attn.T, g_logits, preferred_element_type=wide)
        g_conv_attn = jnp.dot(g_logits, kernel_weight.T, preferred_element_type=wide)
        g_ext_value = sum(
            (
                jnp.pad(
                    conv_weights[:, :, offset : offset + 1] * g_conv,
                    ((offset, 2 * margin - offset), (0, 0), (0, 0)),
                )
                for offset in range(KERNEL)
            )
        ).reshape(tokens_here + 2 * margin, ATT)
        g_key_conv = (g_conv_attn * query_low.astype(wide)).astype(lowtype)
        split_gkc = g_key_conv.reshape(tokens_here, grid_cols, -1)
        d_point_w = jnp.einsum("tra,tcb->rcab", split_depth, split_gkc, preferred_element_type=wide)
        g_depth_in = jnp.einsum(
            "tcb,rcab->tra", split_gkc, proj_point, preferred_element_type=wide
        ).reshape(tokens_here, model_width)
        d_depth = jnp.stack(
            [jnp.sum(g_depth_in * shifted[offset], axis=0) for offset in range(KERNEL)]
        )
        g_ext_tokens = sum(
            (
                jnp.pad(
                    jnp.where(
                        tap_mask[:, offset : offset + 1], g_depth_in * depth_gain[offset], 0.0
                    ),
                    ((offset, 2 * margin - offset), (0, 0)),
                )
                for offset in range(KERNEL)
            )
        )
        query_terms = []
        key_terms = []
        value_terms = []
        row_deltas = []
        for head_index in range(HEADS):
            columns = slice(head_index * HEAD, (head_index + 1) * HEAD)
            raw_scores = (
                jnp.einsum(
                    "qd,kd->qk",
                    query_low[:, columns],
                    keys_all[:, columns],
                    preferred_element_type=wide,
                )
                * score_scale
            )
            masked = jnp.where(same_doc, raw_scores, MASKED)
            probs_full = jnp.exp(masked - row_tops[head_index]) / row_totals[head_index]
            g_probs = jnp.einsum(
                "qd,kd->qk",
                g_attention[:, columns],
                values_all[:, columns],
                preferred_element_type=wide,
            )
            row_delta = jnp.sum(probs_full * g_probs, axis=-1, keepdims=True)
            g_scores = (probs_full * (g_probs - row_delta)).astype(lowtype)
            query_terms.append(
                jnp.dot(g_scores, keys_all[:, columns], preferred_element_type=wide) * score_scale
            )
            row_deltas.append(row_delta)
            probs_low = probs_full.astype(lowtype)
            key_terms.append(
                jnp.einsum(
                    "qk,qd->kd", g_scores, query_low[:, columns], preferred_element_type=wide
                )
                * score_scale
            )
            value_terms.append(
                jnp.einsum(
                    "qk,qd->kd", probs_low, g_attention[:, columns], preferred_element_type=wide
                )
            )
        key_sums, value_sums = (
            lax.psum_scatter(
                jnp.concatenate(key_terms, axis=1).astype(jnp.bfloat16),
                ("row", "col"),
                scatter_dimension=0,
                tiled=True,
            ).astype(jnp.float32),
            lax.psum_scatter(
                jnp.concatenate(value_terms, axis=1).astype(jnp.bfloat16),
                ("row", "col"),
                scatter_dimension=0,
                tiled=True,
            ).astype(jnp.float32),
        )
        rim_send = jnp.concatenate(
            [
                jnp.concatenate([g_ext_value[:margin], g_ext_tokens[:margin]], axis=1),
                jnp.concatenate(
                    [g_ext_value[margin + tokens_here :], g_ext_tokens[margin + tokens_here :]],
                    axis=1,
                ),
            ],
            axis=0,
        )
        rim_recv = padded(rim_send.astype(jnp.bfloat16), ((("row", "col"), 0),), margin).astype(
            rim_send.dtype
        )
        from_before = jnp.pad(rim_recv[:margin], ((0, tokens_here - margin), (0, 0)))
        from_after = jnp.pad(rim_recv[3 * margin :], ((tokens_here - margin, 0), (0, 0)))
        rim_total = from_before + from_after
        g_value_conv = (g_ext_value[margin : margin + tokens_here] + rim_total[:, :ATT]).astype(
            lowtype
        )
        g_tokens_depth = g_ext_tokens[margin : margin + tokens_here] + rim_total[:, ATT:]
        g_query = (jnp.concatenate(query_terms, axis=1) + g_conv_attn * key_conv).astype(lowtype)
        g_key = key_sums.astype(lowtype)
        g_value = value_sums.astype(lowtype)
        g_mixed = jnp.stack([g_query, g_key, g_value, g_value_conv]).reshape(
            4, tokens_here, grid_cols, -1
        )
        d_proj_tokens = jnp.einsum(
            "tra,jtcb->rcjab", split_tokens, g_mixed, preferred_element_type=wide
        )
        d_proj = jnp.concatenate([d_proj_tokens, d_point_w[:, :, None]], axis=2)
        token_grads.append(
            g_resid1
            + jnp.einsum(
                "jtcb,rcjab->tra", g_mixed, proj_tokens, preferred_element_type=wide
            ).reshape(tokens_here, model_width)
            + g_tokens_depth
        )
        d_proj_bias = jnp.stack(
            [
                jnp.sum(g_query.astype(wide), axis=0),
                jnp.sum(g_value.astype(wide), axis=0),
                jnp.sum(g_value_conv.astype(wide), axis=0),
                jnp.sum(g_key_conv.astype(wide), axis=0),
            ]
        )
        grad_items.append(
            (
                d_proj,
                d_out_w,
                d_inner_w,
                d_outer_w,
                d_depth,
                d_proj_bias,
                d_kernel_w,
                jnp.sum(g_logits.astype(wide), axis=0),
                jnp.sum(g_attn.astype(wide), axis=0),
                g_gain1,
                g_shift1,
                jnp.sum(g_inner.astype(wide), axis=0),
                jnp.sum(g_ffn.astype(wide), axis=0),
                g_gain2,
                g_shift2,
            )
        )
    summed = [sum(grad_list) for grad_list in zip(*grad_items)]
    grid_count = grid_rows * grid_cols
    acc_proj = summed[0].reshape((grid_count,) + summed[0].shape[2:])
    acc_out = summed[1].reshape((grid_count,) + summed[1].shape[2:])
    acc_inner = summed[2].reshape((grid_count,) + summed[2].shape[2:])
    acc_outer = summed[3].reshape((grid_count,) + summed[3].shape[2:])
    small_sums = lax.psum(
        (
            summed[4],
            summed[5],
            summed[6],
            summed[7],
            summed[8],
            summed[9],
            summed[10],
            summed[11],
            summed[12],
            summed[13],
            summed[14],
        ),
        ("row", "col"),
    )
    data_totals = lax.psum(
        (
            acc_proj,
            acc_out,
            acc_inner,
            acc_outer,
            small_sums[0],
            small_sums[1],
            small_sums[2],
            small_sums[3],
            small_sums[4],
            small_sums[5],
            small_sums[6],
            small_sums[7],
            small_sums[8],
            small_sums[9],
            small_sums[10],
        ),
        "dp",
    )
    blocks = (
        lax.psum_scatter(
            data_totals[0].astype(jnp.bfloat16), ("row", "col"), scatter_dimension=0, tiled=True
        ).astype(jnp.float32),
        lax.psum_scatter(
            data_totals[1].astype(jnp.bfloat16), ("row", "col"), scatter_dimension=0, tiled=True
        ).astype(jnp.float32),
        lax.psum_scatter(
            data_totals[2].astype(jnp.bfloat16), ("row", "col"), scatter_dimension=0, tiled=True
        ).astype(jnp.float32),
        lax.psum_scatter(
            data_totals[3].astype(jnp.bfloat16), ("row", "col"), scatter_dimension=0, tiled=True
        ).astype(jnp.float32),
    )
    finals = data_totals[4:]
    return (
        jnp.stack(outputs),
        jnp.stack(token_grads),
        blocks[0][0],
        blocks[1][0],
        blocks[2][0],
        blocks[3][0],
        finals[0],
        finals[1],
        finals[2],
        finals[3],
        finals[4],
        finals[5],
        finals[6],
        finals[7],
        finals[8],
        finals[9],
        finals[10],
    )


def solution(mesh):
    return jax.shard_map(
        local,
        mesh=mesh,
        in_specs=(
            P(None, ("dp", "row", "col"), None),
            P(None, ("dp", "row", "col"), None),
            P(None, "dp", ("row", "col")),
            P(None, "row", "col"),
            P("row", "col"),
            P("row", None, "col"),
            P("row", "col", None),
            P(),
            P(),
            P(),
            P(),
            P(),
            P(),
            P(),
            P(),
            P(),
            P(),
            P(),
        ),
        out_specs=(
            P(None, ("dp", "row", "col"), None),
            P(None, ("dp", "row", "col"), None),
            P(None, "row", "col"),
            P("row", "col"),
            P("row", None, "col"),
            P("row", "col", None),
            P(),
            P(),
            P(),
            P(),
            P(),
            P(),
            P(),
            P(),
            P(),
            P(),
            P(),
        ),
        check_vma=False,
    )
```

profile of v0, /device:TPU:0, one launch (start us, length us, event | category | flops | bytes accessed | tf_op | source)
XLA Modules:
  0.0 1411.3 jit_solution(8831720430420663578)
XLA Ops:
  10.8 33.3 %all-gather.22.cloned.1.call-done = bf16[40,384,96]{1,2,0:T(8,128)(2,1)} async-done(((bf16[5,384,96]{1,2,0:T(8,128)(2,1)}), bf16[40,384,96]{1,2,0:T(8,128)(2,1)}) %all-gather.22.cloned.1.call-update) | async-done | bytes 2949136 | tf_op jit(solution)/shard_map/all_gather | solution.py:51
  62.0 11.9 all-gather
  90.8 3.4 reshape.698
  98.7 4.3 dot_general.457
  166.0 15.1 %all-gather.16.cloned.1.call-done = bf16[2048,384]{0,1:T(8,128)(2,1)} async-done(((bf16[256,384]{0,1:T(8,128)(2,1)}), bf16[2048,384]{0,1:T(8,128)(2,1)}) %all-gather.16.cloned.1.call-update) | async-done | bytes 1572880 | tf_op jit(solution)/shard_map/all_gather | solution.py:172
  194.2 17.6 %all-gather.26.cloned.1.call-done = bf16[8,384,384]{2,1,0:T(8,128)(2,1)} async-done(((bf16[1,384,384]{2,1,0:T(8,128)(2,1)}), bf16[8,384,384]{2,1,0:T(8,128)(2,1)}) %all-gather.26.cloned.1.call-update) | async-done | bytes 2359312 | tf_op jit(solution)/shard_map/all_gather | solution.py:53
  211.9 4.4 fusion.247
  216.2 26.4 %all-gather.28.cloned.1.call-done = bf16[8,384,384]{2,1,0:T(8,128)(2,1)} async-done(((bf16[1,384,384]{2,1,0:T(8,128)(2,1)}), bf16[8,384,384]{2,1,0:T(8,128)(2,1)}) %all-gather.28.cloned.1.call-update) | async-done | bytes 2359312 | tf_op jit(solution)/shard_map/all_gather | solution.py:54
  242.7 9.1 convolution_bitcast_fusion.14
  257.3 7.1 convolution_bitcast_fusion.15
  276.5 10.8 convert_reduce_fusion
  295.3 11.0 convert_reduce_fusion.1
  321.9 4.0 multiply_reduce_fusion.47
  332.1 4.1 multiply_reduce_fusion.38
  346.8 3.7 fusion.454
  384.1 4.1 fusion.458
  428.5 3.8 collective-permute-start.4
  432.4 3.0 fusion.75
  455.0 3.2 convolution_add_fusion.1
  460.9 10.4 fusion.423
  474.5 10.4 convolution_add_fusion
  488.5 6.1 copy.393
  494.6 6.2 copy.390
  514.7 10.5 reduce-scatter.13.cloned.1.call-done
  529.7 37.0 %reduce-scatter.9.cloned.1.call-done = bf16[256,384]{0,1:T(8,128)(2,1)} async-done(((bf16[2048,384]{0,1:T(8,128)(2,1)}), bf16[256,384]{0,1:T(8,128)(2,1)}) %reduce-scatter.9.cloned.1.call-update) | async-done | bytes 196624 | tf_op jit(solution)/shard_map/reduce_scatter | solution.py:348
  573.7 23.8 %all-reduce.42 = (f32[9,768]{1,0:T(8,128)S(1)}, f32[4,384]{1,0:T(4,128)S(1)}, f32[54]{0:T(128)S(1)}, f32[768]{0:T(1024)S(1)}, f32[768]{0:T(1024)S(1)}, /*index=5...) all-reduce(f32[9,768]{1,0:T(8,128)S(1)} %add.853, ...), channel_id=1, replica_groups=mesh['dp'=4,'row'=2,'col'=4] {'row','col'}, use_global_device_ids=true, to_apply=%region_110.111 | all-reduce | flops 16182 | bytes 129456 | tf_op jit(solution)/shard_map/psum | solution.py:431
  597.5 587.0 %all-reduce.51 = (bf16[8,5,384,96]{2,3,1,0:T(8,128)(2,1)}, bf16[8,384,192]{1,2,0:T(8,128)(2,1)}, bf16[8,1,384,384]{3,2,1,0:T(8,128)(2,1)}, bf16[8,1,384,384]{3,2...) all-reduce(f32[8,5,384,96]{2,3,1,0:T(8,128)} %maximum_add_fusion, ...), channel_id=1, replica_groups=mesh['dp'=4,'row'=2,'col'=4] {'dp'}, use_global_device_ids=true, to_apply=%region_84.85 | all-reduce | flops 4439862 | bytes 26671536 | tf_op jit(solution)/shard_map/psum | solution.py:447
  1194.2 32.4 %reduce-scatter.19.cloned.1.call-done = bf16[1,384,192]{1,2,0:T(8,128)(2,1)} async-done(((bf16[8,384,192]{1,2,0:T(8,128)(2,1)}), bf16[1,384,192]{1,2,0:T(8,128)(2,1)}) %reduce-scatter.19.cloned.1.call-update) | async-done | bytes 147472 | tf_op jit(solution)/shard_map/reduce_scatter | solution.py:471
  1228.3 43.9 %reduce-scatter.23.cloned.1.call-done = bf16[1,1,384,384]{3,2,1,0:T(8,128)(2,1)} async-done(((bf16[8,1,384,384]{3,2,1,0:T(8,128)(2,1)}), bf16[1,1,384,384]{3,2,1,0:T(8,128)(2,1)}) %reduce-scatter.23.cloned.1.call-update) | async-done | bytes 294928 | tf_op jit(solution)/shard_map/reduce_scatter | solution.py:477
  1274.0 43.8 %reduce-scatter.21.cloned.1.call-done = bf16[1,1,384,384]{3,2,1,0:T(8,128)(2,1)} async-done(((bf16[8,1,384,384]{3,2,1,0:T(8,128)(2,1)}), bf16[1,1,384,384]{3,2,1,0:T(8,128)(2,1)}) %reduce-scatter.21.cloned.1.call-update) | async-done | bytes 294928 | tf_op jit(solution)/shard_map/reduce_scatter | solution.py:474
  1319.6 46.5 %reduce-scatter.17.cloned.1.call-done = bf16[1,5,384,96]{2,3,1,0:T(8,128)(2,1)} async-done(((bf16[8,5,384,96]{2,3,1,0:T(8,128)(2,1)}), bf16[1,5,384,96]{2,3,1,0:T(8,128)(2,1)}) %reduce-scatter.17.cloned.1.call-update) | async-done | bytes 368656 | tf_op jit(solution)/shard_map/reduce_scatter | solution.py:468
  1368.0 34.5 %all-reduce.50.cloned.1.call-done = f32[384,54]{0,1:T(8,128)} async-done(((f32[384,54]{0,1:T(8,128)}), f32[384,54]{0,1:T(8,128)}) %all-reduce.50.cloned.1.call-update) | async-done | bytes 82960 | tf_op jit(solution)/shard_map/psum | solution.py:447
  (1282 shorter events, 317.9 us)
Async XLA Ops:
  7.2 98.6 %copy-start = (bf16[384,54]{0,1:T(8,128)(2,1)S(1)}, bf16[384,54]{0,1:T(8,128)(2,1)}, u32[]{:S(2)}) copy-start(bf16[384,54]{0,1:T(8,128)(2,1)} %param.27) | copy-start | bytes 124420
  7.2 36.8 %all-gather.22.cloned.1.call-start = ((), (), s32[]{:S(2)}) async-start(), calls=%async_computation.22 | async-start | bytes 3317760 | tf_op jit(solution)/shard_map/all_gather | solution.py:51
  7.9 82.8 %all-gather.24.cloned.1.call-start = ((), (), s32[]{:S(2)}) async-start(), calls=%async_computation.23 | async-start | bytes 1327104 | tf_op jit(solution)/shard_map/all_gather | solution.py:52
  8.7 111.2 %all-gather.18.cloned.1.call-start = ((), (), s32[]{:S(2)}) async-start(), calls=%async_computation.10 | async-start | bytes 1769472 | tf_op jit(solution)/shard_map/all_gather | solution.py:171
  48.5 89.2 %all-gather.14.cloned.1.call-start = ((), (), s32[]{:S(2)}) async-start(), calls=%async_computation.8 | async-start | bytes 1769472 | tf_op jit(solution)/shard_map/all_gather | solution.py:171
  52.4 100.6 %all-gather.20.cloned.1.call-start = ((), (), s32[]{:S(2)}) async-start(), calls=%async_computation.11 | async-start | bytes 1769472 | tf_op jit(solution)/shard_map/all_gather | solution.py:172
  56.3 124.7 %all-gather.16.cloned.1.call-start = ((), (), s32[]{:S(2)}) async-start(), calls=%async_computation.9 | async-start | bytes 1769472 | tf_op jit(solution)/shard_map/all_gather | solution.py:172
  56.9 155.0 %all-gather.26.cloned.1.call-start = ((), (), s32[]{:S(2)}) async-start(), calls=%async_computation.24 | async-start | bytes 2654208 | tf_op jit(solution)/shard_map/all_gather | solution.py:53
  57.7 185.0 %all-gather.28.cloned.1.call-start = ((), (), s32[]{:S(2)}) async-start(), calls=%async_computation.25 | async-start | bytes 2654208 | tf_op jit(solution)/shard_map/all_gather | solution.py:54
  58.5 26.4 %collective-permute-start = (bf16[2,4,768]{2,1,0:T(4,128)(2,1)S(1)}, bf16[2,4,768]{2,1,0:T(4,128)(2,1)S(1)}, u32[]{:S(2)}, u32[]{:S(2)}) collective-permute-start(bf16[2,4,768]{2,1,0:T(4,128)(2,1)S(1)} %get-tuple-element.192), channel_id=1, source_target_pairs={{0,1},{1,2},{2,3},{3,4},{4,5},{5,6},{6,7},{8,9},{9,10},{10,11},{11... | collective-permute-start | bytes 36872 | tf_op jit(solution)/shard_map/ppermute | solution.py:22
  60.6 24.3 %collective-permute-start.1 = (bf16[2,4,768]{2,1,0:T(4,128)(2,1)S(1)}, bf16[2,4,768]{2,1,0:T(4,128)(2,1)S(1)}, u32[]{:S(2)}, u32[]{:S(2)}) collective-permute-start(bf16[2,4,768]{2,1,0:T(4,128)(2,1)S(1)} %get-tuple-element.193), channel_id=1, source_target_pairs={{1,0},{2,1},{3,2},{4,3},{5,4},{6,5},{7,6},{9,8},{10,9},{11,10},{12... | collective-permute-start | bytes 36872 | tf_op jit(solution)/shard_map/ppermute | solution.py:25
  61.9 450.5 %reduce-scatter.11.cloned.1.call-start = ((), (), s32[]{:S(2)}) async-start(), calls=%async_computation.13 | async-start | bytes 1769472 | tf_op jit(solution)/shard_map/reduce_scatter | solution.py:354
  110.9 79.3 %copy-start.196 = (f32[256,6,1]{0,1,2:T(8,128)}, f32[256,6,1]{0,1,2:T(8,128)S(1)}, u32[]{:S(2)}) copy-start(f32[256,6,1]{0,1,2:T(8,128)S(1)} %copy.556) | copy-start | bytes 18436
  110.9 79.3 %copy-start.198 = (f32[256,6,1]{0,1,2:T(8,128)}, f32[256,6,1]{0,1,2:T(8,128)S(1)}, u32[]{:S(2)}) copy-start(f32[256,6,1]{0,1,2:T(8,128)S(1)} %copy.557) | copy-start | bytes 18436
  110.9 79.3 %copy-start.200 = (f32[256,6,1]{0,1,2:T(8,128)}, f32[256,6,1]{0,1,2:T(8,128)S(1)}, u32[]{:S(2)}) copy-start(f32[256,6,1]{0,1,2:T(8,128)S(1)} %copy.558) | copy-start | bytes 18436
  110.9 79.3 %copy-start.202 = (f32[256,6,1]{0,1,2:T(8,128)}, f32[256,6,1]{0,1,2:T(8,128)S(1)}, u32[]{:S(2)}) copy-start(f32[256,6,1]{0,1,2:T(8,128)S(1)} %copy.559) | copy-start | bytes 18436
  111.0 79.3 %copy-start.204 = (f32[256,6,1]{0,1,2:T(8,128)}, f32[256,6,1]{0,1,2:T(8,128)S(1)}, u32[]{:S(2)}) copy-start(f32[256,6,1]{0,1,2:T(8,128)S(1)} %copy.560) | copy-start | bytes 18436
  111.0 79.2 %copy-start.206 = (f32[256,6,1]{0,1,2:T(8,128)}, f32[256,6,1]{0,1,2:T(8,128)S(1)}, u32[]{:S(2)}) copy-start(f32[256,6,1]{0,1,2:T(8,128)S(1)} %copy.561) | copy-start | bytes 18436
  346.5 167.2 %reduce-scatter.15.cloned.1.call-start = ((), (), s32[]{:S(2)}) async-start(), calls=%async_computation.15 | async-start | bytes 1769472 | tf_op jit(solution)/shard_map/reduce_scatter | solution.py:354
  379.4 129.9 %collective-permute-start.2 = (bf16[4,1152]{1,0:T(4,128)(2,1)}, bf16[4,1152]{1,0:T(4,128)(2,1)}, u32[]{:S(2)}, u32[]{:S(2)}) collective-permute-start(bf16[4,1152]{1,0:T(4,128)(2,1)} %pad_maximum_fusion.19), channel_id=1, source_target_pairs={{0,1},{1,2},{2,3},{3,4},{4,5},{5,6},{6,7},{8,9},{9,10},{10,11},{11... | collective-permute-start | bytes 27656 | tf_op jit(solution)/shard_map/ppermute | solution.py:22
  382.8 126.5 %collective-permute-start.3 = (bf16[4,1152]{1,0:T(4,128)(2,1)}, bf16[4,1152]{1,0:T(4,128)(2,1)}, u32[]{:S(2)}, u32[]{:S(2)}) collective-permute-start(bf16[4,1152]{1,0:T(4,128)(2,1)} %pad_maximum_fusion.20), channel_id=1, source_target_pairs={{1,0},{2,1},{3,2},{4,3},{5,4},{6,5},{7,6},{9,8},{10,9},{11,10},{12... | collective-permute-start | bytes 27656 | tf_op jit(solution)/shard_map/ppermute | solution.py:25
  428.5 81.7 %collective-permute-start.4 = (bf16[4,1152]{1,0:T(4,128)(2,1)}, bf16[4,1152]{1,0:T(4,128)(2,1)}, u32[]{:S(2)}, u32[]{:S(2)}) collective-permute-start(bf16[4,1152]{1,0:T(4,128)(2,1)} %pad_maximum_fusion.21), channel_id=1, source_target_pairs={{0,1},{1,2},{2,3},{3,4},{4,5},{5,6},{6,7},{8,9},{9,10},{10,11},{11... | collective-permute-start | bytes 27656 | tf_op jit(solution)/shard_map/ppermute | solution.py:22
  443.3 81.9 %reduce-scatter.13.cloned.1.call-start = ((), (), s32[]{:S(2)}) async-start(), calls=%async_computation.14 | async-start | bytes 1769472 | tf_op jit(solution)/shard_map/reduce_scatter | solution.py:348
  458.2 108.5 %reduce-scatter.9.cloned.1.call-start = ((), (), s32[]{:S(2)}) async-start(), calls=%async_computation.12 | async-start | bytes 1769472 | tf_op jit(solution)/shard_map/reduce_scatter | solution.py:348
  458.9 51.4 %collective-permute-start.5 = (bf16[4,1152]{1,0:T(4,128)(2,1)}, bf16[4,1152]{1,0:T(4,128)(2,1)}, u32[]{:S(2)}, u32[]{:S(2)}) collective-permute-start(bf16[4,1152]{1,0:T(4,128)(2,1)} %pad_maximum_fusion.22), channel_id=1, source_target_pairs={{1,0},{2,1},{3,2},{4,3},{5,4},{6,5},{7,6},{9,8},{10,9},{11,10},{12... | collective-permute-start | bytes 27656 | tf_op jit(solution)/shard_map/ppermute | solution.py:25
  471.4 718.1 %all-reduce.48.cloned.1.call-start = ((), (), s32[]{:S(2)}) async-start(), calls=%async_computation.20 | async-start | bytes 172032 | tf_op jit(solution)/shard_map/psum | solution.py:431
  505.3 721.3 %reduce-scatter.19.cloned.1.call-start = ((), (), s32[]{:S(2)}) async-start(), calls=%async_computation.17 | async-start | bytes 1327104 | tf_op jit(solution)/shard_map/reduce_scatter | solution.py:471
  512.4 54.3 %copy-start.160 = (bf16[256,384]{0,1:T(8,128)(2,1)}, bf16[256,384]{0,1:T(8,128)(2,1)S(1)}, u32[]{:S(2)}) copy-start(bf16[256,384]{0,1:T(8,128)(2,1)S(1)} %copy.353) | copy-start | bytes 589828
  1184.6 87.6 %reduce-scatter.23.cloned.1.call-start = ((), (), s32[]{:S(2)}) async-start(), calls=%async_computation.19 | async-start | bytes 2654208 | tf_op jit(solution)/shard_map/reduce_scatter | solution.py:477
  1185.2 132.6 %reduce-scatter.21.cloned.1.call-start = ((), (), s32[]{:S(2)}) async-start(), calls=%async_computation.18 | async-start | bytes 2654208 | tf_op jit(solution)/shard_map/reduce_scatter | solution.py:474
  1185.8 180.4 %reduce-scatter.17.cloned.1.call-start = ((), (), s32[]{:S(2)}) async-start(), calls=%async_computation.16 | async-start | bytes 3317760 | tf_op jit(solution)/shard_map/reduce_scatter | solution.py:468
  1186.3 216.2 %all-reduce.50.cloned.1.call-start = ((), (), s32[]{:S(2)}) async-start(), calls=%async_computation.21 | async-start | bytes 172032 | tf_op jit(solution)/shard_map/psum | solution.py:447
  (404 other events, 2370.4 us)
Sparse Core Ops, SparseCore 0:
  9.9 34.0 all-gather.21
  45.9 24.1 all-gather.23
  72.0 25.7 all-gather.17
  99.6 25.7 all-gather.13
  127.1 25.7 all-gather.19
  155.2 25.7 all-gather.15
  182.9 28.8 all-gather.25
  213.7 28.8 all-gather.27
  346.6 38.3 reduce-scatter.10
  443.4 40.0 reduce-scatter.14
  486.8 38.3 reduce-scatter.12
  528.4 38.3 reduce-scatter.8
  570.4 51.3 all-reduce.47
  1184.7 41.8 reduce-scatter.18
  1229.8 42.3 reduce-scatter.22
  1275.4 42.3 reduce-scatter.20
  1321.0 45.0 reduce-scatter.16
  1368.3 34.1 all-reduce.49
where the time goes:
time: 1420 us; the launch traced here: 1410 us
  blocking collectives  623 us (44%)
  waiting for transfers between devices  345 us (24%)
  matrix products  186 us (13%)
  local copies, waits for them, and re-layouts  122 us (9%)
  other arithmetic  100 us (7%)
  between operations  20.5 us (1%)
    psum x1, blocking collectives, local(): lax.psum((acc_proj, acc_out, acc_inner, acc_outer, small_sums[0], small_s...  587 us
    reduce_scatter x2, waiting for transfers between devices, local(): lax.psum_scatter(jnp.concatenate(key_terms, axis=1).astype(jnp.bfloat16),...  47.5 us
    reduce_scatter x1, waiting for transfers between devices, local(): lax.psum_scatter(data_totals[0].astype(jnp.bfloat16), ('row', 'col'), sca...  46.5 us
    unnamed x849, local copies, waits for them, and re-layouts  45.3 us
    reduce_scatter x1, waiting for transfers between devices, local(): lax.psum_scatter(data_totals[3].astype(jnp.bfloat16), ('row', 'col'), sca...  43.9 us
    reduce_scatter x1, waiting for transfers between devices, local(): lax.psum_scatter(data_totals[2].astype(jnp.bfloat16), ('row', 'col'), sca...  43.8 us
    psum x1, waiting for transfers between devices, local(): lax.psum((acc_proj, acc_out, acc_inner, acc_outer, small_sums[0], small_s...  34.5 us
    all_gather x1, waiting for transfers between devices, fetch_weights(): lax.all_gather(proj_weight[None], ('row', 'col'), axis=0, tiled=True)  33.3 us
  transfers between devices with their start and end apart: 24, of which 11 were waited for; matrix products, arithmetic and copies ran while one was open for 19% of the time, Pallas kernels for 0%

commit v1 on v0

v1 whole, which is shorter than its diff:
```python
import jax
import jax.numpy as jnp
from jax import lax
from jax.sharding import PartitionSpec as P

HEADS = 6
HEAD = 64
KERNEL = 9
FF = 3072
ATT = 384
PARTS = 5

EPSILON = 1e-12
MASKED = -1e30
LOW = jnp.bfloat16
WIDE = jnp.float32


def swap(block, axis, step):
    count = lax.axis_size(axis)
    return lax.ppermute(block, axis, [(i, i ^ step) for i in range(count)])


def shift(block, axis, step):
    count = lax.axis_size(axis)
    return lax.ppermute(block, axis, [(i, (i + step) % count) for i in range(count)])


def steps_of(axis):
    steps = []
    step = 1
    while step < lax.axis_size(axis):
        steps.append(step)
        step *= 2
    return steps


def pick(block, index):
    return lax.dynamic_index_in_dim(block, index, 0, keepdims=False)


def norm_rows(values_in, norm_gain, norm_shift):
    row_mean = jnp.mean(values_in, axis=-1, keepdims=True)
    centred = values_in - row_mean
    row_var = jnp.mean(centred * centred, axis=-1, keepdims=True)
    return centred * lax.rsqrt(row_var + EPSILON) * norm_gain + norm_shift


def conv_softmax(logits, tap_mask):
    allowed = tap_mask[:, None, :]
    masked = jnp.where(allowed, logits, MASKED)
    row_top = jnp.max(masked, axis=-1, keepdims=True)
    exp_terms = jnp.where(allowed, jnp.exp(masked - row_top), 0.0)
    return exp_terms / jnp.sum(exp_terms, axis=-1, keepdims=True)


def gelu_exact(values_in):
    return jax.nn.gelu(values_in, approximate=False)


def gather_grid(slab):
    half = slab.shape[0] // 2
    far = [step for step in steps_of("col") if step > 1]
    first = {(0, 0): slab[:half]}
    second = {(0, 0): slab[half:]}

    def grow_row(held):
        keys = list(held)
        moved = swap(jnp.stack([held[key] for key in keys]), "row", 1)
        for place, key in enumerate(keys):
            held[(key[0] ^ 1, key[1])] = moved[place]

    def grow_col(held, step):
        keys = list(held)
        moved = swap(jnp.stack([held[key] for key in keys]), "col", step)
        for place, key in enumerate(keys):
            held[(key[0], key[1] ^ step)] = moved[place]

    grow_row(first)
    grow_col(second, far[0])
    grow_col(first, far[0])
    grow_row(second)
    for step in far[1:]:
        grow_col(first, step)
        grow_col(second, step)
    grow_col(first, 1)
    grow_col(second, 1)
    return [
        [
            jnp.concatenate([first[(dr, dc)], second[(dr, dc)]], axis=0)
            for dc in range(lax.axis_size("col"))
        ]
        for dr in range(lax.axis_size("row"))
    ]


def to_absolute(grid):
    row_count = len(grid)
    col_count = len(grid[0])
    stacked = jnp.stack([jnp.stack(line) for line in grid])
    row_here = lax.axis_index("row")
    col_here = lax.axis_index("col")
    return jnp.stack(
        [
            jnp.stack(
                [
                    pick(pick(stacked, row_here ^ dr), col_here ^ dc)
                    for dc in range(col_count)
                ]
            )
            for dr in range(row_count)
        ]
    )


def scatter_grid(slabs):
    slabs = slabs.astype(LOW)
    half = slabs.shape[2] // 2
    far = [step for step in steps_of("col") if step > 1]

    def add(kept, moved):
        return (kept.astype(WIDE) + moved.astype(WIDE)).astype(LOW)

    row_count, col_count = slabs.shape[:2]
    held = {(dr, dc): slabs[dr, dc] for dr in range(row_count) for dc in range(col_count)}

    def fold(held, axis, step, chosen):
        keys = [key for key in held if not chosen(key)]
        gone = [(key[0] ^ step, key[1]) if axis == "row" else (key[0], key[1] ^ step) for key in keys]
        moved = swap(jnp.stack([held[key] for key in gone]), axis, step)
        return {key: add(held[key], moved[place]) for place, key in enumerate(keys)}

    held = fold(held, "col", 1, lambda key: key[1] & 1)
    first = {key: held[key][:half] for key in held}
    second = {key: held[key][half:] for key in held}
    for step in far[1:]:
        first = fold(first, "col", step, lambda key: key[1] & step)
        second = fold(second, "col", step, lambda key: key[1] & step)
    first = fold(first, "row", 1, lambda key: key[0] & 1)
    second = fold(second, "col", far[0], lambda key: key[1] & far[0])
    first = fold(first, "col", far[0], lambda key: key[1] & far[0])
    second = fold(second, "row", 1, lambda key: key[0] & 1)
    return jnp.concatenate([first[(0, 0)], second[(0, 0)]], axis=0)


def data_sum(part):
    index = lax.axis_index("dp")
    steps = steps_of("dp")
    sent = part.dtype
    for step in steps:
        bit = (index // step) % 2
        halves = part.reshape((2, part.shape[0] // 2) + part.shape[1:])
        moved = swap(pick(halves, 1 - bit), "dp", step)
        part = (pick(halves, bit).astype(WIDE) + moved.astype(WIDE)).astype(sent)
    for step in reversed(steps):
        bit = (index // step) % 2
        moved = swap(part, "dp", step)
        both = jnp.stack([part, moved])
        part = jnp.concatenate([pick(both, bit), pick(both, 1 - bit)], axis=0)
    return part


def local(
    tokens,
    cotangent,
    doc_ids,
    proj_weight,
    out_weight,
    inner_weight,
    outer_weight,
    depth_weight,
    proj_bias,
    kernel_weight,
    kernel_bias,
    out_bias,
    norm1_gain,
    norm1_shift,
    inner_bias,
    outer_bias,
    norm2_gain,
    norm2_shift,
):
    block_len = tokens.shape[1]
    model_width = tokens.shape[2]
    margin = KERNEL // 2
    row_count = lax.axis_size("row")
    col_count = lax.axis_size("col")
    row_here = lax.axis_index("row")
    col_here = lax.axis_index("col")
    tokens_here = 2 * block_len
    score_scale = HEAD ** (-0.5)
    depth_gain = depth_weight.astype(WIDE)
    bias_proj = proj_bias.astype(WIDE)
    bias_kernel = kernel_bias.astype(WIDE)
    bias_out = out_bias.astype(WIDE)
    gain_first = norm1_gain.astype(WIDE)
    shift_first = norm1_shift.astype(WIDE)
    bias_inner = inner_bias.astype(WIDE)
    bias_outer = outer_bias.astype(WIDE)
    gain_second = norm2_gain.astype(WIDE)
    shift_second = norm2_shift.astype(WIDE)

    slab_proj = jnp.transpose(proj_weight, (0, 2, 1)).reshape(-1, proj_weight.shape[1])
    slab_rest = jnp.concatenate([out_weight.T, inner_weight[0].T, outer_weight[0]], axis=0)
    proj_abs = to_absolute(gather_grid(slab_proj))
    rest_abs = to_absolute(gather_grid(slab_rest))
    lanes = slab_proj.shape[1]
    proj_t = proj_abs.reshape(row_count, col_count, PARTS, -1, lanes)
    cut_out = out_weight.shape[1]
    cut_inner = cut_out + inner_weight.shape[2]
    out_t = rest_abs[:, :, :cut_out]
    inner_t = rest_abs[:, :, cut_out:cut_inner]
    outer_full = rest_abs[:, :, cut_inner:]

    def trade(pair):
        return jnp.stack([pick(pair, row_here), swap(pick(pair, 1 - row_here), "row", 1)])

    own = trade(tokens)
    cot = trade(cotangent).reshape(tokens_here, model_width)

    def rims(last, first):
        wrap_low = col_here == 0
        wrap_high = col_here == col_count - 1
        low = shift(last, "col", 1)
        high = shift(first, "col", -1)
        low = jnp.where(wrap_low, low[::-1], low)
        high = jnp.where(wrap_high, high[::-1], high)
        return low, high

    low_rim, high_rim = rims(own[:, block_len - margin :], own[:, :margin])
    extended = jnp.concatenate([low_rim, own, high_rim], axis=1)
    own_rows = own.reshape(tokens_here, model_width)

    docs = trade(doc_ids[:, 0])[None]
    for step in reversed(steps_of("col")):
        docs = jnp.concatenate([docs, swap(docs, "col", step)], axis=0)
    order = [0]
    for step in reversed(steps_of("col")):
        order = order + [entry ^ step for entry in order]
    ordered = jnp.stack([docs[order.index(dc)] for dc in range(col_count)])
    doc_seq = jnp.concatenate(
        [
            pick(pick(ordered, col_here ^ dc), row_here ^ dr)
            for dr in range(row_count)
            for dc in range(col_count)
        ]
    )
    doc_keys = ordered.reshape(-1)
    doc_padded = jnp.pad(doc_seq, (margin, margin), constant_values=-1)
    starts = [
        ((row_here ^ slot) * col_count + col_here) * block_len for slot in range(2)
    ]
    doc_ext = jnp.stack(
        [lax.dynamic_slice_in_dim(doc_padded, start, block_len + 2 * margin) for start in starts]
    )
    doc_own = doc_ext[:, margin : margin + block_len]
    tap_mask = jnp.stack(
        [doc_ext[:, offset : offset + block_len] == doc_own for offset in range(KERNEL)], axis=2
    ).reshape(tokens_here, KERNEL)
    doc_rows = doc_own.reshape(tokens_here)

    def taps_of(ext):
        width = ext.shape[2:]
        return [
            ext[:, offset : offset + block_len].reshape((tokens_here,) + width)
            for offset in range(KERNEL)
        ]

    shifted = [
        jnp.where(tap_mask[:, offset : offset + 1], piece.astype(WIDE), 0.0)
        for offset, piece in enumerate(taps_of(extended))
    ]
    depth_low = sum((depth_gain[offset] * shifted[offset] for offset in range(KERNEL))).astype(LOW)
    split_depth = depth_low.reshape(tokens_here, row_count, -1)
    split_tokens = own_rows.reshape(tokens_here, row_count, -1)
    mixed_proj = jnp.einsum(
        "tra,rcjba->jtcb", split_tokens, proj_t[:, :, :3], preferred_element_type=WIDE
    ).reshape(3, tokens_here, ATT)
    query_low = (mixed_proj[0] + bias_proj[0]).astype(LOW)
    key_low = mixed_proj[1].astype(LOW)
    value_low = (mixed_proj[2] + bias_proj[1]).astype(LOW)
    conv_ext = (
        jnp.einsum(
            "stra,rcba->stcb",
            extended.reshape(2, block_len + 2 * margin, row_count, -1),
            proj_t[:, :, 3],
            preferred_element_type=WIDE,
        ).reshape(2, block_len + 2 * margin, ATT)
        + bias_proj[2]
    ).astype(LOW)
    conv_taps = [piece.reshape(tokens_here, HEADS, HEAD) for piece in taps_of(conv_ext)]
    key_conv = (
        jnp.einsum(
            "tra,rcba->tcb", split_depth, proj_t[:, :, 4], preferred_element_type=WIDE
        ).reshape(tokens_here, ATT)
        + bias_proj[3]
    )
    conv_attn = (query_low.astype(WIDE) * key_conv).astype(LOW)
    logits = (
        jnp.dot(conv_attn, kernel_weight, preferred_element_type=WIDE) + bias_kernel
    ).reshape(tokens_here, HEADS, KERNEL)
    conv_weights = conv_softmax(logits, tap_mask)
    conv_context = sum(
        (conv_weights[:, :, offset : offset + 1] * conv_taps[offset] for offset in range(KERNEL))
    )

    pair = jnp.concatenate([key_low, value_low], axis=1)[None]
    for step in reversed(steps_of("col")):
        pair = jnp.concatenate([pair, swap(pair, "col", step)], axis=0)
    pair = jnp.concatenate([pair[order.index(dc)] for dc in range(col_count)], axis=0)
    keys_all = pair[:, :ATT]
    values_all = pair[:, ATT:]

    same_doc = doc_rows[:, None] == doc_keys[None, :]
    head_outs = []
    row_tops = []
    row_totals = []
    for head_index in range(HEADS):
        columns = slice(head_index * HEAD, (head_index + 1) * HEAD)
        raw_scores = (
            jnp.einsum(
                "qd,kd->qk", query_low[:, columns], keys_all[:, columns], preferred_element_type=WIDE
            )
            * score_scale
        )
        masked = jnp.where(same_doc, raw_scores, MASKED)
        row_top = jnp.max(masked, axis=-1, keepdims=True)
        exp_terms = jnp.exp(masked - row_top)
        row_total = jnp.sum(exp_terms, axis=-1, keepdims=True)
        probs_low = (exp_terms / row_total).astype(LOW)
        head_outs.append(jnp.dot(probs_low, values_all[:, columns], preferred_element_type=WIDE))
        row_tops.append(row_top)
        row_totals.append(row_total)
    attended = jnp.concatenate(head_outs, axis=1)
    context = jnp.concatenate([attended, conv_context.reshape(tokens_here, ATT)], axis=1).astype(LOW)
    split_context = context.reshape(tokens_here, row_count, -1)
    attn_out = (
        jnp.einsum(
            "tra,rcba->tcb", split_context, out_t, preferred_element_type=WIDE
        ).reshape(tokens_here, model_width)
        + bias_out
    )
    resid_first = own_rows.astype(WIDE) + attn_out
    hidden = norm_rows(resid_first, gain_first, shift_first)
    hidden_low = hidden.astype(LOW).reshape(tokens_here, row_count, -1)
    inner_pre = (
        jnp.einsum(
            "tra,rcba->trcb", hidden_low, inner_t, preferred_element_type=WIDE
        ).reshape(tokens_here, FF)
        + bias_inner
    )
    active = gelu_exact(inner_pre).astype(LOW)
    split_active = active.reshape(tokens_here, row_count, col_count, -1)
    ffn_out = (
        jnp.einsum(
            "trca,rcab->trb", split_active, outer_full, preferred_element_type=WIDE
        ).reshape(tokens_here, model_width)
        + bias_outer
    )
    resid_second = hidden + ffn_out
    output = norm_rows(resid_second, gain_second, shift_second).astype(LOW)

    norm2_back = jax.vjp(norm_rows, resid_second, gain_second, shift_second)[1]
    g_resid2, g_gain2, g_shift2 = norm2_back(cot.astype(WIDE))
    g_ffn = g_resid2.astype(LOW)
    split_gffn = g_ffn.reshape(tokens_here, row_count, -1)
    d_outer_w = jnp.einsum("trca,trb->rcab", split_active, split_gffn, preferred_element_type=WIDE)
    g_active = jnp.einsum(
        "trb,rcab->trca", split_gffn, outer_full, preferred_element_type=WIDE
    ).reshape(tokens_here, FF)
    gelu_back = jax.vjp(gelu_exact, inner_pre)[1]
    g_inner = gelu_back(g_active)[0].astype(LOW)
    split_ginner = g_inner.reshape(tokens_here, row_count, col_count, -1)
    d_inner_w = jnp.einsum("tra,trcb->rcba", hidden_low, split_ginner, preferred_element_type=WIDE)
    g_hidden = g_resid2 + jnp.einsum(
        "trcb,rcba->tra", split_ginner, inner_t, preferred_element_type=WIDE
    ).reshape(tokens_here, model_width)
    norm1_back = jax.vjp(norm_rows, resid_first, gain_first, shift_first)[1]
    g_resid1, g_gain1, g_shift1 = norm1_back(g_hidden)
    g_attn = g_resid1.astype(LOW)
    split_gattn = g_attn.reshape(tokens_here, col_count, -1)
    d_out_w = jnp.einsum("tra,tcb->rcba", split_context, split_gattn, preferred_element_type=WIDE)
    g_context = (
        jnp.einsum("tcb,rcba->tra", split_gattn, out_t, preferred_element_type=WIDE)
        .reshape(tokens_here, model_width)
        .astype(LOW)
    )
    g_attention = g_context[:, :ATT]
    g_conv = g_context[:, ATT:].astype(WIDE).reshape(tokens_here, HEADS, HEAD)
    g_conv_w = jnp.stack([jnp.sum(g_conv * piece, axis=-1) for piece in conv_taps], axis=-1)
    softmax_back = jax.vjp(lambda logit_values: conv_softmax(logit_values, tap_mask), logits)[1]
    g_logits = softmax_back(g_conv_w)[0].reshape(tokens_here, HEADS * KERNEL).astype(LOW)
    d_kernel_w = jnp.dot(conv_attn.T, g_logits, preferred_element_type=WIDE)
    g_conv_attn = jnp.dot(g_logits, kernel_weight.T, preferred_element_type=WIDE)

    def spread(pieces):
        return sum(
            (
                jnp.pad(
                    piece.reshape(2, block_len, -1),
                    ((0, 0), (offset, 2 * margin - offset), (0, 0)),
                )
                for offset, piece in enumerate(pieces)
            )
        )

    g_ext_value = spread(
        [conv_weights[:, :, offset : offset + 1] * g_conv for offset in range(KERNEL)]
    )
    g_key_conv = (g_conv_attn * query_low.astype(WIDE)).astype(LOW)
    split_gkc = g_key_conv.reshape(tokens_here, col_count, -1)
    d_point_w = jnp.einsum("tra,tcb->rcba", split_depth, split_gkc, preferred_element_type=WIDE)
    g_depth_in = jnp.einsum(
        "tcb,rcba->tra", split_gkc, proj_t[:, :, 4], preferred_element_type=WIDE
    ).reshape(tokens_here, model_width)
    d_depth = jnp.stack([jnp.sum(g_depth_in * piece, axis=0) for piece in shifted])
    g_ext_tokens = spread(
        [
            jnp.where(tap_mask[:, offset : offset + 1], g_depth_in * depth_gain[offset], 0.0)
            for offset in range(KERNEL)
        ]
    )
    query_terms = []
    key_terms = []
    value_terms = []
    for head_index in range(HEADS):
        columns = slice(head_index * HEAD, (head_index + 1) * HEAD)
        raw_scores = (
            jnp.einsum(
                "qd,kd->qk", query_low[:, columns], keys_all[:, columns], preferred_element_type=WIDE
            )
            * score_scale
        )
        masked = jnp.where(same_doc, raw_scores, MASKED)
        probs_full = jnp.exp(masked - row_tops[head_index]) / row_totals[head_index]
        g_probs = jnp.einsum(
            "qd,kd->qk", g_attention[:, columns], values_all[:, columns], preferred_element_type=WIDE
        )
        row_delta = jnp.sum(probs_full * g_probs, axis=-1, keepdims=True)
        g_scores = (probs_full * (g_probs - row_delta)).astype(LOW)
        query_terms.append(
            jnp.dot(g_scores, keys_all[:, columns], preferred_element_type=WIDE) * score_scale
        )
        probs_low = probs_full.astype(LOW)
        key_terms.append(
            jnp.einsum("qk,qd->kd", g_scores, query_low[:, columns], preferred_element_type=WIDE)
            * score_scale
        )
        value_terms.append(
            jnp.einsum("qk,qd->kd", probs_low, g_attention[:, columns], preferred_element_type=WIDE)
        )
    pair_grads = jnp.concatenate(key_terms + value_terms, axis=1).astype(LOW)
    pair_grads = pair_grads.reshape(col_count, tokens_here, 2 * ATT)
    held = {dc: pair_grads[dc] for dc in range(col_count)}
    for step in steps_of("col"):
        keys = [dc for dc in held if not dc & step]
        moved = swap(jnp.stack([held[dc ^ step] for dc in keys]), "col", step)
        held = {
            dc: (held[dc].astype(WIDE) + moved[place].astype(WIDE)).astype(LOW)
            for place, dc in enumerate(keys)
        }
    g_key = held[0][:, :ATT]
    g_value = held[0][:, ATT:]

    ext_grads = jnp.concatenate([g_ext_value, g_ext_tokens], axis=2)
    from_after, from_before = (
        shift(ext_grads[:, :margin].astype(LOW), "col", -1),
        shift(ext_grads[:, margin + block_len :].astype(LOW), "col", 1),
    )
    from_after = jnp.where(col_here == col_count - 1, from_after[::-1], from_after)
    from_before = jnp.where(col_here == 0, from_before[::-1], from_before)
    rim_total = jnp.pad(
        from_before.astype(WIDE), ((0, 0), (0, block_len - margin), (0, 0))
    ) + jnp.pad(from_after.astype(WIDE), ((0, 0), (block_len - margin, 0), (0, 0)))
    ext_total = (ext_grads[:, margin : margin + block_len] + rim_total).reshape(tokens_here, -1)
    g_value_conv = ext_total[:, :ATT].astype(LOW)
    g_tokens_depth = ext_total[:, ATT:]
    g_query = (jnp.concatenate(query_terms, axis=1) + g_conv_attn * key_conv).astype(LOW)
    g_mixed = jnp.stack([g_query, g_key, g_value, g_value_conv]).reshape(
        4, tokens_here, col_count, -1
    )
    d_proj_tokens = jnp.einsum(
        "tra,jtcb->rcjba", split_tokens, g_mixed, preferred_element_type=WIDE
    )
    d_proj = jnp.concatenate([d_proj_tokens, d_point_w[:, :, None]], axis=2)
    token_grad = (
        g_resid1
        + jnp.einsum(
            "jtcb,rcjba->tra", g_mixed, proj_t[:, :, :4], preferred_element_type=WIDE
        ).reshape(tokens_here, model_width)
        + g_tokens_depth
    )
    d_proj_bias = jnp.stack(
        [
            jnp.sum(g_query.astype(WIDE), axis=0),
            jnp.sum(g_value.astype(WIDE), axis=0),
            jnp.sum(g_value_conv.astype(WIDE), axis=0),
            jnp.sum(g_key_conv.astype(WIDE), axis=0),
        ]
    )
    smalls = [
        d_depth,
        d_proj_bias,
        d_kernel_w,
        jnp.sum(g_logits.astype(WIDE), axis=0),
        jnp.sum(g_attn.astype(WIDE), axis=0),
        g_gain1,
        g_shift1,
        jnp.sum(g_inner.astype(WIDE), axis=0),
        jnp.sum(g_ffn.astype(WIDE), axis=0),
        g_gain2,
        g_shift2,
    ]
    flat = jnp.concatenate([item.reshape(-1) for item in smalls])
    total_len = flat.shape[0]
    flat = jnp.pad(flat, (0, -total_len % 1024)).reshape(-1, 128)
    for axis in ("col", "row", "dp"):
        for step in steps_of(axis):
            flat = flat + swap(flat, axis, step)
    flat = flat.reshape(-1)
    finals = []
    start = 0
    for item in smalls:
        finals.append(flat[start : start + item.size].reshape(item.shape))
        start += item.size

    def to_relative(slabs):
        return jnp.stack(
            [
                jnp.stack(
                    [pick(pick(slabs, row_here ^ dr), col_here ^ dc) for dc in range(col_count)]
                )
                for dr in range(row_count)
            ]
        )

    grads_rest = jnp.concatenate([d_out_w, d_inner_w, d_outer_w], axis=2).astype(LOW)
    rest_sum = data_sum(scatter_grid(to_relative(grads_rest))).astype(WIDE)
    grads_proj = d_proj.reshape(row_count, col_count, -1, lanes).astype(LOW)
    proj_sum = data_sum(scatter_grid(to_relative(grads_proj))).astype(WIDE)

    def give_back(rows):
        pair_rows = rows.reshape(2, block_len, model_width)
        both = jnp.stack([pair_rows[0], swap(pair_rows[1].astype(LOW), "row", 1).astype(rows.dtype)])
        return jnp.where(row_here == 0, both, both[::-1])

    return (
        give_back(output),
        give_back(token_grad),
        jnp.transpose(proj_sum.reshape(PARTS, -1, lanes), (0, 2, 1)),
        rest_sum[:cut_out].T,
        rest_sum[cut_out:cut_inner].T[None],
        rest_sum[cut_inner:][None],
        *finals,
    )


def solution(mesh):
    return jax.shard_map(
        local,
        mesh=mesh,
        in_specs=(
            P(None, ("dp", "row", "col"), None),
            P(None, ("dp", "row", "col"), None),
            P(None, "dp", ("row", "col")),
            P(None, "row", "col"),
            P("row", "col"),
            P("row", None, "col"),
            P("row", "col", None),
        )
        + (P(),) * 11,
        out_specs=(
            P(None, ("dp", "row", "col"), None),
            P(None, ("dp", "row", "col"), None),
            P(None, "row", "col"),
            P("row", "col"),
            P("row", None, "col"),
            P("row", "col", None),
        )
        + (P(),) * 11,
        check_vma=False,
    )
```

time: 1420 us -> 616 us (0.43)
  blocking collectives: 623 us -> 0 us
  waiting for transfers between devices: 345 us -> 97 us
  matrix products: 186 us -> 113 us
  local copies, waits for them, and re-layouts: 122 us -> 189 us
  other arithmetic: 100 us -> 160 us
  starting transfers between devices: 13.8 us -> 45.6 us
  between operations: 20.5 us -> 4.55 us
    psum x2 -> x0, blocking collectives: 611 us -> none  [the longest x1 587 us: local(): lax.psum((acc_proj, acc_out, acc_inner, acc_outer, small_sums[0], small_s...]
    reduce_scatter x8 -> x0, waiting for transfers between devices: 214 us -> none  [the longest x2 47.5 us: local(): lax.psum_scatter(jnp.concatenate(key_terms, axis=1).astype(jnp.bfloat16),...]
    ppermute x6 -> x50, waiting for transfers between devices: 0.02 us -> 97 us  [the longest x46 81.2 us: swap(): return lax.ppermute(block, axis, [(i, i ^ step) for i in range(count)])]
    all_gather x8 -> x0, waiting for transfers between devices: 92.5 us -> none  [the longest x1 33.3 us: fetch_weights(): lax.all_gather(proj_weight[None], ('row', 'col'), axis=0, tiled=True)]
    convert_element_type x4 -> x38, local copies, waits for them, and re-layouts: 0.63 us -> 81.8 us  [the longest x27 51.1 us: local(): conv_weights[:, :, offset:offset + 1] * conv_taps[offset]]
    dot_general x62 -> x31, matrix products: 123 us -> 80.2 us  [the longest x1 18.3 us: local(): jnp.einsum('tra,rcba->trcb', hidden_low, inner_t, preferred_element_type=...]
    psum x2 -> x0, waiting for transfers between devices: 34.5 us -> none  [the longest x1 34.5 us: local(): lax.psum((acc_proj, acc_out, acc_inner, acc_outer, small_sums[0], small_s...]
    ppermute x6 -> x50, starting transfers between devices: 12.7 us -> 45.6 us  [the longest x46 42.3 us: swap(): return lax.ppermute(block, axis, [(i, i ^ step) for i in range(count)])]
  transfers between devices with their start and end apart: 24 -> 50, of which waited for: 11 -> 23; matrix products, arithmetic and copies ran while one was open for 19% -> 49% of each run, Pallas kernels for 0% -> 0%
where the time goes in v1:
time: 616 us; the launch traced here: 610 us
  local copies, waits for them, and re-layouts  189 us (31%)
  other arithmetic  160 us (26%)
  matrix products  113 us (18%)
  waiting for transfers between devices  97 us (16%)
  starting transfers between devices  45.6 us (7%)
    ppermute x46, waiting for transfers between devices, swap(): return lax.ppermute(block, axis, [(i, i ^ step) for i in range(count)])  81.2 us
    convert_element_type x27, local copies, waits for them, and re-layouts, local(): conv_weights[:, :, offset:offset + 1] * conv_taps[offset]  51.1 us
    ppermute x46, starting transfers between devices, swap(): return lax.ppermute(block, axis, [(i, i ^ step) for i in range(count)])  42.3 us
    unnamed x478, local copies, waits for them, and re-layouts  26.9 us
    convert_element_type x8, local copies, waits for them, and re-layouts, local(): piece.astype(WIDE)  23.9 us
    dot_general x1, matrix products, local(): jnp.einsum('tra,rcba->trcb', hidden_low, inner_t, preferred_element_type=...  18.3 us
    convert_element_type x2, other arithmetic, local(): sum((depth_gain[offset] * shifted[offset] for offset in range(KERNEL)))  16.4 us
    ppermute x4, waiting for transfers between devices, shift(): lax.ppermute(block, axis, [(i, (i + step) % count) for i in range(count)])  15.8 us
  transfers between devices with their start and end apart: 50, of which 23 were waited for; matrix products, arithmetic and copies ran while one was open for 49% of the time, Pallas kernels for 0%

profile of v1, /device:TPU:0, one launch (start us, length us, event | category | flops | bytes accessed | tf_op | source)
XLA Modules:
  0.0 609.7 jit_solution(12036783080869161440)
XLA Ops:
  17.7 3.4 collective-permute-done.2
  47.2 13.3 %collective-permute-done.13 = bf16[2,4,768]{2,1,0:T(4,128)(2,1)S(1)} collective-permute-done((bf16[2,4,768]{2,1,0:T(4,128)(2,1)S(1)}, bf16[2,4,768]{2,1,0:T(4,128)(2,1)S(1)}, u32[]{:S(2)}, u32[]{:S(2)}) %collective-permute-start.13) | collective-permute-done | bytes 12320 | tf_op jit(solution)/shard_map/ppermute | solution.py:26
  64.7 4.8 slice_convert_fusion.5
  93.4 12.7 %add_convert_fusion.1 = bf16[512,2,384]{2,1,0:T(2,128)(2,1)} fusion(f32[512,2,384]{2,1,0:T(2,128)} %reshape.914, f32[512,2,384]{2,1,0:T(2,128)} %reshape.913, f32[512,2,384]{2,1,0:T(2,128)} %reshape.912, f32[512,2,384]{2,1,0:T(2,128)} %reshape.911, bf16[512,2,384]{2,1,0:T(2,128)(2,1)} %reshape_reshape.2, f32[512,2,384]{2,1,0:T(2,128)} %reshape.910, ...), kind=kLoop, calls=%fused_computation.255 | loop fusion | flops 10616832 | bytes 14187520 | tf_op jit(solution)/shard_map/convert_element_type | solution.py:273
  106.3 3.6 fusion.113
  109.9 3.3 convert_element_type.1011
  234.1 4.2 pad_maximum_fusion.1
  265.0 18.3 %fusion.9 = (bf16[512,2,4,384]{0,3,2,1:T(8,128)(2,1)S(1)}, f32[512,2,4,384]{0,3,2,1:T(8,128)}, f32[2,4,384,512]{3,2,1,0:T(8,128)}) fusion(f32[2,4,384]{2,1,0:T(4,128)S(1)} %reshape.924, bf16[512,2,384,1]{2,1,0,3:T(2,128)(2,1)} %bitcast.1107, bf16[1,4,960,384]{3,2,1,0:T(8,128)(2,1)} %copy-done.1, bf16[1,4,960,384]{3,2,1,0:T(8,128)(2,1)S(1)} %maximum_bitcast_fusion.2), kind=kOutput, calls=%fused_computation.39 | convolution fusion | flops 1316487168 | bytes 22425600 | tf_op jit(solution)/shard_map/tra,rcba->trcb/dot_general | solution.py:347
  300.6 8.0 %convert_reduce_fusion = (f32[2,4,384]{2,1,0:T(4,128)}, bf16[512,2,4,384]{0,3,2,1:T(8,128)(2,1)S(1)}) fusion(f32[512,2,4,384]{0,3,2,1:T(8,128)} %get-tuple-element.110, bf16[512,2,384,1]{2,1,0,3:T(2,128)(2,1)} %bitcast.1109, bf16[1,4,960,384]{3,2,1,0:T(8,128)(2,1)} %copy-done.1, bf16[1,4,960,384]{3,2,1,0:T(8,128)(2,1)S(1)} %maximum_bitcast_fusion.2, ...), kind=kOutput, calls=%fused_computation.40 | convolution fusion | flops 1239413760 | bytes 22437888 | tf_op jit(solution)/shard_map/trb,rcab->trca/dot_general | solution.py:368
  341.9 3.4 multiply_convert_fusion.5
  348.9 5.2 convolution_convert_fusion.6
  354.0 5.2 convolution_convert_fusion.7
  386.4 3.8 fusion.338
  390.2 10.7 %pad_add_fusion.1 = f32[2,264,384]{1,0,2:T(2,128)} fusion(f32[2,256,384]{1,0,2:T(2,128)S(1)} %bitcast.1076, f32[2,256,384]{1,0,2:T(2,128)S(1)} %bitcast.1077, f32[2,256,384]{1,0,2:T(2,128)S(1)} %bitcast.1078, f32[2,256,384]{1,0,2:T(2,128)S(1)} %bitcast.1079, f32[2,256,384]{1,0,2:T(2,128)S(1)} %bitcast.1080, f32[2,256,384]{1,0,2:T(2,128)S(1)} %bitcast.1081, ...), kind=kLoop, calls=%fused_computation.286 | loop fusion | flops 1622016 | bytes 7888896 | tf_op jit(solution)/shard_map/add | solution.py:397
  403.5 4.5 multiply_reduce_fusion.10
  437.2 3.8 fusion.94
  441.0 4.1 pad_add_fusion
  448.4 3.4 fusion.78
  474.7 13.1 %collective-permute-done.23 = bf16[1,512,768]{1,2,0:T(8,128)(2,1)} collective-permute-done((bf16[1,512,768]{1,2,0:T(8,128)(2,1)}, bf16[1,512,768]{1,2,0:T(8,128)(2,1)}, u32[]{:S(2)}, u32[]{:S(2)}) %collective-permute-start.23) | collective-permute-done | bytes 786464 | tf_op jit(solution)/shard_map/ppermute | solution.py:21
  501.8 4.5 collective-permute-done.46
  506.7 3.7 collective-permute-done.26
  515.0 3.4 fusion.116
  527.7 4.8 collective-permute-done.49
  549.7 3.5 collective-permute-done.38
  554.6 3.7 collective-permute-done.30
  565.9 4.3 collective-permute-done.41
  572.7 4.4 collective-permute-start.33
  577.2 8.0 %collective-permute-done.33 = bf16[120,384]{1,0:T(8,128)(2,1)S(1)} collective-permute-done((bf16[120,384]{1,0:T(8,128)(2,1)S(1)}, bf16[120,384]{1,0:T(8,128)(2,1)S(1)}, u32[]{:S(2)}, u32[]{:S(2)}) %collective-permute-start.33) | collective-permute-done | bytes 92192 | tf_op jit(solution)/shard_map/ppermute | solution.py:21
  585.3 4.0 collective-permute-done.42
  592.3 3.7 collective-permute-done.43
  596.3 3.6 collective-permute-done.35
  601.1 4.7 collective-permute-done.44
  (963 shorter events, 420.1 us)
Async XLA Ops:
  3.1 35.1 %collective-permute-start.14 = (bf16[1,480,384]{2,1,0:T(8,128)(2,1)S(1)}, bf16[1,480,384]{2,1,0:T(8,128)(2,1)S(1)}, u32[]{:S(2)}, u32[]{:S(2)}) collective-permute-start(bf16[1,480,384]{2,1,0:T(8,128)(2,1)S(1)} %bitcast.1023), channel_id=1, source_target_pairs={{0,4},{4,0},{1,5},{5,1},{2,6},{6,2},{3,7},{7,3},{8,12},{12,8},{9,1... | collective-permute-start | bytes 1105928 | tf_op jit(solution)/shard_map/ppermute | solution.py:21
  6.1 33.6 %collective-permute-start.17 = (bf16[1,480,384]{2,1,0:T(8,128)(2,1)S(1)}, bf16[1,480,384]{2,1,0:T(8,128)(2,1)S(1)}, u32[]{:S(2)}, u32[]{:S(2)}) collective-permute-start(bf16[1,480,384]{2,1,0:T(8,128)(2,1)S(1)} %bitcast.1020), channel_id=1, source_target_pairs={{0,2},{1,3},{2,0},{3,1},{4,6},{5,7},{6,4},{7,5},{8,10},{9,11},{10,... | collective-permute-start | bytes 1105928 | tf_op jit(solution)/shard_map/ppermute | solution.py:21
  10.8 30.0 %collective-permute-start = (bf16[256,768]{1,0:T(8,128)(2,1)}, bf16[256,768]{1,0:T(8,128)(2,1)S(1)}, u32[]{:S(2)}, u32[]{:S(2)}) collective-permute-start(bf16[256,768]{1,0:T(8,128)(2,1)} %get-tuple-element.225), channel_id=1, source_target_pairs={{0,4},{4,0},{1,5},{5,1},{2,6},{6,2},{3,7},{7,3},{8,12},{12,8},{9,1... | collective-permute-start | bytes 1179656 | tf_op jit(solution)/shard_map/ppermute | solution.py:21
  13.1 18.3 %collective-permute-start.4 = (bf16[1,240,384]{2,1,0:T(8,128)(2,1)S(1)}, bf16[1,240,384]{2,1,0:T(8,128)(2,1)S(1)}, u32[]{:S(2)}, u32[]{:S(2)}) collective-permute-start(bf16[1,240,384]{2,1,0:T(8,128)(2,1)S(1)} %get-tuple-element.267), channel_id=1, source_target_pairs={{0,4},{4,0},{1,5},{5,1},{2,6},{6,2},{3,7},{7,3},{8,12},{12,8},{9,1... | collective-permute-start | bytes 552968 | tf_op jit(solution)/shard_map/ppermute | solution.py:21
  31.4 12.3 %collective-permute-start.21 = (bf16[256,768]{1,0:T(8,128)(2,1)}, bf16[256,768]{1,0:T(8,128)(2,1)S(1)}, u32[]{:S(2)}, u32[]{:S(2)}) collective-permute-start(bf16[256,768]{1,0:T(8,128)(2,1)} %get-tuple-element.217), channel_id=1, source_target_pairs={{0,4},{4,0},{1,5},{5,1},{2,6},{6,2},{3,7},{7,3},{8,12},{12,8},{9,1... | collective-permute-start | bytes 1179656 | tf_op jit(solution)/shard_map/ppermute | solution.py:21
  34.9 78.5 %collective-permute-start.5 = (bf16[2,240,384]{2,1,0:T(8,128)(2,1)}, bf16[2,240,384]{2,1,0:T(8,128)(2,1)}, u32[]{:S(2)}, u32[]{:S(2)}) collective-permute-start(bf16[2,240,384]{2,1,0:T(8,128)(2,1)} %pad_maximum_fusion.29), channel_id=1, source_target_pairs={{0,2},{1,3},{2,0},{3,1},{4,6},{5,7},{6,4},{7,5},{8,10},{9,11},{10,... | collective-permute-start | bytes 1105928 | tf_op jit(solution)/shard_map/ppermute | solution.py:21
  38.2 76.4 %collective-permute-start.8 = (bf16[2,240,384]{2,1,0:T(8,128)(2,1)}, bf16[2,240,384]{2,1,0:T(8,128)(2,1)}, u32[]{:S(2)}, u32[]{:S(2)}) collective-permute-start(bf16[2,240,384]{2,1,0:T(8,128)(2,1)} %pad_maximum_fusion.30), channel_id=1, source_target_pairs={{0,4},{4,0},{1,5},{5,1},{2,6},{6,2},{3,7},{7,3},{8,12},{12,8},{9,1... | collective-permute-start | bytes 1105928 | tf_op jit(solution)/shard_map/ppermute | solution.py:21
  39.7 79.9 %collective-permute-start.15 = (bf16[2,480,384]{2,1,0:T(8,128)(2,1)}, bf16[2,480,384]{2,1,0:T(8,128)(2,1)}, u32[]{:S(2)}, u32[]{:S(2)}) collective-permute-start(bf16[2,480,384]{2,1,0:T(8,128)(2,1)} %pad_maximum_fusion.22), channel_id=1, source_target_pairs={{0,2},{1,3},{2,0},{3,1},{4,6},{5,7},{6,4},{7,5},{8,10},{9,11},{10,... | collective-permute-start | bytes 2211848 | tf_op jit(solution)/shard_map/ppermute | solution.py:21
  40.9 81.2 %collective-permute-start.18 = (bf16[2,480,384]{2,1,0:T(8,128)(2,1)}, bf16[2,480,384]{2,1,0:T(8,128)(2,1)}, u32[]{:S(2)}, u32[]{:S(2)}) collective-permute-start(bf16[2,480,384]{2,1,0:T(8,128)(2,1)} %pad_maximum_fusion.23), channel_id=1, source_target_pairs={{0,4},{4,0},{1,5},{5,1},{2,6},{6,2},{3,7},{7,3},{8,12},{12,8},{9,1... | collective-permute-start | bytes 2211848 | tf_op jit(solution)/shard_map/ppermute | solution.py:21
  43.7 16.8 %collective-permute-start.13 = (bf16[2,4,768]{2,1,0:T(4,128)(2,1)S(1)}, bf16[2,4,768]{2,1,0:T(4,128)(2,1)S(1)}, u32[]{:S(2)}, u32[]{:S(2)}) collective-permute-start(bf16[2,4,768]{2,1,0:T(4,128)(2,1)S(1)} %get-tuple-element.223), channel_id=1, source_target_pairs={{0,3},{1,0},{2,1},{3,2},{4,7},{5,4},{6,5},{7,6},{8,11},{9,8},{10,9... | collective-permute-start | bytes 36872 | tf_op jit(solution)/shard_map/ppermute | solution.py:26
  114.5 15.7 %collective-permute-start.6 = (bf16[4,240,384]{2,1,0:T(8,128)(2,1)S(1)}, bf16[4,240,384]{2,1,0:T(8,128)(2,1)S(1)}, u32[]{:S(2)}, u32[]{:S(2)}) collective-permute-start(bf16[4,240,384]{2,1,0:T(8,128)(2,1)S(1)} %pad_maximum_fusion.20), channel_id=1, source_target_pairs={{0,1},{1,0},{2,3},{3,2},{4,5},{5,4},{6,7},{7,6},{8,9},{9,8},{10,11... | collective-permute-start | bytes 2211848 | tf_op jit(solution)/shard_map/ppermute | solution.py:21
  115.9 14.5 %collective-permute-start.9 = (bf16[4,240,384]{2,1,0:T(8,128)(2,1)S(1)}, bf16[4,240,384]{2,1,0:T(8,128)(2,1)S(1)}, u32[]{:S(2)}, u32[]{:S(2)}) collective-permute-start(bf16[4,240,384]{2,1,0:T(8,128)(2,1)S(1)} %pad_maximum_fusion.21), channel_id=1, source_target_pairs={{0,1},{1,0},{2,3},{3,2},{4,5},{5,4},{6,7},{7,6},{8,9},{9,8},{10,11... | collective-permute-start | bytes 2211848 | tf_op jit(solution)/shard_map/ppermute | solution.py:21
  122.1 99.3 %collective-permute-start.16 = (bf16[4,480,384]{2,1,0:T(8,128)(2,1)}, bf16[4,480,384]{2,1,0:T(8,128)(2,1)}, u32[]{:S(2)}, u32[]{:S(2)}) collective-permute-start(bf16[4,480,384]{2,1,0:T(8,128)(2,1)} %pad_maximum_fusion.11), channel_id=1, source_target_pairs={{0,1},{1,0},{2,3},{3,2},{4,5},{5,4},{6,7},{7,6},{8,9},{9,8},{10,11... | collective-permute-start | bytes 4423688 | tf_op jit(solution)/shard_map/ppermute | solution.py:21
  124.6 98.3 %collective-permute-start.19 = (bf16[4,480,384]{2,1,0:T(8,128)(2,1)}, bf16[4,480,384]{2,1,0:T(8,128)(2,1)}, u32[]{:S(2)}, u32[]{:S(2)}) collective-permute-start(bf16[4,480,384]{2,1,0:T(8,128)(2,1)} %pad_maximum_fusion.12), channel_id=1, source_target_pairs={{0,1},{1,0},{2,3},{3,2},{4,5},{5,4},{6,7},{7,6},{8,9},{9,8},{10,11... | collective-permute-start | bytes 4423688 | tf_op jit(solution)/shard_map/ppermute | solution.py:21
  143.9 75.9 %collective-permute-start.10 = (bf16[1,512,768]{1,2,0:T(8,128)(2,1)}, bf16[1,512,768]{1,2,0:T(8,128)(2,1)}, u32[]{:S(2)}, u32[]{:S(2)}) collective-permute-start(bf16[1,512,768]{1,2,0:T(8,128)(2,1)} %maximum_bitcast_fusion.11), channel_id=1, source_target_pairs={{0,2},{1,3},{2,0},{3,1},{4,6},{5,7},{6,4},{7,5},{8,10},{9,11},{10,... | collective-permute-start | bytes 2359304 | tf_op jit(solution)/shard_map/ppermute | solution.py:21
  221.3 11.7 %collective-permute-start.11 = (bf16[2,512,768]{1,2,0:T(8,128)(2,1)S(1)}, bf16[2,512,768]{1,2,0:T(8,128)(2,1)S(1)}, u32[]{:S(2)}, u32[]{:S(2)}) collective-permute-start(bf16[2,512,768]{1,2,0:T(8,128)(2,1)S(1)} %pad_maximum_fusion.7), channel_id=1, source_target_pairs={{0,1},{1,0},{2,3},{3,2},{4,5},{5,4},{6,7},{7,6},{8,9},{9,8},{10,11... | collective-permute-start | bytes 4718600 | tf_op jit(solution)/shard_map/ppermute | solution.py:21
  383.5 81.8 %collective-permute-start.22 = (bf16[2,512,768]{1,2,0:T(8,128)(2,1)}, bf16[2,512,768]{1,2,0:T(8,128)(2,1)}, u32[]{:S(2)}, u32[]{:S(2)}) collective-permute-start(bf16[2,512,768]{1,2,0:T(8,128)(2,1)} %pad_maximum_fusion.8), channel_id=1, source_target_pairs={{0,1},{1,0},{2,3},{3,2},{4,5},{5,4},{6,7},{7,6},{8,9},{9,8},{10,11... | collective-permute-start | bytes 4718600 | tf_op jit(solution)/shard_map/ppermute | solution.py:21
  446.0 17.8 %collective-permute-start.24 = (bf16[2,4,1152]{2,1,0:T(4,128)(2,1)}, bf16[2,4,1152]{2,1,0:T(4,128)(2,1)}, u32[]{:S(2)}, u32[]{:S(2)}) collective-permute-start(bf16[2,4,1152]{2,1,0:T(4,128)(2,1)} %get-tuple-element.191), channel_id=1, source_target_pairs={{0,1},{1,2},{2,3},{3,0},{4,5},{5,6},{6,7},{7,4},{8,9},{9,10},{10,1... | collective-permute-start | bytes 55304 | tf_op jit(solution)/shard_map/ppermute | solution.py:26
  446.0 18.5 %collective-permute-start.25 = (bf16[2,4,1152]{2,1,0:T(4,128)(2,1)}, bf16[2,4,1152]{2,1,0:T(4,128)(2,1)}, u32[]{:S(2)}, u32[]{:S(2)}) collective-permute-start(bf16[2,4,1152]{2,1,0:T(4,128)(2,1)} %get-tuple-element.192), channel_id=1, source_target_pairs={{0,3},{1,0},{2,1},{3,2},{4,7},{5,4},{6,5},{7,6},{8,11},{9,8},{10,9... | collective-permute-start | bytes 55304 | tf_op jit(solution)/shard_map/ppermute | solution.py:26
  459.9 55.1 %collective-permute-start.36 = (bf16[4,960,384]{2,1,0:T(8,128)(2,1)}, bf16[4,960,384]{2,1,0:T(8,128)(2,1)}, u32[]{:S(2)}, u32[]{:S(2)}) collective-permute-start(bf16[4,960,384]{2,1,0:T(8,128)(2,1)} %pad_maximum_fusion.4), channel_id=1, source_target_pairs={{0,1},{1,0},{2,3},{3,2},{4,5},{5,4},{6,7},{7,6},{8,9},{9,8},{10,11... | collective-permute-start | bytes 8847368 | tf_op jit(solution)/shard_map/ppermute | solution.py:21
  460.7 11.8 %collective-permute-start.20 = (bf16[256,768]{1,0:T(8,128)(2,1)}, bf16[256,768]{1,0:T(8,128)(2,1)}, u32[]{:S(2)}, u32[]{:S(2)}) collective-permute-start(bf16[256,768]{1,0:T(8,128)(2,1)} %get-tuple-element.219), channel_id=1, source_target_pairs={{0,4},{4,0},{1,5},{5,1},{2,6},{6,2},{3,7},{7,3},{8,12},{12,8},{9,1... | collective-permute-start | bytes 1179656 | tf_op jit(solution)/shard_map/ppermute | solution.py:21
  467.8 19.9 %collective-permute-start.23 = (bf16[1,512,768]{1,2,0:T(8,128)(2,1)}, bf16[1,512,768]{1,2,0:T(8,128)(2,1)}, u32[]{:S(2)}, u32[]{:S(2)}) collective-permute-start(bf16[1,512,768]{1,2,0:T(8,128)(2,1)} %fusion.75), channel_id=1, source_target_pairs={{0,2},{1,3},{2,0},{3,1},{4,6},{5,7},{6,4},{7,5},{8,10},{9,11},{10,... | collective-permute-start | bytes 2359304 | tf_op jit(solution)/shard_map/ppermute | solution.py:21
  494.9 48.4 %collective-permute-start.27 = (bf16[4,480,384]{2,1,0:T(8,128)(2,1)}, bf16[4,480,384]{2,1,0:T(8,128)(2,1)}, u32[]{:S(2)}, u32[]{:S(2)}) collective-permute-start(bf16[4,480,384]{2,1,0:T(8,128)(2,1)} %pad_maximum_fusion.13), channel_id=1, source_target_pairs={{0,1},{1,0},{2,3},{3,2},{4,5},{5,4},{6,7},{7,6},{8,9},{9,8},{10,11... | collective-permute-start | bytes 4423688 | tf_op jit(solution)/shard_map/ppermute | solution.py:21
  498.4 12.1 %collective-permute-start.26 = (bf16[256,768]{1,0:T(8,128)(2,1)S(1)}, bf16[256,768]{1,0:T(8,128)(2,1)S(1)}, u32[]{:S(2)}, u32[]{:S(2)}) collective-permute-start(bf16[256,768]{1,0:T(8,128)(2,1)S(1)} %slice.1485), channel_id=1, source_target_pairs={{0,4},{4,0},{1,5},{5,1},{2,6},{6,2},{3,7},{7,3},{8,12},{12,8},{9,1... | collective-permute-start | bytes 1179656 | tf_op jit(solution)/shard_map/ppermute | solution.py:21
  519.6 18.0 %collective-permute-start.39 = (bf16[2,480,384]{2,1,0:T(8,128)(2,1)}, bf16[2,480,384]{2,1,0:T(8,128)(2,1)}, u32[]{:S(2)}, u32[]{:S(2)}) collective-permute-start(bf16[2,480,384]{2,1,0:T(8,128)(2,1)} %pad_maximum_fusion.25), channel_id=1, source_target_pairs={{0,2},{1,3},{2,0},{3,1},{4,6},{5,7},{6,4},{7,5},{8,10},{9,11},{10,... | collective-permute-start | bytes 2211848 | tf_op jit(solution)/shard_map/ppermute | solution.py:21
  522.3 18.2 %collective-permute-start.37 = (bf16[2,480,384]{2,1,0:T(8,128)(2,1)}, bf16[2,480,384]{2,1,0:T(8,128)(2,1)}, u32[]{:S(2)}, u32[]{:S(2)}) collective-permute-start(bf16[2,480,384]{2,1,0:T(8,128)(2,1)} %pad_maximum_fusion.24), channel_id=1, source_target_pairs={{0,4},{4,0},{1,5},{5,1},{2,6},{6,2},{3,7},{7,3},{8,12},{12,8},{9,1... | collective-permute-start | bytes 2211848 | tf_op jit(solution)/shard_map/ppermute | solution.py:21
  538.9 10.8 %collective-permute-start.40 = (bf16[1,480,384]{2,1,0:T(8,128)(2,1)S(1)}, bf16[1,480,384]{2,1,0:T(8,128)(2,1)S(1)}, u32[]{:S(2)}, u32[]{:S(2)}) collective-permute-start(bf16[1,480,384]{2,1,0:T(8,128)(2,1)S(1)} %fusion.202), channel_id=1, source_target_pairs={{0,4},{4,0},{1,5},{5,1},{2,6},{6,2},{3,7},{7,3},{8,12},{12,8},{9,1... | collective-permute-start | bytes 1105928 | tf_op jit(solution)/shard_map/ppermute | solution.py:21
  541.7 11.5 %collective-permute-start.38 = (bf16[1,480,384]{2,1,0:T(8,128)(2,1)S(1)}, bf16[1,480,384]{2,1,0:T(8,128)(2,1)S(1)}, u32[]{:S(2)}, u32[]{:S(2)}) collective-permute-start(bf16[1,480,384]{2,1,0:T(8,128)(2,1)S(1)} %fusion.201), channel_id=1, source_target_pairs={{0,2},{1,3},{2,0},{3,1},{4,6},{5,7},{6,4},{7,5},{8,10},{9,11},{10,... | collective-permute-start | bytes 1105928 | tf_op jit(solution)/shard_map/ppermute | solution.py:21
  545.2 13.2 %collective-permute-start.30 = (bf16[2,240,384]{2,1,0:T(8,128)(2,1)S(1)}, bf16[2,240,384]{2,1,0:T(8,128)(2,1)S(1)}, u32[]{:S(2)}, u32[]{:S(2)}) collective-permute-start(bf16[2,240,384]{2,1,0:T(8,128)(2,1)S(1)} %pad_maximum_fusion.32), channel_id=1, source_target_pairs={{0,2},{1,3},{2,0},{3,1},{4,6},{5,7},{6,4},{7,5},{8,10},{9,11},{10,... | collective-permute-start | bytes 1105928 | tf_op jit(solution)/shard_map/ppermute | solution.py:21
  545.8 13.7 %collective-permute-start.28 = (bf16[2,240,384]{2,1,0:T(8,128)(2,1)S(1)}, bf16[2,240,384]{2,1,0:T(8,128)(2,1)S(1)}, u32[]{:S(2)}, u32[]{:S(2)}) collective-permute-start(bf16[2,240,384]{2,1,0:T(8,128)(2,1)S(1)} %pad_maximum_fusion.31), channel_id=1, source_target_pairs={{0,4},{4,0},{1,5},{5,1},{2,6},{6,2},{3,7},{7,3},{8,12},{12,8},{9,1... | collective-permute-start | bytes 1105928 | tf_op jit(solution)/shard_map/ppermute | solution.py:21
  572.7 12.5 %collective-permute-start.33 = (bf16[120,384]{1,0:T(8,128)(2,1)S(1)}, bf16[120,384]{1,0:T(8,128)(2,1)S(1)}, u32[]{:S(2)}, u32[]{:S(2)}) collective-permute-start(bf16[120,384]{1,0:T(8,128)(2,1)S(1)} %dynamic-slice_bitcast_fusion.21), channel_id=1, source_target_pairs={{0,16},{8,24},{16,0},{24,8},{1,17},{9,25},{17,1},{25,9},{2,18},{10... | collective-permute-start | bytes 276488 | tf_op jit(solution)/shard_map/ppermute | solution.py:21
  577.1 12.2 %collective-permute-start.42 = (bf16[240,384]{1,0:T(8,128)(2,1)S(1)}, bf16[240,384]{1,0:T(8,128)(2,1)S(1)}, u32[]{:S(2)}, u32[]{:S(2)}) collective-permute-start(bf16[240,384]{1,0:T(8,128)(2,1)S(1)} %dynamic-slice_bitcast_fusion.19), channel_id=1, source_target_pairs={{0,16},{8,24},{16,0},{24,8},{1,17},{9,25},{17,1},{25,9},{2,18},{10... | collective-permute-start | bytes 552968 | tf_op jit(solution)/shard_map/ppermute | solution.py:21
  (246 other events, 2872.9 us)

commit v2 on v1

v2 whole, which is shorter than its diff:
```python
import functools

import jax
import jax.numpy as jnp
from jax import lax
from jax.experimental import pallas as pl
from jax.experimental.pallas import tpu as pltpu
from jax.sharding import PartitionSpec as P

HEADS = 6
HEAD = 64
KERNEL = 9
FF = 3072
ATT = 384
PAIRS = HEADS // 2
LANE = 128
RIM = 8

EPSILON = 1e-12
MASKED = -1e30
LOW = jnp.bfloat16
WIDE = jnp.float32


def swap(block, axis, step):
    count = lax.axis_size(axis)
    return lax.ppermute(block, axis, [(i, i ^ step) for i in range(count)])


def shift(block, axis, step):
    count = lax.axis_size(axis)
    return lax.ppermute(block, axis, [(i, (i + step) % count) for i in range(count)])


def steps_of(axis):
    steps = []
    step = 1
    while step < lax.axis_size(axis):
        steps.append(step)
        step *= 2
    return steps


def pick(block, index):
    return lax.dynamic_index_in_dim(block, index, 0, keepdims=False)


NT = (((1,), (1,)), ((), ()))
NN = (((1,), (0,)), ((), ()))
TN = (((0,), (0,)), ((), ()))


def mm(left, right, how):
    return lax.dot_general(left, right, how, preferred_element_type=WIDE)


def kernel_call(body, outs, scratch=(), smem=1, cost=None):
    def run(*args):
        specs = [
            pl.BlockSpec(memory_space=pltpu.SMEM if place < smem else pltpu.VMEM)
            for place in range(len(args))
        ]
        return pl.pallas_call(
            body,
            in_specs=specs,
            out_specs=[pl.BlockSpec(memory_space=pltpu.VMEM)] * len(outs),
            out_shape=[jax.ShapeDtypeStruct(shape, kind) for shape, kind in outs],
            scratch_shapes=[pltpu.VMEM(shape, kind) for shape, kind in scratch],
            cost_estimate=cost,
        )(*args)

    return run


def place_of(entry, kind):
    if kind == "col":
        entry = (entry & 1) * 2 + (entry // 2) % 2 + (entry // 4) * 4
    return entry % 2, (entry // 2) * 2


def stages_of(kind):
    far = [("col", step) for step in steps_of("col") if step > 1]
    row = [("row", 1)]
    return row + far if kind == "row" else far[:1] + row + far[1:]


def gather(slab, kind):
    stack = slab[None]
    for axis, step in stages_of(kind):
        stack = jnp.concatenate([stack, swap(stack, axis, step)], axis=0)
    return stack, swap(stack, "col", 1)


def add_low(kept, moved):
    return (kept.astype(WIDE) + moved.astype(WIDE)).astype(LOW)


def scatter(kept, sent, kind):
    stack = add_low(kept, swap(sent, "col", 1))
    for axis, step in reversed(stages_of(kind)):
        half = stack.shape[0] // 2
        stack = add_low(stack[:half], swap(stack[half:], axis, step))
    return stack[0]


def data_sum(part):
    index = lax.axis_index("dp")
    steps = steps_of("dp")
    sent = part.dtype
    for step in steps:
        bit = (index // step) % 2
        halves = part.reshape((2, part.shape[0] // 2) + part.shape[1:])
        moved = swap(pick(halves, 1 - bit), "dp", step)
        part = (pick(halves, bit).astype(WIDE) + moved.astype(WIDE)).astype(sent)
    for step in reversed(steps):
        bit = (index // step) % 2
        moved = swap(part, "dp", step)
        both = jnp.stack([part, moved])
        part = jnp.concatenate([pick(both, bit), pick(both, 1 - bit)], axis=0)
    return part


def grid_sum(flat):
    for axis in ("col", "row", "dp"):
        for step in steps_of(axis):
            flat = flat + swap(flat, axis, step)
    return flat


def assemble(here, stacks, kind, full, parts, size, start):
    for core, stack in enumerate(stacks):

        def one(entry, carry):
            dr, dc = place_of(entry, kind)
            row = here[0] ^ dr
            col = here[1] ^ (dc + core)
            for part in range(parts):
                full[part, row, pl.ds(pl.multiple_of(col * size, 16), size), :] = stack[
                    entry, start + part * size : start + (part + 1) * size, :
                ]
            return carry

        lax.fori_loop(0, stack.shape[0], one, 0)


def cut(here, full, outs, kind, parts, size, start):
    for core, out in enumerate(outs):

        def one(entry, carry):
            dr, dc = place_of(entry, kind)
            row = here[0] ^ dr
            col = here[1] ^ (dc + core)
            for part in range(parts):
                out[entry, start + part * size : start + (part + 1) * size, :] = full[
                    part, row, pl.ds(pl.multiple_of(col * size, 16), size), :
                ]
            return carry

        lax.fori_loop(0, out.shape[0], one, 0)


def two(left, right):
    return jnp.concatenate([left, right], axis=1)


def half_pair(value):
    return value[:, : value.shape[1] // 2], value[:, value.shape[1] // 2 :]


def project_kernel(here, own, other, w_own, w_far, bias, query, *rest):
    pairs, w_full = rest[:PAIRS], rest[PAIRS]
    size = w_own.shape[1] // 3
    block_len = own.shape[0]
    assemble(here, (w_own, w_far), "row", w_full, 3, size, 0)
    for slot, source in enumerate((own, other)):
        left, right = half_pair(source[...])
        rows = pl.ds(slot * block_len, block_len)

        def product(part):
            return mm(left, w_full[part, 0], NT) + mm(right, w_full[part, 1], NT)

        query[rows, :] = (product(0) + bias[0:1, :]).astype(LOW)
        key_low = product(1).astype(LOW)
        value_low = (product(2) + bias[1:2, :]).astype(LOW)
        for index, pair in enumerate(pairs):
            lanes = slice(index * LANE, (index + 1) * LANE)
            pair[rows, :] = two(key_low[:, lanes], value_low[:, lanes])


def tile_lanes(mask, times):
    return jnp.concatenate([mask] * times, axis=1)


def split_low(values):
    high = values.astype(LOW)
    return high, (values - high.astype(WIDE)).astype(LOW)


def fill_wide(wide, slot, low_rim, source, high_rim):
    block_len = source.shape[0]
    wide[slot, 0:RIM, :] = low_rim[slot].astype(WIDE)
    wide[slot, RIM : RIM + block_len, :] = source[...].astype(WIDE)
    wide[slot, RIM + block_len : RIM + block_len + RIM, :] = high_rim[slot].astype(WIDE)


def same_doc(docs, slot, offset, block_len):
    start = RIM - KERNEL // 2 + offset
    return docs[slot, start : start + block_len, :] == docs[slot, RIM : RIM + block_len, :]


def spread_heads():
    head = lax.broadcasted_iota(jnp.int32, (2 * LANE, ATT), 0) % LANE
    lane = lax.broadcasted_iota(jnp.int32, (2 * LANE, ATT), 1)
    return jnp.where(lane // HEAD == head, 1.0, 0.0).astype(LOW)


def branch_kernel(
    here,
    own,
    other,
    low_rim,
    high_rim,
    docs,
    w_own,
    w_far,
    depth_gain,
    bias,
    tap_weight,
    tap_bias,
    query,
    context,
    depth_low,
    value_wide,
    key_conv,
    conv_attn,
    conv_weights,
    w_full,
    wide,
):
    size = w_own.shape[1] // 2
    block_len = own.shape[0]
    start = RIM - KERNEL // 2
    assemble(here, (w_own, w_far), "col", w_full, 2, size, 0)
    spread = spread_heads()
    for slot, source in enumerate((own, other)):
        rows = slice(slot * block_len, (slot + 1) * block_len)
        fill_wide(wide, slot, low_rim, source, high_rim)
        for block in range(wide.shape[2] // LANE):
            lanes = slice(block * LANE, (block + 1) * LANE)
            total = jnp.zeros((block_len, LANE), WIDE)
            for offset in range(KERNEL):
                piece = wide[slot, start + offset : start + offset + block_len, lanes]
                piece = jnp.where(same_doc(docs, slot, offset, block_len), piece, 0.0)
                total = total + piece * depth_gain[offset : offset + 1, lanes]
            depth_low[rows, lanes] = total.astype(LOW)
        left, right = half_pair(wide[slot].astype(LOW))
        value = (mm(left, w_full[0, 0], NT) + mm(right, w_full[0, 1], NT) + bias[2:3, :]).astype(LOW)
        value_wide[slot] = value.astype(WIDE)
        left, right = half_pair(depth_low[rows, :])
        key_here = mm(left, w_full[1, 0], NT) + mm(right, w_full[1, 1], NT) + bias[3:4, :]
        key_conv[rows, :] = key_here
        attn = (query[rows, :].astype(WIDE) * key_here).astype(LOW)
        conv_attn[rows, :] = attn
        conv_weights[rows, :] = mm(attn, tap_weight[...], NN) + tap_bias[...]
        top = jnp.full((block_len, LANE), MASKED, WIDE)
        for offset in range(KERNEL):
            lanes = slice(offset * LANE, (offset + 1) * LANE)
            top = jnp.maximum(
                top,
                jnp.where(
                    same_doc(docs, slot, offset, block_len), conv_weights[rows, lanes], MASKED
                ),
            )
        total = jnp.zeros((block_len, LANE), WIDE)
        for offset in range(KERNEL):
            lanes = slice(offset * LANE, (offset + 1) * LANE)
            mask = same_doc(docs, slot, offset, block_len)
            term = jnp.where(
                mask, jnp.exp(jnp.where(mask, conv_weights[rows, lanes], MASKED) - top), 0.0
            )
            conv_weights[rows, lanes] = term
            total = total + term
        scale = 1.0 / total
        mixed = jnp.zeros((block_len, ATT), WIDE)
        for offset in range(KERNEL):
            lanes = slice(offset * LANE, (offset + 1) * LANE)
            weight = conv_weights[rows, lanes] * scale
            conv_weights[rows, lanes] = weight
            wide_weight = mm(two(*split_low(weight)), spread, NN)
            mixed = mixed + wide_weight * value_wide[slot, start + offset : start + offset + block_len, :]
        context[rows, :] = mixed.astype(LOW)


def head_queries(values, head):
    lane = lax.broadcasted_iota(jnp.int32, values.shape, 1)
    return jnp.where(lane // HEAD == head, values, jnp.zeros_like(values))


def blocks_overlap(bounds, slot, block):
    return (bounds[block, 0] <= bounds[slot, 1]) & (bounds[block, 1] >= bounds[slot, 0])


def attend_kernel(bounds, query, kv_own, kv_far, doc_query, doc_key, out, stats, scores, top, total, mixed):
    entries, tokens_here, _ = kv_own.shape
    block_len = tokens_here // 2
    score_scale = HEAD ** (-0.5)
    for slot in range(2):
        rows = slice(slot * block_len, (slot + 1) * block_len)
        scaled = query[rows, :] * jnp.asarray(score_scale, LOW)
        queries = [head_queries(scaled, head) for head in range(2)]
        doc_here = doc_query[slot : slot + 1, :]
        top[...] = jnp.full(top.shape, MASKED, WIDE)
        total[...] = jnp.zeros(total.shape, WIDE)
        mixed[...] = jnp.zeros(mixed.shape, WIDE)

        def each(body):
            for core, stack in enumerate((kv_own, kv_far)):

                def one(step, carry):
                    block = core * entries * 2 + step

                    @pl.when(blocks_overlap(bounds, slot, block))
                    def _():
                        keys = pl.ds(pl.multiple_of((step % 2) * block_len, 16), block_len)
                        body(stack, step // 2, keys, block)

                    return carry

                lax.fori_loop(0, entries * 2, one, 0)

        def first(stack, entry, keys, block):
            key_rows = stack[entry, keys, :LANE]
            doc_rows = doc_key[block]
            allowed = tile_lanes(doc_rows, block_len // LANE) == doc_here
            for head in range(2):
                score = jnp.where(allowed, mm(key_rows, queries[head], NT), MASKED)
                scores[block, head] = score
                top[head] = jnp.maximum(top[head], jnp.max(score, axis=0, keepdims=True))

        each(first)

        def second(stack, entry, keys, block):
            value_rows = stack[entry, keys, LANE:]
            for head in range(2):
                term = jnp.exp(scores[block, head] - top[head, 0:1, :])
                total[head] = total[head] + jnp.sum(term, axis=0, keepdims=True)
                mixed[head] = mixed[head] + mm(value_rows, term.astype(LOW), TN)

        each(second)
        parts = []
        for head in range(2):
            scale = 1.0 / total[head, 0:1, :]
            parts.append(mixed[head, head * HEAD : (head + 1) * HEAD, :] * scale)
            stats[slot, head : head + 1, :] = top[head, 0:1, :] + jnp.log(total[head, 0:1, :])
        out[rows, :] = jnp.concatenate(parts, axis=0).T.astype(LOW)


def attend_back_kernel(
    bounds,
    query,
    kv_own,
    kv_far,
    doc_query,
    doc_key,
    attended,
    grad,
    stats,
    grad_query,
    grad_own,
    grad_far,
    delta,
    grad_kv,
):
    entries, tokens_here, _ = kv_own.shape
    block_len = tokens_here // 2
    score_scale = HEAD ** (-0.5)
    head_row = lax.broadcasted_iota(jnp.int32, (8, LANE), 0)
    head_lane = lax.broadcasted_iota(jnp.int32, (8, LANE), 1) // HEAD
    chosen = jnp.where(head_row == head_lane, 1.0, 0.0).astype(LOW)
    for slot in range(2):
        rows = slice(slot * block_len, (slot + 1) * block_len)
        both = attended[rows, :].astype(WIDE) * grad[rows, :].astype(WIDE)
        high, low = split_low(both)
        delta[slot] = mm(chosen, high, NT) + mm(chosen, low, NT)
    grad_query[...] = jnp.zeros(grad_query.shape, WIDE)

    for core, (stack, out) in enumerate(((kv_own, grad_own), (kv_far, grad_far))):

        def one(step, carry):
            block = core * entries * 2 + step
            keys = pl.ds(pl.multiple_of((step % 2) * block_len, 16), block_len)
            entry = step // 2
            grad_kv[...] = jnp.zeros(grad_kv.shape, WIDE)
            for slot in range(2):

                @pl.when(blocks_overlap(bounds, slot, block))
                def _():
                    rows = slice(slot * block_len, (slot + 1) * block_len)
                    key_rows = stack[entry, keys, :LANE]
                    value_rows = stack[entry, keys, LANE:]
                    scaled = query[rows, :] * jnp.asarray(score_scale, LOW)
                    allowed = tile_lanes(doc_key[block], block_len // LANE) == doc_query[slot : slot + 1, :]
                    for head in range(2):
                        query_here = head_queries(scaled, head)
                        grad_here = head_queries(grad[rows, :], head)
                        score = mm(key_rows, query_here, NT)
                        probs = jnp.where(
                            allowed, jnp.exp(score - stats[slot, head : head + 1, :]), 0.0
                        )
                        g_probs = mm(value_rows, grad_here, NT)
                        g_score = (probs * (g_probs - delta[slot, head : head + 1, :])).astype(LOW)
                        key_here = head_queries(key_rows, head)
                        grad_query[rows, :] += mm(g_score, key_here, TN)
                        grad_kv[:, :LANE] += mm(g_score, query_here, NN)
                        grad_kv[:, LANE:] += mm(probs.astype(LOW), grad_here, NN)

            out[entry, keys, :] = grad_kv[...].astype(LOW)
            return carry

        lax.fori_loop(0, entries * 2, one, 0)
    grad_query[...] = grad_query[...] * score_scale


def norm_stats(values):
    mean = jnp.mean(values, axis=-1, keepdims=True)
    centred = values - mean
    spread = jnp.mean(centred * centred, axis=-1, keepdims=True)
    scale = lax.rsqrt(spread + EPSILON)
    return centred * scale, scale


def norm_back(normal, scale, grad):
    return scale * (
        grad
        - jnp.mean(grad, axis=-1, keepdims=True)
        - normal * jnp.mean(grad * normal, axis=-1, keepdims=True)
    )


def column_sum(values):
    return jnp.sum(values, axis=0, keepdims=True)


def middle_kernel(
    here,
    own,
    other,
    cot_own,
    cot_other,
    att_0,
    att_1,
    att_2,
    conv_context,
    inner_own,
    inner_far,
    tail_own,
    tail_far,
    vectors,
    inner_bias,
    out_own,
    out_other,
    resid_grad,
    g_att_0,
    g_att_1,
    g_att_2,
    g_conv,
    d_inner_own,
    d_inner_far,
    d_tail_own,
    d_tail_far,
    vector_grads,
    inner_bias_grad,
    w_out,
    context,
    normal_1,
    scale_1,
    hidden_low,
    active,
    slope,
    ffn_sum,
    grad_2,
    ffn_grad,
    attn_grad,
    d_out,
):
    block_len = own.shape[0]
    tokens_here = 2 * block_len
    inner_size = inner_own.shape[1]
    out_size = tail_own.shape[1] - inner_size
    half_width = inner_own.shape[2]
    cols = inner_own.shape[0]
    assemble(here, (tail_own, tail_far), "col", w_out, 1, out_size, inner_size)
    bias_out, gain_1, shift_1 = vectors[0:1, :], vectors[1:2, :], vectors[2:3, :]
    bias_outer, gain_2, shift_2 = vectors[3:4, :], vectors[4:5, :], vectors[5:6, :]
    context[0] = jnp.concatenate([att_0[...], att_1[...], att_2[...]], axis=1)
    context[1] = conv_context[...]
    sources = ((own, cot_own, out_own), (other, cot_other, out_other))
    for slot, (source, _, _) in enumerate(sources):
        rows = slice(slot * block_len, (slot + 1) * block_len)
        attn = (
            mm(context[0, rows, :], w_out[0, 0], NT)
            + mm(context[1, rows, :], w_out[0, 1], NT)
            + bias_out
        )
        normal, scale = norm_stats(source[...].astype(WIDE) + attn)
        normal_1[rows, :] = normal
        scale_1[rows, :] = jnp.broadcast_to(scale, (block_len, LANE))
        hidden = normal * gain_1 + shift_1
        left, right = half_pair(hidden.astype(LOW))
        hidden_low[0, rows, :] = left
        hidden_low[1, rows, :] = right
    ffn_sum[...] = jnp.zeros(ffn_sum.shape, WIDE)

    def each(body):
        for core, (inner, tail) in enumerate(((inner_own, tail_own), (inner_far, tail_far))):

            def one(entry, carry):
                dr, dc = place_of(entry, "row")
                entry_tail = (entry % 2) * 2 + (entry // 2) % 2 + (entry // 4) * 4
                group = here[0] ^ dr
                spot = group * (2 * cols // 2) + (here[1] ^ (dc + core))
                body(core, entry, entry_tail, group, spot, inner, tail)
                return carry

            lax.fori_loop(0, cols, one, 0)

    def forward(core, entry, entry_tail, group, spot, inner, tail):
        for slot in range(2):
            rows = slice(slot * block_len, (slot + 1) * block_len)
            pre = mm(hidden_low[group, rows, :], inner[entry], NT) + inner_bias[spot]
            half = 0.5 * (1.0 + lax.erf(pre * (0.5**0.5)))
            low = (pre * half).astype(LOW)
            active[core * cols + entry, rows, :] = low
            slope[core * cols + entry, rows, :] = half + pre * jnp.exp(-0.5 * pre * pre) * (
                0.3989422804014327
            )
            ffn_sum[group, rows, :] += mm(low, tail[entry_tail, :inner_size, :], NN)

    each(forward)
    vector_grads[...] = jnp.zeros(vector_grads.shape, WIDE)
    for slot, (_, cot, out) in enumerate(sources):
        rows = slice(slot * block_len, (slot + 1) * block_len)
        hidden = normal_1[rows, :] * gain_1 + shift_1
        resid = hidden + (two(ffn_sum[0, rows, :], ffn_sum[1, rows, :]) + bias_outer)
        normal, scale = norm_stats(resid)
        out[...] = (normal * gain_2 + shift_2).astype(LOW)
        cot_wide = cot[...].astype(WIDE)
        vector_grads[0:1, :] += column_sum(cot_wide * normal)
        vector_grads[1:2, :] += column_sum(cot_wide)
        grad = norm_back(normal, scale, cot_wide * gain_2)
        grad_2[rows, :] = grad
        low = grad.astype(LOW)
        vector_grads[2:3, :] += column_sum(low.astype(WIDE))
        left, right = half_pair(low)
        ffn_grad[0, rows, :] = left
        ffn_grad[1, rows, :] = right
    ffn_sum[...] = jnp.zeros(ffn_sum.shape, WIDE)

    def backward(core, entry, entry_tail, group, spot, inner, tail):
        d_inner = (d_inner_own, d_inner_far)[core]
        d_tail = (d_tail_own, d_tail_far)[core]
        where = core * cols + entry
        lows = []
        for slot in range(2):
            rows = slice(slot * block_len, (slot + 1) * block_len)
            g_active = mm(ffn_grad[group, rows, :], tail[entry_tail, :inner_size, :], NT)
            low = (g_active * slope[where, rows, :]).astype(LOW)
            lows.append(low)
            ffn_sum[group, rows, :] += mm(low, inner[entry], NN)
        g_inner = jnp.concatenate(lows, axis=0)
        inner_bias_grad[spot] = column_sum(g_inner.astype(WIDE))
        d_inner[entry] = mm(g_inner, hidden_low[group], TN).astype(LOW)
        d_tail[entry_tail, :inner_size, :] = mm(active[where], ffn_grad[group], TN).astype(LOW)

    each(backward)
    for slot in range(2):
        rows = slice(slot * block_len, (slot + 1) * block_len)
        grad = grad_2[rows, :] + two(ffn_sum[0, rows, :], ffn_sum[1, rows, :])
        normal = normal_1[rows, :]
        vector_grads[3:4, :] += column_sum(grad * normal)
        vector_grads[4:5, :] += column_sum(grad)
        grad = norm_back(normal, scale_1[rows, 0:1], grad * gain_1)
        resid_grad[rows, :] = grad
        low = grad.astype(LOW)
        vector_grads[5:6, :] += column_sum(low.astype(WIDE))
        attn_grad[rows, :] = low
        g_att = mm(low, w_out[0, 0], NN).astype(LOW)
        for index, out in enumerate((g_att_0, g_att_1, g_att_2)):
            out[rows, :] = g_att[:, index * LANE : (index + 1) * LANE]
        g_conv[rows, :] = mm(low, w_out[0, 1], NN).astype(LOW)
    for half in range(2):
        d_out[0, half] = mm(attn_grad[...], context[half], TN).astype(LOW)
    cut(here, d_out, (d_tail_own, d_tail_far), "col", 1, out_size, inner_size)


def branch_back_kernel(
    own,
    other,
    low_rim,
    high_rim,
    docs,
    w_full,
    depth_gain,
    tap_weight,
    query,
    g_conv,
    value_wide,
    key_conv,
    conv_attn,
    conv_weights,
    g_key_conv,
    g_query,
    d_tap_weight,
    d_tap_bias,
    d_depth,
    g_ext_value,
    g_ext_tokens,
    wide,
    weight_grad,
    low_grad,
):
    block_len = own.shape[0]
    start = RIM - KERNEL // 2
    spread = spread_heads()
    d_tap_weight[...] = jnp.zeros(d_tap_weight.shape, WIDE)
    d_tap_bias[...] = jnp.zeros(d_tap_bias.shape, WIDE)
    d_depth[...] = jnp.zeros(d_depth.shape, WIDE)
    g_ext_value[...] = jnp.zeros(g_ext_value.shape, WIDE)
    g_ext_tokens[...] = jnp.zeros(g_ext_tokens.shape, WIDE)
    for slot, source in enumerate((own, other)):
        rows = slice(slot * block_len, (slot + 1) * block_len)
        fill_wide(wide, slot, low_rim, source, high_rim)
        grad = g_conv[rows, :].astype(WIDE)
        mean = jnp.zeros((block_len, LANE), WIDE)
        for offset in range(KERNEL):
            lanes = slice(offset * LANE, (offset + 1) * LANE)
            place = slice(start + offset, start + offset + block_len)
            high, low = split_low(grad * value_wide[slot, place, :])
            back = mm(high, spread[:LANE], NT) + mm(low, spread[:LANE], NT)
            weight_grad[:, lanes] = back
            mean = mean + conv_weights[rows, lanes] * back
        for offset in range(KERNEL):
            lanes = slice(offset * LANE, (offset + 1) * LANE)
            place = slice(start + offset, start + offset + block_len)
            weight = conv_weights[rows, lanes]
            low_grad[:, lanes] = (weight * (weight_grad[:, lanes] - mean)).astype(LOW)
            g_ext_value[slot, place, :] += mm(two(*split_low(weight)), spread, NN) * grad
        d_tap_weight[...] += mm(conv_attn[rows, :], low_grad[...], TN)
        d_tap_bias[...] += column_sum(low_grad[...].astype(WIDE))
        g_attn = mm(low_grad[...], tap_weight[...], NT)
        g_key = (g_attn * query[rows, :].astype(WIDE)).astype(LOW)
        g_key_conv[rows, :] = g_key
        g_query[rows, :] = g_attn * key_conv[rows, :]
        for half in range(2):
            g_depth = mm(g_key, w_full[1, half], NN)
            for block in range(g_depth.shape[1] // LANE):
                column = half * g_depth.shape[1] + block * LANE
                lanes = slice(column, column + LANE)
                piece = g_depth[:, block * LANE : (block + 1) * LANE]
                for offset in range(KERNEL):
                    place = slice(start + offset, start + offset + block_len)
                    masked = jnp.where(same_doc(docs, slot, offset, block_len), piece, 0.0)
                    d_depth[offset : offset + 1, lanes] += column_sum(masked * wide[slot, place, lanes])
                    g_ext_tokens[slot, place, lanes] += masked * depth_gain[offset : offset + 1, lanes]


def branch_weights_kernel(
    here,
    own,
    other,
    w_full,
    depth_low,
    g_key_conv,
    g_ext_value,
    g_ext_tokens,
    after,
    before,
    resid_grad,
    d_own,
    d_far,
    token_grad,
    bias_grad,
    ext,
    d_full,
    tokens,
    value_grad,
):
    block_len = own.shape[0]
    size = d_own.shape[1] // 2
    for slot, source in enumerate((own, other)):
        rows = slice(slot * block_len, (slot + 1) * block_len)
        tokens[rows, :] = source[...]
        for grads, lanes in ((g_ext_value, slice(0, ATT)), (g_ext_tokens, slice(ATT, ext.shape[1]))):
            ext[:, lanes] = grads[slot, RIM : RIM + block_len, :]
        ext[0:RIM, :] += before[slot].astype(WIDE)
        ext[block_len - RIM :, :] += after[slot].astype(WIDE)
        low = ext[:, :ATT].astype(LOW)
        value_grad[rows, :] = low
        token_grad[rows, :] = (
            resid_grad[rows, :]
            + ext[:, ATT:]
            + two(mm(low, w_full[0, 0], NN), mm(low, w_full[0, 1], NN))
        )
    bias_grad[0:1, :] = column_sum(value_grad[...].astype(WIDE))
    bias_grad[1:2, :] = column_sum(g_key_conv[...].astype(WIDE))
    for half in range(2):
        lanes = slice(half * d_own.shape[2], (half + 1) * d_own.shape[2])
        d_full[0, half] = mm(value_grad[...], tokens[:, lanes], TN).astype(LOW)
        d_full[1, half] = mm(g_key_conv[...], depth_low[:, lanes], TN).astype(LOW)
    cut(here, d_full, (d_own, d_far), "col", 2, size, 0)


def query_weights_kernel(
    here, own, other, w_full, grad_0, grad_1, grad_2, g_query, token_in, d_own, d_far, token_grad, bias_grad, d_full, tokens
):
    block_len = own.shape[0]
    size = d_own.shape[1]
    low = (jnp.concatenate([grad_0[...], grad_1[...], grad_2[...]], axis=1) + g_query[...]).astype(LOW)
    bias_grad[...] = column_sum(low.astype(WIDE))
    for slot, source in enumerate((own, other)):
        tokens[slot * block_len : (slot + 1) * block_len, :] = source[...]
    token_grad[...] = token_in[...] + two(mm(low, w_full[0, 0], NN), mm(low, w_full[0, 1], NN))
    for half in range(2):
        lanes = slice(half * d_own.shape[2], (half + 1) * d_own.shape[2])
        d_full[0, half] = mm(low, tokens[:, lanes], TN).astype(LOW)
    cut(here, d_full, (d_own, d_far), "col", 1, size, 0)


def pair_weights_kernel(
    here, own, other, w_full, pair_0, pair_1, pair_2, token_in, d_own, d_far, token_own, token_other, bias_grad, d_full, tokens
):
    block_len = own.shape[0]
    size = d_own.shape[1] // 2
    pairs = (pair_0, pair_1, pair_2)
    for slot, source in enumerate((own, other)):
        tokens[slot * block_len : (slot + 1) * block_len, :] = source[...]
    lows = [
        jnp.concatenate([pair[:, part * LANE : (part + 1) * LANE] for pair in pairs], axis=1)
        for part in range(2)
    ]
    bias_grad[...] = column_sum(lows[1].astype(WIDE))
    for part in range(2):
        for half in range(2):
            lanes = slice(half * d_own.shape[2], (half + 1) * d_own.shape[2])
            d_full[part, half] = mm(lows[part], tokens[:, lanes], TN).astype(LOW)
    cut(here, d_full, (d_own, d_far), "row", 2, size, 0)
    for slot, out in enumerate((token_own, token_other)):
        rows = slice(slot * block_len, (slot + 1) * block_len)
        total = token_in[rows, :]
        for part in range(2):
            total = total + two(
                mm(lows[part][rows], w_full[part + 1, 0], NN), mm(lows[part][rows], w_full[part + 1, 1], NN)
            )
        out[...] = total.astype(out.dtype)


def local(
    tokens,
    cotangent,
    doc_ids,
    proj_weight,
    out_weight,
    inner_weight,
    outer_weight,
    depth_weight,
    proj_bias,
    kernel_weight,
    kernel_bias,
    out_bias,
    norm1_gain,
    norm1_shift,
    inner_bias,
    outer_bias,
    norm2_gain,
    norm2_shift,
):
    block_len = tokens.shape[1]
    model_width = tokens.shape[2]
    margin = KERNEL // 2
    col_count = lax.axis_size("col")
    row_count = lax.axis_size("row")
    row_here = lax.axis_index("row")
    col_here = lax.axis_index("col")
    here = jnp.stack([row_here, col_here]).astype(jnp.int32)
    tokens_here = 2 * block_len
    entries = col_count // 2 * row_count
    pair_entries = col_count // 2
    cut_proj = proj_weight.shape[2]
    cut_out = out_weight.shape[1]
    cut_inner = inner_weight.shape[2]
    lanes = proj_weight.shape[1]

    proj_t = jnp.transpose(proj_weight, (0, 2, 1))
    first_own, first_far = gather(proj_t[:3].reshape(-1, lanes), "row")

    def trade(pair):
        return pick(pair, row_here), swap(pick(pair, 1 - row_here), "row", 1)

    own, other = trade(tokens)
    branch_own, branch_far = gather(proj_t[3:].reshape(-1, lanes), "col")

    def wrapped(block, step):
        moved = shift(block, "col", step)
        edge = 0 if step > 0 else col_count - 1
        return jnp.where(col_here == edge, moved[::-1], moved)

    low_rim = wrapped(jnp.stack([own[block_len - RIM :], other[block_len - RIM :]]), 1)
    high_rim = wrapped(jnp.stack([own[:RIM], other[:RIM]]), -1)

    docs = jnp.stack(trade(doc_ids[:, 0]))[None]
    far_steps = [step for step in steps_of("col") if step > 1]
    for step in far_steps + [1]:
        docs = jnp.concatenate([docs, swap(docs, "col", step)], axis=0)
    relative = [0]
    for step in far_steps + [1]:
        relative = relative + [entry ^ step for entry in relative]
    doc_blocks = docs.reshape(-1, block_len)
    bounds = jnp.stack([doc_blocks[:, 0], doc_blocks[:, -1]], axis=1)
    doc_key = jnp.broadcast_to(doc_blocks[:, :, None], doc_blocks.shape + (LANE,))
    ordered = jnp.stack([docs[relative.index(dc)] for dc in range(col_count)])

    def doc_rim(slot, step):
        position = (row_here ^ slot) * col_count + col_here + step
        inside = (position >= 0) & (position < row_count * col_count)
        position = jnp.clip(position, 0, row_count * col_count - 1)
        dr = (position // col_count) ^ row_here
        dc = (position % col_count) ^ col_here
        return jnp.where(inside, pick(pick(ordered, dc), dr), -1)

    doc_ext = jnp.stack(
        [
            jnp.concatenate(
                [doc_rim(slot, -1)[block_len - RIM :], docs[0, slot], doc_rim(slot, 1)[:RIM]]
            )
            for slot in range(2)
        ]
    )
    doc_rows = jnp.broadcast_to(doc_ext[:, :, None], doc_ext.shape + (LANE,))

    inner_own, inner_far = gather(inner_weight[0].T, "row")
    tail_own, tail_far = gather(jnp.concatenate([outer_weight[0], out_weight.T], axis=0), "col")
    cot_own, cot_other = trade(cotangent)

    wide_bias = proj_bias.astype(WIDE)
    tap_weight = jnp.pad(
        kernel_weight.reshape(ATT, HEADS, KERNEL).transpose(0, 2, 1),
        ((0, 0), (0, 0), (0, LANE - HEADS)),
    ).reshape(ATT, KERNEL * LANE)
    tap_bias = (
        jnp.pad(kernel_bias.reshape(HEADS, KERNEL).T, ((0, 0), (0, LANE - HEADS)))
        .reshape(1, KERNEL * LANE)
        .astype(WIDE)
    )
    depth_gain = jnp.pad(depth_weight.astype(WIDE), ((0, 16 - KERNEL), (0, 0)))
    vectors = jnp.stack(
        [out_bias, norm1_gain, norm1_shift, outer_bias, norm2_gain, norm2_shift, norm2_shift, norm2_shift]
    ).astype(WIDE)

    query, *pairs = kernel_call(
        project_kernel,
        [((tokens_here, ATT), LOW)]
        + [((tokens_here, 2 * LANE), LOW)] * PAIRS
        + [((3, row_count, ATT, lanes), LOW)],
    )(here, own, other, first_own, first_far, wide_bias)
    w_first = pairs.pop()

    def gather_pair(pair):
        stack = pair[None]
        for step in far_steps:
            stack = jnp.concatenate([stack, swap(stack, "col", step)], axis=0)
        return stack, swap(stack, "col", 1)

    gathered = [gather_pair(pair) for pair in pairs]

    ext_len = block_len + 2 * RIM
    conv_context, depth_low, value_wide, key_conv, conv_attn, conv_weights, w_branch = kernel_call(
        branch_kernel,
        [
            ((tokens_here, ATT), LOW),
            ((tokens_here, model_width), LOW),
            ((2, ext_len, ATT), WIDE),
            ((tokens_here, ATT), WIDE),
            ((tokens_here, ATT), LOW),
            ((tokens_here, KERNEL * LANE), WIDE),
            ((2, row_count, ATT, lanes), LOW),
        ],
        [((2, ext_len, model_width), WIDE)],
    )(
        here,
        own,
        other,
        low_rim,
        high_rim,
        doc_rows,
        branch_own,
        branch_far,
        depth_gain,
        wide_bias,
        tap_weight,
        tap_bias,
        query,
    )

    doc_query = doc_blocks[:2]
    attended = []
    stats = []
    for index in range(PAIRS):
        out, stat = kernel_call(
            attend_kernel,
            [((tokens_here, LANE), LOW), ((2, 8, block_len), WIDE)],
            [
                ((2 * col_count, 2, block_len, block_len), WIDE),
                ((2, 1, block_len), WIDE),
                ((2, 1, block_len), WIDE),
                ((2, LANE, block_len), WIDE),
            ],
        )(bounds, query[:, index * LANE : (index + 1) * LANE], *gathered[index], doc_query, doc_key)
        attended.append(out)
        stats.append(stat)

    (
        out_own,
        out_other,
        resid_grad,
        *g_att,
        g_conv,
        d_inner_own,
        d_inner_far,
        d_tail_own,
        d_tail_far,
        vector_grads,
        inner_bias_grad,
    ) = kernel_call(
        middle_kernel,
        [
            ((block_len, model_width), LOW),
            ((block_len, model_width), LOW),
            ((tokens_here, model_width), WIDE),
        ]
        + [((tokens_here, LANE), LOW)] * PAIRS
        + [((tokens_here, ATT), LOW)]
        + [((entries, cut_inner, lanes), LOW)] * 2
        + [((entries, cut_inner + cut_out, lanes), LOW)] * 2
        + [((8, model_width), WIDE), ((2 * entries, 1, cut_inner), WIDE)],
        [
            ((1, row_count, model_width, lanes), LOW),
            ((row_count, tokens_here, lanes), LOW),
            ((tokens_here, model_width), WIDE),
            ((tokens_here, LANE), WIDE),
            ((row_count, tokens_here, lanes), LOW),
            ((2 * entries, tokens_here, cut_inner), LOW),
            ((2 * entries, tokens_here, cut_inner), WIDE),
            ((row_count, tokens_here, lanes), WIDE),
            ((tokens_here, model_width), WIDE),
            ((row_count, tokens_here, lanes), LOW),
            ((tokens_here, model_width), LOW),
            ((1, row_count, model_width, lanes), LOW),
        ],
    )(
        here,
        own,
        other,
        cot_own,
        cot_other,
        *attended,
        conv_context,
        inner_own,
        inner_far,
        tail_own,
        tail_far,
        vectors,
        inner_bias.astype(WIDE).reshape(2 * entries, 1, cut_inner),
    )

    inner_sum = data_sum(scatter(d_inner_own, d_inner_far, "row")).astype(WIDE)
    tail_sum = data_sum(scatter(d_tail_own, d_tail_far, "col")).astype(WIDE)

    (
        g_key_conv,
        g_query,
        d_tap_weight,
        d_tap_bias,
        d_depth,
        g_ext_value,
        g_ext_tokens,
    ) = kernel_call(
        branch_back_kernel,
        [
            ((tokens_here, ATT), LOW),
            ((tokens_here, ATT), WIDE),
            ((ATT, KERNEL * LANE), WIDE),
            ((1, KERNEL * LANE), WIDE),
            ((16, model_width), WIDE),
            ((2, ext_len, ATT), WIDE),
            ((2, ext_len, model_width), WIDE),
        ],
        [
            ((2, ext_len, model_width), WIDE),
            ((block_len, KERNEL * LANE), WIDE),
            ((block_len, KERNEL * LANE), LOW),
        ],
        smem=0,
    )(
        own,
        other,
        low_rim,
        high_rim,
        doc_rows,
        w_branch,
        depth_gain,
        tap_weight,
        query,
        g_conv,
        value_wide,
        key_conv,
        conv_attn,
        conv_weights,
    )

    def rim_of(start):
        return jnp.concatenate(
            [g_ext_value[:, start : start + RIM], g_ext_tokens[:, start : start + RIM]], axis=2
        ).astype(LOW)

    after = wrapped(rim_of(0), -1)
    before = wrapped(rim_of(RIM + block_len), 1)

    query_grads = []
    pair_grads = []
    for index in range(PAIRS):
        grad_query, grad_own, grad_far = kernel_call(
            attend_back_kernel,
            [
                ((tokens_here, LANE), WIDE),
                ((pair_entries, tokens_here, 2 * LANE), LOW),
                ((pair_entries, tokens_here, 2 * LANE), LOW),
            ],
            [((2, 8, block_len), WIDE), ((block_len, 2 * LANE), WIDE)],
        )(
            bounds,
            query[:, index * LANE : (index + 1) * LANE],
            *gathered[index],
            doc_query,
            doc_key,
            attended[index],
            g_att[index],
            stats[index],
        )
        query_grads.append(grad_query)
        stack = add_low(grad_own, swap(grad_far, "col", 1))
        for step in reversed(far_steps):
            half = stack.shape[0] // 2
            stack = add_low(stack[:half], swap(stack[half:], "col", step))
        pair_grads.append(stack[0])

    d_branch_own, d_branch_far, token_grad, branch_bias = kernel_call(
        branch_weights_kernel,
        [((entries, 2 * cut_proj, lanes), LOW)] * 2
        + [((tokens_here, model_width), WIDE), ((8, ATT), WIDE)],
        [
            ((block_len, ATT + model_width), WIDE),
            ((2, row_count, ATT, lanes), LOW),
            ((tokens_here, model_width), LOW),
            ((tokens_here, ATT), LOW),
        ],
    )(
        here,
        own,
        other,
        w_branch,
        depth_low,
        g_key_conv,
        g_ext_value,
        g_ext_tokens,
        after,
        before,
        resid_grad,
    )
    branch_sum = data_sum(scatter(d_branch_own, d_branch_far, "col")).astype(WIDE)

    d_query_own, d_query_far, token_grad, query_bias = kernel_call(
        query_weights_kernel,
        [((entries, cut_proj, lanes), LOW)] * 2
        + [((tokens_here, model_width), WIDE), ((1, ATT), WIDE)],
        [((1, row_count, ATT, lanes), LOW), ((tokens_here, model_width), LOW)],
    )(here, own, other, w_first, *query_grads, g_query, token_grad)
    query_sum = data_sum(scatter(d_query_own, d_query_far, "col")).astype(WIDE)

    d_pair_own, d_pair_far, token_own, token_other, value_bias = kernel_call(
        pair_weights_kernel,
        [((entries, 2 * cut_proj, lanes), LOW)] * 2
        + [((block_len, model_width), WIDE), ((block_len, model_width), LOW), ((1, ATT), WIDE)],
        [((2, row_count, ATT, lanes), LOW), ((tokens_here, model_width), LOW)],
    )(here, own, other, w_first, *pair_grads, token_grad)
    pair_sum = data_sum(scatter(d_pair_own, d_pair_far, "row")).astype(WIDE)

    def tap_layout(grads):
        return grads.reshape(-1, KERNEL, LANE)[:, :, :HEADS].transpose(0, 2, 1).reshape(-1, HEADS * KERNEL)

    early = [vector_grads[:6], inner_bias_grad]
    late = [
        d_depth[:KERNEL],
        tap_layout(d_tap_weight),
        tap_layout(d_tap_bias),
        branch_bias[:2],
        query_bias,
        value_bias,
    ]

    def small_sum(items):
        flat = jnp.concatenate([item.reshape(-1) for item in items])
        flat = jnp.pad(flat, (0, -flat.shape[0] % 1024)).reshape(-1, LANE)
        flat = grid_sum(flat).reshape(-1)
        finals = []
        start = 0
        for item in items:
            finals.append(flat[start : start + item.size].reshape(item.shape))
            start += item.size
        return finals

    vector_sum, inner_bias_sum = small_sum(early)
    depth_sum, tap_weight_sum, tap_bias_sum, branch_bias_sum, query_bias_sum, value_bias_sum = small_sum(late)

    def give_back(here_rows, there_rows):
        moved = swap(there_rows, "row", 1).astype(here_rows.dtype)
        return jnp.where(
            row_here == 0, jnp.stack([here_rows, moved]), jnp.stack([moved, here_rows])
        )

    proj_sum = jnp.concatenate([query_sum, pair_sum, branch_sum], axis=0)
    return (
        give_back(out_own, out_other),
        give_back(token_own, token_other),
        jnp.transpose(proj_sum.reshape(5, cut_proj, lanes), (0, 2, 1)),
        tail_sum[cut_inner:].T,
        inner_sum.T[None],
        tail_sum[:cut_inner][None],
        depth_sum,
        jnp.concatenate([query_bias_sum, value_bias_sum, branch_bias_sum], axis=0),
        tap_weight_sum,
        tap_bias_sum[0],
        vector_sum[5],
        vector_sum[3],
        vector_sum[4],
        inner_bias_sum.reshape(-1),
        vector_sum[2],
        vector_sum[0],
        vector_sum[1],
    )


def solution(mesh):
    return jax.shard_map(
        local,
        mesh=mesh,
        in_specs=(
            P(None, ("dp", "row", "col"), None),
            P(None, ("dp", "row", "col"), None),
            P(None, "dp", ("row", "col")),
            P(None, "row", "col"),
            P("row", "col"),
            P("row", None, "col"),
            P("row", "col", None),
        )
        + (P(),) * 11,
        out_specs=(
            P(None, ("dp", "row", "col"), None),
            P(None, ("dp", "row", "col"), None),
            P(None, "row", "col"),
            P("row", "col"),
            P("row", None, "col"),
            P("row", "col", None),
        )
        + (P(),) * 11,
        check_vma=False,
    )
```

time: 616 us -> 443 us (0.72)
  local copies, waits for them, and re-layouts: 189 us -> 22.9 us
  Pallas kernels: 0 us -> 130 us
  matrix products: 113 us -> 0 us
  other arithmetic: 160 us -> 50.7 us
  starting transfers between devices: 45.6 us -> 101 us
  waiting for transfers between devices: 97 us -> 133 us
    pallas_call x0 -> x13, Pallas kernels: none -> 130 us  [run(): pl.pallas_call(body, in_specs=specs, out_specs=[pl.BlockSpec(memory_space...]
    dot_general x55 -> x0, matrix products: 113 us -> none  [the longest x1 18.3 us: local(): jnp.einsum('tra,rcba->trcb', hidden_low, inner_t, preferred_element_type=...]
    convert_element_type x38 -> x0, local copies, waits for them, and re-layouts: 81.8 us -> none  [the longest x27 51.1 us: local(): conv_weights[:, :, offset:offset + 1] * conv_taps[offset]]
    ppermute x46 -> x76, starting transfers between devices: 42.3 us -> 95.7 us  [swap(): return lax.ppermute(block, axis, [(i, i ^ step) for i in range(count)])]
    ppermute x46 -> x76, waiting for transfers between devices: 81.2 us -> 130 us  [swap(): return lax.ppermute(block, axis, [(i, i ^ step) for i in range(count)])]
    convert_element_type x29 -> x20, other arithmetic: 52.2 us -> 8.25 us  [the longest x18 7.05 us: add_low(): return (kept.astype(WIDE) + moved.astype(WIDE)).astype(LOW)]
    another operation x50 -> x10, other arithmetic: 35.6 us -> 3.53 us  [the longest x6 9.94 us: grow_col(): moved = swap(jnp.stack([held[key] for key in keys]), 'col', step)]
    reduce_sum x24 -> x0, other arithmetic: 28.8 us -> none  [the longest x3 4.88 us: norm_rows(): return centred * lax.rsqrt(row_var + EPSILON) * norm_gain + norm_shift]
  transfers between devices with their start and end apart: 50 -> 80, of which waited for: 23 -> 37; matrix products, arithmetic and copies ran while one was open for 49% -> 15% of each run, Pallas kernels for 0% -> 22%
where the time goes in v2:
time: 443 us; the launch traced here: 439 us
  waiting for transfers between devices  133 us (30%)
  Pallas kernels  130 us (29%)
  starting transfers between devices  101 us (23%)
  other arithmetic  50.7 us (11%)
  local copies, waits for them, and re-layouts  22.9 us (5%)
    ppermute x76, waiting for transfers between devices, swap(): return lax.ppermute(block, axis, [(i, i ^ step) for i in range(count)])  130 us
    pallas_call x13, Pallas kernels, run(): pl.pallas_call(body, in_specs=specs, out_specs=[pl.BlockSpec(memory_space...  130 us
    ppermute x76, starting transfers between devices, swap(): return lax.ppermute(block, axis, [(i, i ^ step) for i in range(count)])  95.7 us
    concatenate x8, other arithmetic, gather(): stack = jnp.concatenate([stack, swap(stack, axis, step)], axis=0)  10.4 us
  transfers between devices with their start and end apart: 80, of which 37 were waited for; matrix products, arithmetic and copies ran while one was open for 15% of the time, Pallas kernels for 22%

profile of v2, /device:TPU:0, one launch (start us, length us, event | category | flops | bytes accessed | tf_op | source)
XLA Modules:
  0.0 439.1 jit_solution(2256476619848752371)
XLA Ops:
  1.5 3.0 collective-permute-start.2
  29.2 7.7 %collective-permute-done.6 = bf16[2,288,384]{2,1,0:T(8,128)(2,1)} collective-permute-done((bf16[2,288,384]{2,1,0:T(8,128)(2,1)S(1)}, bf16[2,288,384]{2,1,0:T(8,128)(2,1)}, u32[]{:S(2)}, u32[]{:S(2)}) %collective-permute-start.6) | collective-permute-done | bytes 442400 | tf_op jit(solution)/shard_map/ppermute | solution.py:27
  44.2 9.0 %collective-permute-done.23 = bf16[2,576,384]{2,1,0:T(8,128)(2,1)} collective-permute-done((bf16[2,576,384]{2,1,0:T(8,128)(2,1)}, bf16[2,576,384]{2,1,0:T(8,128)(2,1)}, u32[]{:S(2)}, u32[]{:S(2)}) %collective-permute-start.23) | collective-permute-done | bytes 884768 | tf_op jit(solution)/shard_map/ppermute | solution.py:27
  57.0 5.2 %shard_map.305 = (bf16[512,384]{1,0:T(8,128)(2,1)}, bf16[512,256]{1,0:T(8,128)(2,1)}, bf16[512,256]{1,0:T(8,128)(2,1)}, bf16[512,256]{1,0:T(8,128)(2,1)}, bf16[3,2,384,384]{3,2,1,0:T(8,128)(2,1)}) custom-call(s32[2]{0:T(128)} %pad_add_fusion.8.here, bf16[256,768]{1,0:T(8,128)(2,1)} %get-tuple-element.195.own, bf16[256,768]{1,0:T(8,128)(2,1)} %copy-done, ...), custom_call_target="tpu_custom_call" | custom-call | tf_op jit(solution)/shard_map/pallas_call | solution.py:63
  73.9 3.1 collective-permute-done.10
  81.4 3.2 collective-permute-done.14
  88.4 10.9 %shard_map.309 = (bf16[512,384]{1,0:T(8,128)(2,1)}, bf16[512,768]{1,0:T(8,128)(2,1)}, f32[2,272,384]{2,1,0:T(8,128)}, f32[512,384]{1,0:T(8,128)}, bf16[512,384]{...) custom-call(s32[2]{0:T(128)} %pad_add_fusion.8.here, bf16[256,768]{1,0:T(8,128)(2,1)} %get-tuple-element.195.own, ...), custom_call_target="tpu_custom_call" | custom-call | tf_op jit(solution)/shard_map/pallas_call | solution.py:63
  101.5 6.3 %shard_map.308 = (bf16[512,128]{1,0:T(8,128)(2,1)}, f32[2,8,256]{2,1,0:T(8,128)}) custom-call(s32[8,2]{1,0:T(8,128)} %copy.73.bounds, bf16[512,128]{1,0:T(8,128)(2,1)} %get-tuple-element.204.query, bf16[2,512,256]{2,1,0:T(8,128)(2,1)} %copy-done.3, bf16[2,512,256]{2,1,0:T(8,128)(2,1)} %copy-done.9, s32[2,256]{1,0:T(2,128)} %get-tuple-element.247.doc_query, ...), custom_call_target="tpu_custom_call" | custom-call | tf_op jit(solution)/shard_map/pallas_call | solution.py:63
  107.8 6.3 %shard_map.307 = (bf16[512,128]{1,0:T(8,128)(2,1)}, f32[2,8,256]{2,1,0:T(8,128)}) custom-call(s32[8,2]{1,0:T(8,128)} %copy.73.bounds, bf16[512,128]{1,0:T(8,128)(2,1)} %get-tuple-element.205.query, bf16[2,512,256]{2,1,0:T(8,128)(2,1)} %pad_maximum_fusion.7.kv_own, bf16[2,512,256]{2,1,0:T(8,128)(2,1)} %collective-permute-done.11.kv_far, ...), custom_call_target="tpu_custom_call" | custom-call | tf_op jit(solution)/shard_map/pallas_call | solution.py:63
  114.0 6.3 %shard_map.306 = (bf16[512,128]{1,0:T(8,128)(2,1)}, f32[2,8,256]{2,1,0:T(8,128)}) custom-call(s32[8,2]{1,0:T(8,128)} %copy.73.bounds, bf16[512,128]{1,0:T(8,128)(2,1)} %get-tuple-element.206.query, bf16[2,512,256]{2,1,0:T(8,128)(2,1)} %copy-done.2, bf16[2,512,256]{2,1,0:T(8,128)(2,1)} %collective-permute-done.9.kv_far, ...), custom_call_target="tpu_custom_call" | custom-call | tf_op jit(solution)/shard_map/pallas_call | solution.py:63
  120.4 32.2 %shard_map.310 = (bf16[256,768]{1,0:T(8,128)(2,1)}, bf16[256,768]{1,0:T(8,128)(2,1)}, f32[512,768]{1,0:T(8,128)}, bf16[512,128]{1,0:T(8,128)(2,1)}, bf16[512,128...) custom-call(s32[2]{0:T(128)} %pad_add_fusion.8.here, ...), custom_call_target="tpu_custom_call" | custom-call | tf_op jit(solution)/shard_map/pallas_call | solution.py:63
  154.6 15.6 %shard_map.314 = (bf16[512,384]{1,0:T(8,128)(2,1)}, f32[512,384]{1,0:T(8,128)}, f32[384,1152]{1,0:T(8,128)}, f32[1,1152]{1,0:T(1,128)}, f32[16,768]{1,0:T(8,128)...) custom-call(bf16[256,768]{1,0:T(8,128)(2,1)} %get-tuple-element.195.own, bf16[256,768]{1,0:T(8,128)(2,1)} %copy-done, ...), custom_call_target="tpu_custom_call" | custom-call | tf_op jit(solution)/shard_map/pallas_call | solution.py:63
  176.4 10.0 %shard_map.313 = (f32[512,128]{1,0:T(8,128)}, bf16[2,512,256]{2,1,0:T(8,128)(2,1)}, bf16[2,512,256]{2,1,0:T(8,128)(2,1)}) custom-call(s32[8,2]{1,0:T(8,128)} %copy.73.bounds, bf16[512,128]{1,0:T(8,128)(2,1)} %get-tuple-element.204.query, bf16[2,512,256]{2,1,0:T(8,128)(2,1)} %copy-done.3, bf16[2,512,256]{2,1,0:T(8,128)(2,1)} %copy-done.9, ...), custom_call_target="tpu_custom_call" | custom-call | tf_op jit(solution)/shard_map/pallas_call | solution.py:63
  186.4 9.7 %shard_map.312 = (f32[512,128]{1,0:T(8,128)}, bf16[2,512,256]{2,1,0:T(8,128)(2,1)}, bf16[2,512,256]{2,1,0:T(8,128)(2,1)}) custom-call(s32[8,2]{1,0:T(8,128)} %copy.73.bounds, bf16[512,128]{1,0:T(8,128)(2,1)} %get-tuple-element.205.query, bf16[2,512,256]{2,1,0:T(8,128)(2,1)} %pad_maximum_fusion.7.kv_own, bf16[2,512,256]{2,1,0:T(8,128)(2,1)} %collective-permute-done.11.kv_far, ...), custom_call_target="tpu_custom_call" | custom-call | tf_op jit(solution)/shard_map/pallas_call | solution.py:63
  198.5 3.1 collective-permute-start.76
  202.3 9.6 %shard_map.311 = (f32[512,128]{1,0:T(8,128)}, bf16[2,512,256]{2,1,0:T(8,128)(2,1)}, bf16[2,512,256]{2,1,0:T(8,128)(2,1)}) custom-call(s32[8,2]{1,0:T(8,128)} %copy.73.bounds, bf16[512,128]{1,0:T(8,128)(2,1)} %get-tuple-element.206.query, bf16[2,512,256]{2,1,0:T(8,128)(2,1)} %copy-done.2, bf16[2,512,256]{2,1,0:T(8,128)(2,1)} %collective-permute-done.9.kv_far, ...), custom_call_target="tpu_custom_call" | custom-call | tf_op jit(solution)/shard_map/pallas_call | solution.py:63
  216.9 19.4 %collective-permute-start.78 = (f32[64,128]{1,0:T(8,128)S(1)}, f32[64,128]{1,0:T(8,128)S(1)}, u32[]{:S(2)}, u32[]{:S(2)}) collective-permute-start(f32[64,128]{1,0:T(8,128)S(1)} %add.366), channel_id=1, source_target_pairs={{0,8},{8,0},{16,24},{24,16},{1,9},{9,1},{17,25},{25,17},{2,10},{10... | collective-permute-start | bytes 98312 | tf_op jit(solution)/shard_map/ppermute | solution.py:27
  237.8 6.5 %shard_map.315 = (bf16[4,192,384]{2,1,0:T(8,128)(2,1)}, bf16[4,192,384]{2,1,0:T(8,128)(2,1)}, f32[512,768]{1,0:T(8,128)}, f32[8,384]{1,0:T(8,128)}) custom-call(s32[2]{0:T(128)} %pad_add_fusion.8.here, bf16[256,768]{1,0:T(8,128)(2,1)} %get-tuple-element.195.own, bf16[256,768]{1,0:T(8,128)(2,1)} %copy-done, ...), custom_call_target="tpu_custom_call" | custom-call | tf_op jit(solution)/shard_map/pallas_call | solution.py:63
  244.3 5.3 %shard_map.316 = (bf16[4,96,384]{2,1,0:T(8,128)(2,1)}, bf16[4,96,384]{2,1,0:T(8,128)(2,1)}, f32[512,768]{1,0:T(8,128)}, f32[1,384]{1,0:T(1,128)}) custom-call(s32[2]{0:T(128)} %pad_add_fusion.8.here, bf16[256,768]{1,0:T(8,128)(2,1)} %get-tuple-element.195.own, bf16[256,768]{1,0:T(8,128)(2,1)} %copy-done, bf16[3,2,384,384]{3,2,1,0:T(8,128)(2,1)} %get-tuple-element.87.w_full, ...), custom_call_target="tpu_custom_call" | custom-call | tf_op jit(solution)/shard_map/pallas_call | solution.py:63
  258.7 11.3 %collective-permute-done.36 = bf16[2,96,384]{2,1,0:T(8,128)(2,1)S(1)} collective-permute-done((bf16[2,96,384]{2,1,0:T(8,128)(2,1)S(1)}, bf16[2,96,384]{2,1,0:T(8,128)(2,1)S(1)}, u32[]{:S(2)}, u32[]{:S(2)}) %collective-permute-start.36) | collective-permute-done | bytes 147488 | tf_op jit(solution)/shard_map/ppermute | solution.py:27
  270.1 3.1 collective-permute-start.37
  288.1 3.4 collective-permute-done.40
  296.7 4.0 collective-permute-done.29
  304.6 5.6 %shard_map.317 = (bf16[4,192,384]{2,1,0:T(8,128)(2,1)}, bf16[4,192,384]{2,1,0:T(8,128)(2,1)}, f32[256,768]{1,0:T(8,128)}, bf16[256,768]{1,0:T(8,128)(2,1)}, f32[1,384]{1,0:T(1,128)}) custom-call(s32[2]{0:T(128)} %pad_add_fusion.8.here, bf16[256,768]{1,0:T(8,128)(2,1)} %get-tuple-element.195.own, bf16[256,768]{1,0:T(8,128)(2,1)} %copy-done, ...), custom_call_target="tpu_custom_call" | custom-call | tf_op jit(solution)/shard_map/pallas_call | solution.py:63
  315.6 5.2 %collective-permute-done.50 = bf16[2,192,384]{2,1,0:T(8,128)(2,1)S(1)} collective-permute-done((bf16[2,192,384]{2,1,0:T(8,128)(2,1)S(1)}, bf16[2,192,384]{2,1,0:T(8,128)(2,1)S(1)}, u32[]{:S(2)}, u32[]{:S(2)}) %collective-permute-start.50) | collective-permute-done | bytes 294944 | tf_op jit(solution)/shard_map/ppermute | solution.py:27
  343.4 13.4 %collective-permute-done.43 = bf16[2,192,384]{2,1,0:T(8,128)(2,1)S(1)} collective-permute-done((bf16[2,192,384]{2,1,0:T(8,128)(2,1)S(1)}, bf16[2,192,384]{2,1,0:T(8,128)(2,1)S(1)}, u32[]{:S(2)}, u32[]{:S(2)}) %collective-permute-start.43) | collective-permute-done | bytes 294944 | tf_op jit(solution)/shard_map/ppermute | solution.py:27
  359.1 3.0 collective-permute-done.44
  383.8 17.4 %collective-permute-done.65 = bf16[1,384,384]{2,1,0:T(8,128)(2,1)S(1)} collective-permute-done((bf16[1,384,384]{2,1,0:T(8,128)(2,1)S(1)}, bf16[1,384,384]{2,1,0:T(8,128)(2,1)S(1)}, u32[]{:S(2)}, u32[]{:S(2)}) %collective-permute-start.65) | collective-permute-done | bytes 294944 | tf_op jit(solution)/shard_map/ppermute | solution.py:27
  413.8 4.7 %collective-permute-done.59 = bf16[288,384]{1,0:T(8,128)(2,1)S(1)} collective-permute-done((bf16[288,384]{1,0:T(8,128)(2,1)S(1)}, bf16[288,384]{1,0:T(8,128)(2,1)S(1)}, u32[]{:S(2)}, u32[]{:S(2)}) %collective-permute-start.59) | collective-permute-done | bytes 221216 | tf_op jit(solution)/shard_map/ppermute | solution.py:27
  420.8 4.2 collective-permute-done.60
  427.6 3.3 collective-permute-done.61
  433.6 3.5 collective-permute-done.62
  (448 shorter events, 182.5 us)
Async XLA Ops:
  6.6 48.1 %collective-permute-start = (bf16[256,768]{1,0:T(8,128)(2,1)}, bf16[256,768]{1,0:T(8,128)(2,1)S(1)}, u32[]{:S(2)}, u32[]{:S(2)}) collective-permute-start(bf16[256,768]{1,0:T(8,128)(2,1)} %get-tuple-element.194), channel_id=1, source_target_pairs={{0,4},{4,0},{1,5},{5,1},{2,6},{6,2},{3,7},{7,3},{8,12},{12,8},{9,1... | collective-permute-start | bytes 1179656 | tf_op jit(solution)/shard_map/ppermute | solution.py:27
  6.7 17.9 %collective-permute-start.5 = (bf16[1,288,384]{2,1,0:T(8,128)(2,1)S(1)}, bf16[1,288,384]{2,1,0:T(8,128)(2,1)S(1)}, u32[]{:S(2)}, u32[]{:S(2)}) collective-permute-start(bf16[1,288,384]{2,1,0:T(8,128)(2,1)S(1)} %bitcast.257), channel_id=1, source_target_pairs={{0,4},{4,0},{1,5},{5,1},{2,6},{6,2},{3,7},{7,3},{8,12},{12,8},{9,1... | collective-permute-start | bytes 663560 | tf_op jit(solution)/shard_map/ppermute | solution.py:27
  8.7 29.7 %collective-permute-start.16 = (bf16[1,192,384]{2,1,0:T(8,128)(2,1)S(1)}, bf16[1,192,384]{2,1,0:T(8,128)(2,1)}, u32[]{:S(2)}, u32[]{:S(2)}) collective-permute-start(bf16[1,192,384]{2,1,0:T(8,128)(2,1)S(1)} %bitcast.262), channel_id=1, source_target_pairs={{0,2},{1,3},{2,0},{3,1},{4,6},{5,7},{6,4},{7,5},{8,10},{9,11},{10,... | collective-permute-start | bytes 442376 | tf_op jit(solution)/shard_map/ppermute | solution.py:27
  10.4 16.1 %collective-permute-start.22 = (bf16[1,576,384]{2,1,0:T(8,128)(2,1)S(1)}, bf16[1,576,384]{2,1,0:T(8,128)(2,1)S(1)}, u32[]{:S(2)}, u32[]{:S(2)}) collective-permute-start(bf16[1,576,384]{2,1,0:T(8,128)(2,1)S(1)} %maximum_bitcast_fusion), channel_id=1, source_target_pairs={{0,2},{1,3},{2,0},{3,1},{4,6},{5,7},{6,4},{7,5},{8,10},{9,11},{10,... | collective-permute-start | bytes 1327112 | tf_op jit(solution)/shard_map/ppermute | solution.py:27
  24.2 17.5 %collective-permute-start.19 = (bf16[1,384,384]{2,1,0:T(8,128)(2,1)S(1)}, bf16[1,384,384]{2,1,0:T(8,128)(2,1)S(1)}, u32[]{:S(2)}, u32[]{:S(2)}) collective-permute-start(bf16[1,384,384]{2,1,0:T(8,128)(2,1)S(1)} %bitcast.253), channel_id=1, source_target_pairs={{0,4},{4,0},{1,5},{5,1},{2,6},{6,2},{3,7},{7,3},{8,12},{12,8},{9,1... | collective-permute-start | bytes 884744 | tf_op jit(solution)/shard_map/ppermute | solution.py:27
  27.5 25.7 %collective-permute-start.23 = (bf16[2,576,384]{2,1,0:T(8,128)(2,1)}, bf16[2,576,384]{2,1,0:T(8,128)(2,1)}, u32[]{:S(2)}, u32[]{:S(2)}) collective-permute-start(bf16[2,576,384]{2,1,0:T(8,128)(2,1)} %pad_maximum_fusion.3), channel_id=1, source_target_pairs={{0,4},{4,0},{1,5},{5,1},{2,6},{6,2},{3,7},{7,3},{8,12},{12,8},{9,1... | collective-permute-start | bytes 2654216 | tf_op jit(solution)/shard_map/ppermute | solution.py:27
  38.0 19.0 %collective-permute-start.7 = (bf16[4,288,384]{2,1,0:T(8,128)(2,1)S(1)}, bf16[4,288,384]{2,1,0:T(8,128)(2,1)}, u32[]{:S(2)}, u32[]{:S(2)}) collective-permute-start(bf16[4,288,384]{2,1,0:T(8,128)(2,1)S(1)} %pad_maximum_fusion.2.w_own), channel_id=1, source_target_pairs={{0,1},{1,0},{2,3},{3,2},{4,5},{5,4},{6,7},{7,6},{8,9},{9,8},{10,11... | collective-permute-start | bytes 2654216 | tf_op jit(solution)/shard_map/ppermute | solution.py:27
  40.1 22.6 %collective-permute-start.17 = (bf16[2,192,384]{2,1,0:T(8,128)(2,1)}, bf16[2,192,384]{2,1,0:T(8,128)(2,1)}, u32[]{:S(2)}, u32[]{:S(2)}) collective-permute-start(bf16[2,192,384]{2,1,0:T(8,128)(2,1)} %pad_maximum_fusion.11), channel_id=1, source_target_pairs={{0,4},{4,0},{1,5},{5,1},{2,6},{6,2},{3,7},{7,3},{8,12},{12,8},{9,1... | collective-permute-start | bytes 884744 | tf_op jit(solution)/shard_map/ppermute | solution.py:27
  42.7 21.9 %collective-permute-start.20 = (bf16[2,384,384]{2,1,0:T(8,128)(2,1)}, bf16[2,384,384]{2,1,0:T(8,128)(2,1)}, u32[]{:S(2)}, u32[]{:S(2)}) collective-permute-start(bf16[2,384,384]{2,1,0:T(8,128)(2,1)} %pad_maximum_fusion.5), channel_id=1, source_target_pairs={{0,2},{1,3},{2,0},{3,1},{4,6},{5,7},{6,4},{7,5},{8,10},{9,11},{10,... | collective-permute-start | bytes 1769480 | tf_op jit(solution)/shard_map/ppermute | solution.py:27
  54.6 65.7 %collective-permute-start.24 = (bf16[4,576,384]{2,1,0:T(8,128)(2,1)S(1)}, bf16[4,576,384]{2,1,0:T(8,128)(2,1)}, u32[]{:S(2)}, u32[]{:S(2)}) collective-permute-start(bf16[4,576,384]{2,1,0:T(8,128)(2,1)S(1)} %pad_maximum_fusion.tail_own), channel_id=1, source_target_pairs={{0,1},{1,0},{2,3},{3,2},{4,5},{5,4},{6,7},{7,6},{8,9},{9,8},{10,11... | collective-permute-start | bytes 5308424 | tf_op jit(solution)/shard_map/ppermute | solution.py:27
  64.6 19.9 %collective-permute-start.18 = (bf16[4,192,384]{2,1,0:T(8,128)(2,1)}, bf16[4,192,384]{2,1,0:T(8,128)(2,1)}, u32[]{:S(2)}, u32[]{:S(2)}) collective-permute-start(bf16[4,192,384]{2,1,0:T(8,128)(2,1)} %pad_maximum_fusion.4.w_own), channel_id=1, source_target_pairs={{0,1},{1,0},{2,3},{3,2},{4,5},{5,4},{6,7},{7,6},{8,9},{9,8},{10,11... | collective-permute-start | bytes 1769480 | tf_op jit(solution)/shard_map/ppermute | solution.py:27
  68.5 51.9 %collective-permute-start.21 = (bf16[4,384,384]{2,1,0:T(8,128)(2,1)}, bf16[4,384,384]{2,1,0:T(8,128)(2,1)}, u32[]{:S(2)}, u32[]{:S(2)}) collective-permute-start(bf16[4,384,384]{2,1,0:T(8,128)(2,1)} %pad_maximum_fusion.1.inner_own), channel_id=1, source_target_pairs={{0,1},{1,0},{2,3},{3,2},{4,5},{5,4},{6,7},{7,6},{8,9},{9,8},{10,11... | collective-permute-start | bytes 3538952 | tf_op jit(solution)/shard_map/ppermute | solution.py:27
  84.5 23.2 %collective-permute-start.11 = (bf16[2,512,256]{2,1,0:T(8,128)(2,1)}, bf16[2,512,256]{2,1,0:T(8,128)(2,1)}, u32[]{:S(2)}, u32[]{:S(2)}) collective-permute-start(bf16[2,512,256]{2,1,0:T(8,128)(2,1)} %pad_maximum_fusion.7.kv_own), channel_id=1, source_target_pairs={{0,1},{1,0},{2,3},{3,2},{4,5},{5,4},{6,7},{7,6},{8,9},{9,8},{10,11... | collective-permute-start | bytes 1572872 | tf_op jit(solution)/shard_map/ppermute | solution.py:27
  84.5 29.5 %collective-permute-start.9 = (bf16[2,512,256]{2,1,0:T(8,128)(2,1)S(1)}, bf16[2,512,256]{2,1,0:T(8,128)(2,1)}, u32[]{:S(2)}, u32[]{:S(2)}) collective-permute-start(bf16[2,512,256]{2,1,0:T(8,128)(2,1)S(1)} %pad_maximum_fusion.6.kv_own), channel_id=1, source_target_pairs={{0,1},{1,0},{2,3},{3,2},{4,5},{5,4},{6,7},{7,6},{8,9},{9,8},{10,11... | collective-permute-start | bytes 1572872 | tf_op jit(solution)/shard_map/ppermute | solution.py:27
  86.5 33.9 %collective-permute-start.1 = (bf16[256,768]{1,0:T(8,128)(2,1)}, bf16[256,768]{1,0:T(8,128)(2,1)}, u32[]{:S(2)}, u32[]{:S(2)}) collective-permute-start(bf16[256,768]{1,0:T(8,128)(2,1)} %get-tuple-element.192), channel_id=1, source_target_pairs={{0,4},{4,0},{1,5},{5,1},{2,6},{6,2},{3,7},{7,3},{8,12},{12,8},{9,1... | collective-permute-start | bytes 1179656 | tf_op jit(solution)/shard_map/ppermute | solution.py:27
  154.6 43.1 %collective-permute-start.75 = (f32[64,128]{1,0:T(8,128)}, f32[64,128]{1,0:T(8,128)}, u32[]{:S(2)}, u32[]{:S(2)}) collective-permute-start(f32[64,128]{1,0:T(8,128)} %fusion.53), channel_id=1, source_target_pairs={{0,1},{1,0},{2,3},{3,2},{4,5},{5,4},{6,7},{7,6},{8,9},{9,8},{10,11... | collective-permute-start | bytes 98312 | tf_op jit(solution)/shard_map/ppermute | solution.py:27
  172.5 40.4 %collective-permute-start.33 = (bf16[2,8,1152]{2,1,0:T(8,128)(2,1)}, bf16[2,8,1152]{2,1,0:T(8,128)(2,1)}, u32[]{:S(2)}, u32[]{:S(2)}) collective-permute-start(bf16[2,8,1152]{2,1,0:T(8,128)(2,1)} %pad_maximum_fusion.17), channel_id=1, source_target_pairs={{0,1},{1,2},{2,3},{3,0},{4,5},{5,6},{6,7},{7,4},{8,9},{9,10},{10,1... | collective-permute-start | bytes 110600 | tf_op jit(solution)/shard_map/ppermute | solution.py:32
  173.7 62.6 %collective-permute-start.32 = (bf16[2,8,1152]{2,1,0:T(8,128)(2,1)}, bf16[2,8,1152]{2,1,0:T(8,128)(2,1)}, u32[]{:S(2)}, u32[]{:S(2)}) collective-permute-start(bf16[2,8,1152]{2,1,0:T(8,128)(2,1)} %pad_maximum_fusion.16), channel_id=1, source_target_pairs={{0,3},{1,0},{2,1},{3,2},{4,7},{5,4},{6,5},{7,6},{8,11},{9,8},{10,9... | collective-permute-start | bytes 110600 | tf_op jit(solution)/shard_map/ppermute | solution.py:32
  186.4 89.9 %collective-permute-start.30 = (bf16[2,512,256]{2,1,0:T(8,128)(2,1)}, bf16[2,512,256]{2,1,0:T(8,128)(2,1)}, u32[]{:S(2)}, u32[]{:S(2)}) collective-permute-start(bf16[2,512,256]{2,1,0:T(8,128)(2,1)} %get-tuple-element.99), channel_id=1, source_target_pairs={{0,1},{1,0},{2,3},{3,2},{4,5},{5,4},{6,7},{7,6},{8,9},{9,8},{10,11... | collective-permute-start | bytes 1572872 | tf_op jit(solution)/shard_map/ppermute | solution.py:27
  196.1 84.2 %collective-permute-start.28 = (bf16[2,512,256]{2,1,0:T(8,128)(2,1)}, bf16[2,512,256]{2,1,0:T(8,128)(2,1)}, u32[]{:S(2)}, u32[]{:S(2)}) collective-permute-start(bf16[2,512,256]{2,1,0:T(8,128)(2,1)} %get-tuple-element.95), channel_id=1, source_target_pairs={{0,1},{1,0},{2,3},{3,2},{4,5},{5,4},{6,7},{7,6},{8,9},{9,8},{10,11... | collective-permute-start | bytes 1572872 | tf_op jit(solution)/shard_map/ppermute | solution.py:27
  211.9 74.9 %collective-permute-start.26 = (bf16[2,512,256]{2,1,0:T(8,128)(2,1)}, bf16[2,512,256]{2,1,0:T(8,128)(2,1)S(1)}, u32[]{:S(2)}, u32[]{:S(2)}) collective-permute-start(bf16[2,512,256]{2,1,0:T(8,128)(2,1)} %get-tuple-element.91), channel_id=1, source_target_pairs={{0,1},{1,0},{2,3},{3,2},{4,5},{5,4},{6,7},{7,6},{8,9},{9,8},{10,11... | collective-permute-start | bytes 1572872 | tf_op jit(solution)/shard_map/ppermute | solution.py:27
  216.9 32.7 %collective-permute-start.78 = (f32[64,128]{1,0:T(8,128)S(1)}, f32[64,128]{1,0:T(8,128)S(1)}, u32[]{:S(2)}, u32[]{:S(2)}) collective-permute-start(f32[64,128]{1,0:T(8,128)S(1)} %add.366), channel_id=1, source_target_pairs={{0,8},{8,0},{16,24},{24,16},{1,9},{9,1},{17,25},{25,17},{2,10},{10... | collective-permute-start | bytes 98312 | tf_op jit(solution)/shard_map/ppermute | solution.py:27
  270.0 106.6 %collective-permute-start.56 = (bf16[4,576,384]{2,1,0:T(8,128)(2,1)}, bf16[4,576,384]{2,1,0:T(8,128)(2,1)}, u32[]{:S(2)}, u32[]{:S(2)}) collective-permute-start(bf16[4,576,384]{2,1,0:T(8,128)(2,1)} %get-tuple-element.126), channel_id=1, source_target_pairs={{0,1},{1,0},{2,3},{3,2},{4,5},{5,4},{6,7},{7,6},{8,9},{9,8},{10,11... | collective-permute-start | bytes 5308424 | tf_op jit(solution)/shard_map/ppermute | solution.py:27
  276.2 55.5 %collective-permute-start.63 = (bf16[4,384,384]{2,1,0:T(8,128)(2,1)}, bf16[4,384,384]{2,1,0:T(8,128)(2,1)S(1)}, u32[]{:S(2)}, u32[]{:S(2)}) collective-permute-start(bf16[4,384,384]{2,1,0:T(8,128)(2,1)} %get-tuple-element.128), channel_id=1, source_target_pairs={{0,1},{1,0},{2,3},{3,2},{4,5},{5,4},{6,7},{7,6},{8,9},{9,8},{10,11... | collective-permute-start | bytes 3538952 | tf_op jit(solution)/shard_map/ppermute | solution.py:27
  280.3 30.8 %collective-permute-start.49 = (bf16[4,192,384]{2,1,0:T(8,128)(2,1)}, bf16[4,192,384]{2,1,0:T(8,128)(2,1)S(1)}, u32[]{:S(2)}, u32[]{:S(2)}) collective-permute-start(bf16[4,192,384]{2,1,0:T(8,128)(2,1)} %get-tuple-element.124), channel_id=1, source_target_pairs={{0,1},{1,0},{2,3},{3,2},{4,5},{5,4},{6,7},{7,6},{8,9},{9,8},{10,11... | collective-permute-start | bytes 1769480 | tf_op jit(solution)/shard_map/ppermute | solution.py:27
  336.6 44.6 %collective-permute-start.64 = (bf16[2,384,384]{2,1,0:T(8,128)(2,1)}, bf16[2,384,384]{2,1,0:T(8,128)(2,1)}, u32[]{:S(2)}, u32[]{:S(2)}) collective-permute-start(bf16[2,384,384]{2,1,0:T(8,128)(2,1)} %slice.360), channel_id=1, source_target_pairs={{0,2},{1,3},{2,0},{3,1},{4,6},{5,7},{6,4},{7,5},{8,10},{9,11},{10,... | collective-permute-start | bytes 1769480 | tf_op jit(solution)/shard_map/ppermute | solution.py:27
  337.9 19.5 %collective-permute-start.54 = (bf16[48,384]{1,0:T(8,128)(2,1)S(1)}, bf16[48,384]{1,0:T(8,128)(2,1)S(1)}, u32[]{:S(2)}, u32[]{:S(2)}) collective-permute-start(bf16[48,384]{1,0:T(8,128)(2,1)S(1)} %fusion.35), channel_id=1, source_target_pairs={{0,16},{8,24},{16,0},{24,8},{1,17},{9,25},{17,1},{25,9},{2,18},{10... | collective-permute-start | bytes 110600 | tf_op jit(solution)/shard_map/ppermute | solution.py:27
  340.1 16.7 %collective-permute-start.43 = (bf16[2,192,384]{2,1,0:T(8,128)(2,1)S(1)}, bf16[2,192,384]{2,1,0:T(8,128)(2,1)S(1)}, u32[]{:S(2)}, u32[]{:S(2)}) collective-permute-start(bf16[2,192,384]{2,1,0:T(8,128)(2,1)S(1)} %slice.348), channel_id=1, source_target_pairs={{0,2},{1,3},{2,0},{3,1},{4,6},{5,7},{6,4},{7,5},{8,10},{9,11},{10,... | collective-permute-start | bytes 884744 | tf_op jit(solution)/shard_map/ppermute | solution.py:27
  342.3 16.8 %collective-permute-start.74 = (f32[232,128]{1,0:T(8,128)S(1)}, f32[232,128]{1,0:T(8,128)S(1)}, u32[]{:S(2)}, u32[]{:S(2)}) collective-permute-start(f32[232,128]{1,0:T(8,128)S(1)} %add.362), channel_id=1, source_target_pairs={{0,16},{8,24},{16,0},{24,8},{1,17},{9,25},{17,1},{25,9},{2,18},{10... | collective-permute-start | bytes 356360 | tf_op jit(solution)/shard_map/ppermute | solution.py:27
  358.1 25.6 %collective-permute-start.55 = (bf16[96,384]{1,0:T(8,128)(2,1)}, bf16[96,384]{1,0:T(8,128)(2,1)S(1)}, u32[]{:S(2)}, u32[]{:S(2)}) collective-permute-start(bf16[96,384]{1,0:T(8,128)(2,1)} %get-tuple-element.217), channel_id=1, source_target_pairs={{0,8},{8,0},{16,24},{24,16},{1,9},{9,1},{17,25},{25,17},{2,10},{10... | collective-permute-start | bytes 221192 | tf_op jit(solution)/shard_map/ppermute | solution.py:27
  378.6 23.5 %collective-permute-start.57 = (bf16[2,576,384]{2,1,0:T(8,128)(2,1)S(1)}, bf16[2,576,384]{2,1,0:T(8,128)(2,1)S(1)}, u32[]{:S(2)}, u32[]{:S(2)}) collective-permute-start(bf16[2,576,384]{2,1,0:T(8,128)(2,1)S(1)} %slice.356), channel_id=1, source_target_pairs={{0,4},{4,0},{1,5},{5,1},{2,6},{6,2},{3,7},{7,3},{8,12},{12,8},{9,1... | collective-permute-start | bytes 2654216 | tf_op jit(solution)/shard_map/ppermute | solution.py:27
  382.4 18.9 %collective-permute-start.65 = (bf16[1,384,384]{2,1,0:T(8,128)(2,1)S(1)}, bf16[1,384,384]{2,1,0:T(8,128)(2,1)S(1)}, u32[]{:S(2)}, u32[]{:S(2)}) collective-permute-start(bf16[1,384,384]{2,1,0:T(8,128)(2,1)S(1)} %slice.362), channel_id=1, source_target_pairs={{0,4},{4,0},{1,5},{5,1},{2,6},{6,2},{3,7},{7,3},{8,12},{12,8},{9,1... | collective-permute-start | bytes 884744 | tf_op jit(solution)/shard_map/ppermute | solution.py:27
  (105 other events, 908.8 us)

commit v3 on v2

--- a/solution.py
+++ b/solution.py
@@ -15,6 +15,7 @@
 PAIRS = HEADS // 2
 LANE = 128
 RIM = 8
+DOC_ROWS = 16
 
 EPSILON = 1e-12
 MASKED = -1e30
@@ -54,7 +55,7 @@
     return lax.dot_general(left, right, how, preferred_element_type=WIDE)
 
 
-def kernel_call(body, outs, scratch=(), smem=1, cost=None):
+def kernel_call(body, outs, scratch=(), smem=1, cost=5):
     def run(*args):
         specs = [
             pl.BlockSpec(memory_space=pltpu.SMEM if place < smem else pltpu.VMEM)
@@ -66,7 +67,9 @@
             out_specs=[pl.BlockSpec(memory_space=pltpu.VMEM)] * len(outs),
             out_shape=[jax.ShapeDtypeStruct(shape, kind) for shape, kind in outs],
             scratch_shapes=[pltpu.VMEM(shape, kind) for shape, kind in scratch],
-            cost_estimate=cost,
+            cost_estimate=pl.CostEstimate(
+                flops=int(cost * 1e9), bytes_accessed=int(cost * 3.6e6), transcendentals=0
+            ),
         )(*args)
 
     return run
@@ -84,40 +87,59 @@
     return row + far if kind == "row" else far[:1] + row + far[1:]
 
 
-def gather(slab, kind):
-    stack = slab[None]
-    for axis, step in stages_of(kind):
-        stack = jnp.concatenate([stack, swap(stack, axis, step)], axis=0)
-    return stack, swap(stack, "col", 1)
+def after(value, *marks):
+    return lax.optimization_barrier((value,) + marks)[0]
+
+
+def grow(stack, axis, step):
+    return jnp.concatenate([stack, swap(stack, axis, step)], axis=0)
 
 
 def add_low(kept, moved):
     return (kept.astype(WIDE) + moved.astype(WIDE)).astype(LOW)
 
 
-def scatter(kept, sent, kind):
-    stack = add_low(kept, swap(sent, "col", 1))
-    for axis, step in reversed(stages_of(kind)):
-        half = stack.shape[0] // 2
-        stack = add_low(stack[:half], swap(stack[half:], axis, step))
-    return stack[0]
-
-
-def data_sum(part):
-    index = lax.axis_index("dp")
-    steps = steps_of("dp")
-    sent = part.dtype
-    for step in steps:
-        bit = (index // step) % 2
-        halves = part.reshape((2, part.shape[0] // 2) + part.shape[1:])
-        moved = swap(pick(halves, 1 - bit), "dp", step)
-        part = (pick(halves, bit).astype(WIDE) + moved.astype(WIDE)).astype(sent)
-    for step in reversed(steps):
-        bit = (index // step) % 2
-        moved = swap(part, "dp", step)
-        both = jnp.stack([part, moved])
-        part = jnp.concatenate([pick(both, bit), pick(both, 1 - bit)], axis=0)
-    return part
+def join(kept, moved):
+    half = kept.shape[0] // 2
+    return add_low(kept[:half], moved[:half]), add_low(kept[half:], moved[half:])
+
+
+class DataSum:
+    def __init__(self, part):
+        self.index = lax.axis_index("dp")
+        steps = steps_of("dp")
+        self.todo = [(True, step) for step in steps] + [(False, step) for step in reversed(steps)]
+        self.part = part
+        self.start()
+
+    def start(self):
+        down, step = self.todo[0]
+        self.bit = (self.index // step) % 2
+        if down:
+            self.halves = self.part.reshape((2, self.part.shape[0] // 2) + self.part.shape[1:])
+            self.moved = swap(pick(self.halves, 1 - self.bit), "dp", step)
+        else:
+            self.moved = swap(self.part, "dp", step)
+
+    def finish(self, *marks):
+        moved = after(self.moved, *marks) if marks else self.moved
+        down, _ = self.todo.pop(0)
+        if down:
+            self.part = add_low(pick(self.halves, self.bit), moved)
+        else:
+            self.part = jnp.where(
+                self.bit == 0,
+                jnp.concatenate([self.part, moved], axis=0),
+                jnp.concatenate([moved, self.part], axis=0),
+            )
+        if self.todo:
+            self.start()
+        return self.part
+
+    def rest(self):
+        while self.todo:
+            self.finish()
+        return self.part
 
 
 def grid_sum(flat):
@@ -125,6 +147,16 @@
         for step in steps_of(axis):
             flat = flat + swap(flat, axis, step)
     return flat
+
+
+def assemble_pieces(here, pieces, full, parts, size):
+    for (dr, dc), piece in pieces:
+        row = here[0] ^ dr
+        col = here[1] ^ dc
+        for part in range(parts):
+            full[part, row, pl.ds(pl.multiple_of(col * size, 16), size), :] = piece[
+                part * size : (part + 1) * size, :
+            ]
 
 
 def assemble(here, stacks, kind, full, parts, size, start):
@@ -167,11 +199,12 @@
     return value[:, : value.shape[1] // 2], value[:, value.shape[1] // 2 :]
 
 
-def project_kernel(here, own, other, w_own, w_far, bias, query, *rest):
-    pairs, w_full = rest[:PAIRS], rest[PAIRS]
-    size = w_own.shape[1] // 3
+def project_kernel(keys, here, own, other, bias, *rest):
+    weights, rest = rest[: len(keys)], rest[len(keys) :]
+    query, pairs, w_full = rest[0], rest[1 : 1 + PAIRS], rest[1 + PAIRS]
+    size = (weights[0].shape[0] - DOC_ROWS) // 3
     block_len = own.shape[0]
-    assemble(here, (w_own, w_far), "row", w_full, 3, size, 0)
+    assemble_pieces(here, list(zip(keys, weights)), w_full, 3, size)
     for slot, source in enumerate((own, other)):
         left, right = half_pair(source[...])
         rows = pl.ds(slot * block_len, block_len)
@@ -215,32 +248,14 @@
 
 
 def branch_kernel(
-    here,
-    own,
-    other,
-    low_rim,
-    high_rim,
-    docs,
-    w_own,
-    w_far,
-    depth_gain,
-    bias,
-    tap_weight,
-    tap_bias,
-    query,
-    context,
-    depth_low,
-    value_wide,
-    key_conv,
-    conv_attn,
-    conv_weights,
-    w_full,
-    wide,
+    keys, here, own, other, low_rim, high_rim, docs, depth_gain, bias, tap_weight, tap_bias, query, *rest
 ):
-    size = w_own.shape[1] // 2
+    weights, rest = rest[: len(keys)], rest[len(keys) :]
+    context, depth_low, value_wide, key_conv, conv_attn, conv_weights, w_full, wide = rest
+    size = weights[0].shape[0] // 2
     block_len = own.shape[0]
     start = RIM - KERNEL // 2
-    assemble(here, (w_own, w_far), "col", w_full, 2, size, 0)
+    assemble_pieces(here, list(zip(keys, weights)), w_full, 2, size)
     spread = spread_heads()
     for slot, source in enumerate((own, other)):
         rows = slice(slot * block_len, (slot + 1) * block_len)
@@ -300,8 +315,10 @@
     return (bounds[block, 0] <= bounds[slot, 1]) & (bounds[block, 1] >= bounds[slot, 0])
 
 
-def attend_kernel(bounds, query, kv_own, kv_far, doc_query, doc_key, out, stats, scores, top, total, mixed):
-    entries, tokens_here, _ = kv_own.shape
+def attend_kernel(count, bounds, query, doc_query, doc_key, *rest):
+    stacks, rest = rest[:count], rest[count:]
+    out, stats, scores, top, total, mixed = rest
+    tokens_here = query.shape[0]
     block_len = tokens_here // 2
     score_scale = HEAD ** (-0.5)
     for slot in range(2):
@@ -314,22 +331,22 @@
         mixed[...] = jnp.zeros(mixed.shape, WIDE)
 
         def each(body):
-            for core, stack in enumerate((kv_own, kv_far)):
+            for place, stack in enumerate(stacks):
 
                 def one(step, carry):
-                    block = core * entries * 2 + step
+                    block = place * 2 + step
 
                     @pl.when(blocks_overlap(bounds, slot, block))
                     def _():
-                        keys = pl.ds(pl.multiple_of((step % 2) * block_len, 16), block_len)
-                        body(stack, step // 2, keys, block)
+                        keys = pl.ds(pl.multiple_of(step * block_len, 16), block_len)
+                        body(stack, keys, block)
 
                     return carry
 
-                lax.fori_loop(0, entries * 2, one, 0)
-
-        def first(stack, entry, keys, block):
-            key_rows = stack[entry, keys, :LANE]
+                lax.fori_loop(0, 2, one, 0)
+
+        def first(stack, keys, block):
+            key_rows = stack[keys, :LANE]
             doc_rows = doc_key[block]
             allowed = tile_lanes(doc_rows, block_len // LANE) == doc_here
             for head in range(2):
@@ -339,8 +356,8 @@
 
         each(first)
 
-        def second(stack, entry, keys, block):
-            value_rows = stack[entry, keys, LANE:]
+        def second(stack, keys, block):
+            value_rows = stack[keys, LANE:]
             for head in range(2):
                 term = jnp.exp(scores[block, head] - top[head, 0:1, :])
                 total[head] = total[head] + jnp.sum(term, axis=0, keepdims=True)
@@ -355,23 +372,10 @@
         out[rows, :] = jnp.concatenate(parts, axis=0).T.astype(LOW)
 
 
-def attend_back_kernel(
-    bounds,
-    query,
-    kv_own,
-    kv_far,
-    doc_query,
-    doc_key,
-    attended,
-    grad,
-    stats,
-    grad_query,
-    grad_own,
-    grad_far,
-    delta,
-    grad_kv,
-):
-    entries, tokens_here, _ = kv_own.shape
+def attend_back_kernel(count, bounds, query, doc_query, doc_key, attended, grad, stats, *rest):
+    stacks, rest = rest[:count], rest[count:]
+    grad_query, grad_own, grad_far, delta, grad_kv = rest
+    tokens_here = query.shape[0]
     block_len = tokens_here // 2
     score_scale = HEAD ** (-0.5)
     head_row = lax.broadcasted_iota(jnp.int32, (8, LANE), 0)
@@ -384,20 +388,21 @@
         delta[slot] = mm(chosen, high, NT) + mm(chosen, low, NT)
     grad_query[...] = jnp.zeros(grad_query.shape, WIDE)
 
-    for core, (stack, out) in enumerate(((kv_own, grad_own), (kv_far, grad_far))):
+    for place, stack in enumerate(stacks):
+        out = (grad_own, grad_far)[2 * place // count]
+        entry = place % (count // 2)
 
         def one(step, carry):
-            block = core * entries * 2 + step
-            keys = pl.ds(pl.multiple_of((step % 2) * block_len, 16), block_len)
-            entry = step // 2
+            block = place * 2 + step
+            keys = pl.ds(pl.multiple_of(step * block_len, 16), block_len)
             grad_kv[...] = jnp.zeros(grad_kv.shape, WIDE)
             for slot in range(2):
 
                 @pl.when(blocks_overlap(bounds, slot, block))
                 def _():
                     rows = slice(slot * block_len, (slot + 1) * block_len)
-                    key_rows = stack[entry, keys, :LANE]
-                    value_rows = stack[entry, keys, LANE:]
+                    key_rows = stack[keys, :LANE]
+                    value_rows = stack[keys, LANE:]
                     scaled = query[rows, :] * jnp.asarray(score_scale, LOW)
                     allowed = tile_lanes(doc_key[block], block_len // LANE) == doc_query[slot : slot + 1, :]
                     for head in range(2):
@@ -417,7 +422,7 @@
             out[entry, keys, :] = grad_kv[...].astype(LOW)
             return carry
 
-        lax.fori_loop(0, entries * 2, one, 0)
+        lax.fori_loop(0, 2, one, 0)
     grad_query[...] = grad_query[...] * score_scale
 
 
@@ -613,6 +618,7 @@
     d_tap_weight,
     d_tap_bias,
     d_depth,
+    bias_grad,
     g_ext_value,
     g_ext_tokens,
     wide,
@@ -625,6 +631,7 @@
     d_tap_weight[...] = jnp.zeros(d_tap_weight.shape, WIDE)
     d_tap_bias[...] = jnp.zeros(d_tap_bias.shape, WIDE)
     d_depth[...] = jnp.zeros(d_depth.shape, WIDE)
+    bias_grad[...] = jnp.zeros(bias_grad.shape, WIDE)
     g_ext_value[...] = jnp.zeros(g_ext_value.shape, WIDE)
     g_ext_tokens[...] = jnp.zeros(g_ext_tokens.shape, WIDE)
     for slot, source in enumerate((own, other)):
@@ -650,6 +657,8 @@
         g_attn = mm(low_grad[...], tap_weight[...], NT)
         g_key = (g_attn * query[rows, :].astype(WIDE)).astype(LOW)
         g_key_conv[rows, :] = g_key
+        bias_grad[0:1, :] += column_sum(g_ext_value[slot])
+        bias_grad[1:2, :] += column_sum(g_key.astype(WIDE))
         g_query[rows, :] = g_attn * key_conv[rows, :]
         for half in range(2):
             g_depth = mm(g_key, w_full[1, half], NN)
@@ -679,7 +688,6 @@
     d_own,
     d_far,
     token_grad,
-    bias_grad,
     ext,
     d_full,
     tokens,
@@ -701,8 +709,6 @@
             + ext[:, ATT:]
             + two(mm(low, w_full[0, 0], NN), mm(low, w_full[0, 1], NN))
         )
-    bias_grad[0:1, :] = column_sum(value_grad[...].astype(WIDE))
-    bias_grad[1:2, :] = column_sum(g_key_conv[...].astype(WIDE))
     for half in range(2):
         lanes = slice(half * d_own.shape[2], (half + 1) * d_own.shape[2])
         d_full[0, half] = mm(value_grad[...], tokens[:, lanes], TN).astype(LOW)
@@ -710,47 +716,53 @@
     cut(here, d_full, (d_own, d_far), "col", 2, size, 0)
 
 
-def query_weights_kernel(
-    here, own, other, w_full, grad_0, grad_1, grad_2, g_query, token_in, d_own, d_far, token_grad, bias_grad, d_full, tokens
+def first_weights_kernel(
+    here,
+    own,
+    other,
+    grad_0,
+    grad_1,
+    grad_2,
+    g_query,
+    pair_0,
+    pair_1,
+    pair_2,
+    d_own,
+    d_far,
+    lows,
+    bias_grad,
+    d_full,
+    tokens,
 ):
     block_len = own.shape[0]
-    size = d_own.shape[1]
-    low = (jnp.concatenate([grad_0[...], grad_1[...], grad_2[...]], axis=1) + g_query[...]).astype(LOW)
-    bias_grad[...] = column_sum(low.astype(WIDE))
-    for slot, source in enumerate((own, other)):
-        tokens[slot * block_len : (slot + 1) * block_len, :] = source[...]
-    token_grad[...] = token_in[...] + two(mm(low, w_full[0, 0], NN), mm(low, w_full[0, 1], NN))
-    for half in range(2):
-        lanes = slice(half * d_own.shape[2], (half + 1) * d_own.shape[2])
-        d_full[0, half] = mm(low, tokens[:, lanes], TN).astype(LOW)
-    cut(here, d_full, (d_own, d_far), "col", 1, size, 0)
-
-
-def pair_weights_kernel(
-    here, own, other, w_full, pair_0, pair_1, pair_2, token_in, d_own, d_far, token_own, token_other, bias_grad, d_full, tokens
-):
-    block_len = own.shape[0]
-    size = d_own.shape[1] // 2
+    size = d_own.shape[1] // 3
     pairs = (pair_0, pair_1, pair_2)
     for slot, source in enumerate((own, other)):
         tokens[slot * block_len : (slot + 1) * block_len, :] = source[...]
-    lows = [
-        jnp.concatenate([pair[:, part * LANE : (part + 1) * LANE] for pair in pairs], axis=1)
-        for part in range(2)
-    ]
-    bias_grad[...] = column_sum(lows[1].astype(WIDE))
+    lows[0] = (
+        jnp.concatenate([grad_0[...], grad_1[...], grad_2[...]], axis=1) + g_query[...]
+    ).astype(LOW)
     for part in range(2):
+        lows[1 + part] = jnp.concatenate(
+            [pair[:, part * LANE : (part + 1) * LANE] for pair in pairs], axis=1
+        )
+    bias_grad[0:1, :] = column_sum(lows[0].astype(WIDE))
+    bias_grad[1:2, :] = column_sum(lows[2].astype(WIDE))
+    for part in range(3):
         for half in range(2):
             lanes = slice(half * d_own.shape[2], (half + 1) * d_own.shape[2])
             d_full[part, half] = mm(lows[part], tokens[:, lanes], TN).astype(LOW)
-    cut(here, d_full, (d_own, d_far), "row", 2, size, 0)
+    cut(here, d_full, (d_own, d_far), "row", 3, size, 0)
+
+
+def token_kernel(w_full, lows, token_in, token_own, token_other):
+    block_len = token_own.shape[0]
     for slot, out in enumerate((token_own, token_other)):
         rows = slice(slot * block_len, (slot + 1) * block_len)
         total = token_in[rows, :]
-        for part in range(2):
-            total = total + two(
-                mm(lows[part][rows], w_full[part + 1, 0], NN), mm(lows[part][rows], w_full[part + 1, 1], NN)
-            )
+        for part in range(3):
+            low = lows[part, rows, :]
+            total = total + two(mm(low, w_full[part, 0], NN), mm(low, w_full[part, 1], NN))
         out[...] = total.astype(out.dtype)
 
 
@@ -790,14 +802,42 @@
     cut_inner = inner_weight.shape[2]
     lanes = proj_weight.shape[1]
 
+    far_steps = [step for step in steps_of("col") if step > 1]
+
     proj_t = jnp.transpose(proj_weight, (0, 2, 1))
-    first_own, first_far = gather(proj_t[:3].reshape(-1, lanes), "row")
-
-    def trade(pair):
-        return pick(pair, row_here), swap(pick(pair, 1 - row_here), "row", 1)
-
-    own, other = trade(tokens)
-    branch_own, branch_far = gather(proj_t[3:].reshape(-1, lanes), "col")
+    doc_slab = jnp.pad(
+        doc_ids[:, 0].astype(LOW), ((0, DOC_ROWS - doc_ids.shape[0]), (0, lanes - block_len))
+    )
+    first = {(0, 0): jnp.concatenate([proj_t[:3].reshape(-1, lanes), doc_slab], axis=0)}
+    branch = {(0, 0): proj_t[3:].reshape(-1, lanes)}
+
+    def spread_row(held, *marks):
+        for dr, dc in list(held):
+            held[(1, dc)] = swap(after(held[(dr, dc)], *marks), "row", 1)
+
+    def spread_col(held, step):
+        for dr, dc in list(held):
+            held[(dr, dc ^ step)] = swap(held[(dr, dc)], "col", step)
+
+    def trade(pair, *marks):
+        sent = pick(pair, 1 - row_here)
+        if marks:
+            sent = after(sent, *marks)
+        return pick(pair, row_here), swap(sent, "row", 1)
+
+    spread_row(first)
+    first_row = first[(1, 0)]
+    for step in far_steps:
+        spread_col(first, step)
+    own, other = trade(tokens, first_row)
+    for dr, dc in list(first):
+        first[(dr, dc ^ 1)] = swap(first[(dr, dc)], "col", 1)
+    branch[(0, 0)] = after(branch[(0, 0)], first[(0, far_steps[0])])
+    for step in far_steps:
+        spread_col(branch, step)
+    spread_row(branch, other)
+    for dr, dc in list(branch):
+        branch[(dr, dc ^ 1)] = swap(branch[(dr, dc)], "col", 1)
 
     def wrapped(block, step):
         moved = shift(block, "col", step)
@@ -807,39 +847,15 @@
     low_rim = wrapped(jnp.stack([own[block_len - RIM :], other[block_len - RIM :]]), 1)
     high_rim = wrapped(jnp.stack([own[:RIM], other[:RIM]]), -1)
 
-    docs = jnp.stack(trade(doc_ids[:, 0]))[None]
-    far_steps = [step for step in steps_of("col") if step > 1]
-    for step in far_steps + [1]:
-        docs = jnp.concatenate([docs, swap(docs, "col", step)], axis=0)
-    relative = [0]
-    for step in far_steps + [1]:
-        relative = relative + [entry ^ step for entry in relative]
-    doc_blocks = docs.reshape(-1, block_len)
-    bounds = jnp.stack([doc_blocks[:, 0], doc_blocks[:, -1]], axis=1)
-    doc_key = jnp.broadcast_to(doc_blocks[:, :, None], doc_blocks.shape + (LANE,))
-    ordered = jnp.stack([docs[relative.index(dc)] for dc in range(col_count)])
-
-    def doc_rim(slot, step):
-        position = (row_here ^ slot) * col_count + col_here + step
-        inside = (position >= 0) & (position < row_count * col_count)
-        position = jnp.clip(position, 0, row_count * col_count - 1)
-        dr = (position // col_count) ^ row_here
-        dc = (position % col_count) ^ col_here
-        return jnp.where(inside, pick(pick(ordered, dc), dr), -1)
-
-    doc_ext = jnp.stack(
-        [
-            jnp.concatenate(
-                [doc_rim(slot, -1)[block_len - RIM :], docs[0, slot], doc_rim(slot, 1)[:RIM]]
-            )
-            for slot in range(2)
-        ]
+    inner = grow(after(inner_weight[0].T, other, branch[(1, 0)])[None], "row", 1)
+    inner_row = inner
+    tail = grow(
+        after(
+            jnp.concatenate([outer_weight[0], out_weight.T], axis=0), first[(1, far_steps[-1])]
+        )[None],
+        "col",
+        far_steps[0],
     )
-    doc_rows = jnp.broadcast_to(doc_ext[:, :, None], doc_ext.shape + (LANE,))
-
-    inner_own, inner_far = gather(inner_weight[0].T, "row")
-    tail_own, tail_far = gather(jnp.concatenate([outer_weight[0], out_weight.T], axis=0), "col")
-    cot_own, cot_other = trade(cotangent)
 
     wide_bias = proj_bias.astype(WIDE)
     tap_weight = jnp.pad(
@@ -856,25 +872,65 @@
         [out_bias, norm1_gain, norm1_shift, outer_bias, norm2_gain, norm2_shift, norm2_shift, norm2_shift]
     ).astype(WIDE)
 
+    first_keys = sorted(first, key=lambda key: (key[1] & 1, key[1], key[0]))
     query, *pairs = kernel_call(
-        project_kernel,
+        functools.partial(project_kernel, first_keys),
         [((tokens_here, ATT), LOW)]
         + [((tokens_here, 2 * LANE), LOW)] * PAIRS
         + [((3, row_count, ATT, lanes), LOW)],
-    )(here, own, other, first_own, first_far, wide_bias)
+    )(here, own, other, wide_bias, *[first[key] for key in first_keys])
     w_first = pairs.pop()
 
-    def gather_pair(pair):
-        stack = pair[None]
+    gathered = []
+    for pair in pairs:
+        pieces = [pair]
         for step in far_steps:
-            stack = jnp.concatenate([stack, swap(stack, "col", step)], axis=0)
-        return stack, swap(stack, "col", 1)
-
-    gathered = [gather_pair(pair) for pair in pairs]
+            pieces = pieces + [swap(piece, "col", step) for piece in pieces]
+        gathered.append(pieces)
+    far_pair = gathered[0][1]
+    for pieces in gathered:
+        pieces.extend([swap(piece, "col", 1) for piece in list(pieces)])
+    tail = grow(after(tail, inner_row, query), "row", 1)
+    inner = after(inner, far_pair)
+    for step in far_steps:
+        inner = grow(inner, "col", step)
+    for step in far_steps[1:]:
+        tail = grow(tail, "col", step)
+    inner_own, inner_far = inner, swap(inner, "col", 1)
+    tail_own, tail_far = tail, swap(tail, "col", 1)
+    cot_own, cot_other = trade(cotangent, inner_row, query)
+
+    doc_blocks = jnp.stack(
+        [
+            lax.dynamic_slice(first[key], (3 * cut_proj + row_here, 0), (1, block_len))[0]
+            for key in first_keys
+        ]
+    ).astype(jnp.int32)
+    bounds = jnp.stack([doc_blocks[:, 0], doc_blocks[:, -1]], axis=1)
+    doc_key = jnp.broadcast_to(doc_blocks[:, :, None], doc_blocks.shape + (LANE,))
+
+    def doc_rim(slot, step):
+        position = (row_here ^ slot) * col_count + col_here + step
+        inside = (position >= 0) & (position < row_count * col_count)
+        position = jnp.clip(position, 0, row_count * col_count - 1)
+        dr = (position // col_count) ^ row_here
+        dc = (position % col_count) ^ col_here
+        return jnp.where(inside, pick(doc_blocks, (dc % 2) * entries + (dc // 2) * 2 + dr), -1)
+
+    doc_ext = jnp.stack(
+        [
+            jnp.concatenate(
+                [doc_rim(slot, -1)[block_len - RIM :], doc_blocks[slot], doc_rim(slot, 1)[:RIM]]
+            )
+            for slot in range(2)
+        ]
+    )
+    doc_rows = jnp.broadcast_to(doc_ext[:, :, None], doc_ext.shape + (LANE,))
 
     ext_len = block_len + 2 * RIM
+    branch_keys = list(branch)
     conv_context, depth_low, value_wide, key_conv, conv_attn, conv_weights, w_branch = kernel_call(
-        branch_kernel,
+        functools.partial(branch_kernel, branch_keys),
         [
             ((tokens_here, ATT), LOW),
             ((tokens_here, model_width), LOW),
@@ -885,6 +941,7 @@
             ((2, row_count, ATT, lanes), LOW),
         ],
         [((2, ext_len, model_width), WIDE)],
+        cost=11,
     )(
         here,
         own,
@@ -892,21 +949,23 @@
         low_rim,
         high_rim,
         doc_rows,
-        branch_own,
-        branch_far,
         depth_gain,
         wide_bias,
         tap_weight,
         tap_bias,
         query,
+        *[branch[key] for key in branch_keys],
     )
 
     doc_query = doc_blocks[:2]
     attended = []
     stats = []
     for index in range(PAIRS):
+        query_pair = query[:, index * LANE : (index + 1) * LANE]
+        if index == 0:
+            query_pair = after(query_pair, conv_context)
         out, stat = kernel_call(
-            attend_kernel,
+            functools.partial(attend_kernel, col_count),
             [((tokens_here, LANE), LOW), ((2, 8, block_len), WIDE)],
             [
                 ((2 * col_count, 2, block_len, block_len), WIDE),
@@ -914,7 +973,8 @@
                 ((2, 1, block_len), WIDE),
                 ((2, LANE, block_len), WIDE),
             ],
-        )(bounds, query[:, index * LANE : (index + 1) * LANE], *gathered[index], doc_query, doc_key)
+            cost=8,
+        )(bounds, query_pair, doc_query, doc_key, *gathered[index])
         attended.append(out)
         stats.append(stat)
 
@@ -956,6 +1016,7 @@
             ((tokens_here, model_width), LOW),
             ((1, row_count, model_width, lanes), LOW),
         ],
+        cost=30,
     )(
         here,
         own,
@@ -972,8 +1033,70 @@
         inner_bias.astype(WIDE).reshape(2 * entries, 1, cut_inner),
     )
 
-    inner_sum = data_sum(scatter(d_inner_own, d_inner_far, "row")).astype(WIDE)
-    tail_sum = data_sum(scatter(d_tail_own, d_tail_far, "col")).astype(WIDE)
+    row_stages = [("row", 1)] + [("col", step) for step in far_steps]
+    col_stages = [("col", far_steps[0]), ("row", 1)] + [("col", step) for step in far_steps[1:]]
+    row_stages.reverse()
+    col_stages.reverse()
+
+    class GridSum:
+        def __init__(self, kept, sent, stages):
+            self.kept = kept
+            self.moved = swap(sent, "col", 1)
+            self.todo = list(stages)
+
+        def finish(self, *marks):
+            moved = after(self.moved, *marks) if marks else self.moved
+            if not self.todo:
+                self.kept = add_low(self.kept, moved)
+                return self.kept
+            self.kept, sent = join(self.kept, moved)
+            axis, step = self.todo.pop(0)
+            self.moved = swap(sent, axis, step)
+            return sent
+
+        def rest(self, *marks):
+            while self.todo:
+                self.finish(*marks)
+            return self.finish(*marks)[0]
+
+    inner_sum = GridSum(d_inner_own, d_inner_far, row_stages)
+    tail_sum = GridSum(d_tail_own, d_tail_far, col_stages)
+    query_grads = []
+    pair_sums = []
+    marks = []
+    for index in range(PAIRS):
+        query_pair = query[:, index * LANE : (index + 1) * LANE]
+        if marks:
+            query_pair = after(query_pair, *marks)
+        grad_query, grad_own, grad_far = kernel_call(
+            functools.partial(attend_back_kernel, col_count),
+            [
+                ((tokens_here, LANE), WIDE),
+                ((pair_entries, tokens_here, 2 * LANE), LOW),
+                ((pair_entries, tokens_here, 2 * LANE), LOW),
+            ],
+            [((2, 8, block_len), WIDE), ((block_len, 2 * LANE), WIDE)],
+            cost=13,
+        )(
+            bounds,
+            query_pair,
+            doc_query,
+            doc_key,
+            attended[index],
+            g_att[index],
+            stats[index],
+            *gathered[index],
+        )
+        query_grads.append(grad_query)
+        pair_sums.append(GridSum(grad_own, grad_far, [("col", step) for step in reversed(far_steps)]))
+        marks = [grad_query]
+        if len(inner_sum.todo) > 0:
+            marks += [inner_sum.finish(grad_query), tail_sum.finish(grad_query)]
+        if index > 0:
+            marks.append(pair_sums[index - 1].finish(grad_query))
+    marks.append(pair_sums[-1].finish())
+    wide_part = jnp.concatenate([inner_sum.rest(grad_query), tail_sum.rest(grad_query)], axis=0)
+    wide_sum = DataSum(wide_part)
 
     (
         g_key_conv,
@@ -981,6 +1104,7 @@
         d_tap_weight,
         d_tap_bias,
         d_depth,
+        branch_bias,
         g_ext_value,
         g_ext_tokens,
     ) = kernel_call(
@@ -991,6 +1115,7 @@
             ((ATT, KERNEL * LANE), WIDE),
             ((1, KERNEL * LANE), WIDE),
             ((16, model_width), WIDE),
+            ((8, ATT), WIDE),
             ((2, ext_len, ATT), WIDE),
             ((2, ext_len, model_width), WIDE),
         ],
@@ -1000,6 +1125,7 @@
             ((block_len, KERNEL * LANE), LOW),
         ],
         smem=0,
+        cost=16,
     )(
         own,
         other,
@@ -1010,116 +1136,93 @@
         depth_gain,
         tap_weight,
         query,
-        g_conv,
+        after(g_conv, wide_part, *marks),
         value_wide,
         key_conv,
         conv_attn,
         conv_weights,
     )
+    pair_grads = [part.rest(g_query) for part in pair_sums]
+    wide_stage = wide_sum.finish(g_query)
 
     def rim_of(start):
         return jnp.concatenate(
             [g_ext_value[:, start : start + RIM], g_ext_tokens[:, start : start + RIM]], axis=2
         ).astype(LOW)
 
-    after = wrapped(rim_of(0), -1)
-    before = wrapped(rim_of(RIM + block_len), 1)
-
-    query_grads = []
-    pair_grads = []
-    for index in range(PAIRS):
-        grad_query, grad_own, grad_far = kernel_call(
-            attend_back_kernel,
-            [
-                ((tokens_here, LANE), WIDE),
-                ((pair_entries, tokens_here, 2 * LANE), LOW),
-                ((pair_entries, tokens_here, 2 * LANE), LOW),
-            ],
-            [((2, 8, block_len), WIDE), ((block_len, 2 * LANE), WIDE)],
-        )(
-            bounds,
-            query[:, index * LANE : (index + 1) * LANE],
-            *gathered[index],
-            doc_query,
-            doc_key,
-            attended[index],
-            g_att[index],
-            stats[index],
-        )
-        query_grads.append(grad_query)
-        stack = add_low(grad_own, swap(grad_far, "col", 1))
-        for step in reversed(far_steps):
-            half = stack.shape[0] // 2
-            stack = add_low(stack[:half], swap(stack[half:], "col", step))
-        pair_grads.append(stack[0])
-
-    d_branch_own, d_branch_far, token_grad, branch_bias = kernel_call(
+    from_after = wrapped(rim_of(0), -1)
+    from_before = wrapped(rim_of(RIM + block_len), 1)
+
+    d_first_own, d_first_far, lows, first_bias = kernel_call(
+        first_weights_kernel,
+        [((entries, 3 * cut_proj, lanes), LOW)] * 2
+        + [((3, tokens_here, ATT), LOW), ((8, ATT), WIDE)],
+        [((3, row_count, ATT, lanes), LOW), ((tokens_here, model_width), LOW)],
+        cost=6,
+    )(here, own, other, *query_grads, after(g_query, wide_stage), *pair_grads)
+    first_sum = GridSum(d_first_own, d_first_far, row_stages)
+    wide_stage = wide_sum.finish(first_bias)
+
+    d_branch_own, d_branch_far, token_grad = kernel_call(
         branch_weights_kernel,
-        [((entries, 2 * cut_proj, lanes), LOW)] * 2
-        + [((tokens_here, model_width), WIDE), ((8, ATT), WIDE)],
+        [((entries, 2 * cut_proj, lanes), LOW)] * 2 + [((tokens_here, model_width), WIDE)],
         [
             ((block_len, ATT + model_width), WIDE),
             ((2, row_count, ATT, lanes), LOW),
             ((tokens_here, model_width), LOW),
             ((tokens_here, ATT), LOW),
         ],
+        cost=6,
     )(
         here,
         own,
         other,
         w_branch,
         depth_low,
-        g_key_conv,
+        after(g_key_conv, lows, wide_stage),
         g_ext_value,
         g_ext_tokens,
-        after,
-        before,
+        from_after,
+        from_before,
         resid_grad,
     )
-    branch_sum = data_sum(scatter(d_branch_own, d_branch_far, "col")).astype(WIDE)
-
-    d_query_own, d_query_far, token_grad, query_bias = kernel_call(
-        query_weights_kernel,
-        [((entries, cut_proj, lanes), LOW)] * 2
-        + [((tokens_here, model_width), WIDE), ((1, ATT), WIDE)],
-        [((1, row_count, ATT, lanes), LOW), ((tokens_here, model_width), LOW)],
-    )(here, own, other, w_first, *query_grads, g_query, token_grad)
-    query_sum = data_sum(scatter(d_query_own, d_query_far, "col")).astype(WIDE)
-
-    d_pair_own, d_pair_far, token_own, token_other, value_bias = kernel_call(
-        pair_weights_kernel,
-        [((entries, 2 * cut_proj, lanes), LOW)] * 2
-        + [((block_len, model_width), WIDE), ((block_len, model_width), LOW), ((1, ATT), WIDE)],
-        [((2, row_count, ATT, lanes), LOW), ((tokens_here, model_width), LOW)],
-    )(here, own, other, w_first, *pair_grads, token_grad)
-    pair_sum = data_sum(scatter(d_pair_own, d_pair_far, "row")).astype(WIDE)
+    branch_sum = GridSum(d_branch_own, d_branch_far, col_stages)
+    wide_stage = wide_sum.finish(token_grad)
+    first_stage = first_sum.finish(token_grad)
+    branch_stage = branch_sum.finish()
+    token_own, token_other = kernel_call(
+        token_kernel,
+        [((block_len, model_width), WIDE), ((block_len, model_width), LOW)],
+        smem=0,
+        cost=6,
+    )(w_first, lows, after(token_grad, wide_stage, first_stage, branch_stage))
+    wide_sum.finish(token_own)
+    wide_sum = wide_sum.rest().astype(WIDE)
+    first_part = first_sum.rest(token_own)
+    branch_part = branch_sum.rest(token_own)
+    proj_sum = DataSum(jnp.concatenate([first_part, branch_part], axis=0)).rest().astype(WIDE)
 
     def tap_layout(grads):
         return grads.reshape(-1, KERNEL, LANE)[:, :, :HEADS].transpose(0, 2, 1).reshape(-1, HEADS * KERNEL)
 
-    early = [vector_grads[:6], inner_bias_grad]
-    late = [
+    items = [
+        vector_grads[:6],
+        inner_bias_grad,
         d_depth[:KERNEL],
         tap_layout(d_tap_weight),
         tap_layout(d_tap_bias),
         branch_bias[:2],
-        query_bias,
-        value_bias,
+        first_bias[:2],
     ]
-
-    def small_sum(items):
-        flat = jnp.concatenate([item.reshape(-1) for item in items])
-        flat = jnp.pad(flat, (0, -flat.shape[0] % 1024)).reshape(-1, LANE)
-        flat = grid_sum(flat).reshape(-1)
-        finals = []
-        start = 0
-        for item in items:
-            finals.append(flat[start : start + item.size].reshape(item.shape))
-            start += item.size
-        return finals
-
-    vector_sum, inner_bias_sum = small_sum(early)
-    depth_sum, tap_weight_sum, tap_bias_sum, branch_bias_sum, query_bias_sum, value_bias_sum = small_sum(late)
+    flat = jnp.concatenate([item.reshape(-1) for item in items])
+    flat = jnp.pad(flat, (0, -flat.shape[0] % 1024)).reshape(-1, LANE)
+    flat = grid_sum(flat).reshape(-1)
+    finals = []
+    start = 0
+    for item in items:
+        finals.append(flat[start : start + item.size].reshape(item.shape))
+        start += item.size
+    vector_sum, inner_bias_sum, depth_sum, tap_weight_sum, tap_bias_sum, branch_bias_sum, first_bias_sum = finals
 
     def give_back(here_rows, there_rows):
         moved = swap(there_rows, "row", 1).astype(here_rows.dtype)
@@ -1127,16 +1230,15 @@
             row_here == 0, jnp.stack([here_rows, moved]), jnp.stack([moved, here_rows])
         )
 
-    proj_sum = jnp.concatenate([query_sum, pair_sum, branch_sum], axis=0)
     return (
         give_back(out_own, out_other),
         give_back(token_own, token_other),
         jnp.transpose(proj_sum.reshape(5, cut_proj, lanes), (0, 2, 1)),
-        tail_sum[cut_inner:].T,
-        inner_sum.T[None],
-        tail_sum[:cut_inner][None],
+        wide_sum[2 * cut_inner :].T,
+        wide_sum[:cut_inner].T[None],
+        wide_sum[cut_inner : 2 * cut_inner][None],
         depth_sum,
-        jnp.concatenate([query_bias_sum, value_bias_sum, branch_bias_sum], axis=0),
+        jnp.concatenate([first_bias_sum, branch_bias_sum], axis=0),
         tap_weight_sum,
         tap_bias_sum[0],
         vector_sum[5],

time: 443 us -> 356 us (0.80)
  waiting for transfers between devices: 133 us -> 81.4 us
  starting transfers between devices: 101 us -> 59.9 us
  other arithmetic: 50.7 us -> 40.5 us
  local copies, waits for them, and re-layouts: 22.9 us -> 31.7 us
  Pallas kernels: 130 us -> 137 us
    ppermute x76 -> x64, waiting for transfers between devices: 130 us -> 72.2 us  [swap(): return lax.ppermute(block, axis, [(i, i ^ step) for i in range(count)])]
    ppermute x76 -> x64, starting transfers between devices: 95.7 us -> 54.3 us  [swap(): return lax.ppermute(block, axis, [(i, i ^ step) for i in range(count)])]
    concatenate x20 -> x8, other arithmetic: 14.9 us -> 1.04 us  [the longest x1 0.6 us: local(): jnp.concatenate([first_bias_sum, branch_bias_sum], axis=0)]
    convert_element_type x18 -> x15, other arithmetic: 7.05 us -> 15.2 us  [add_low(): return (kept.astype(WIDE) + moved.astype(WIDE)).astype(LOW)]
    pallas_call x13, Pallas kernels: 130 us -> 137 us  [run(): pl.pallas_call(body, in_specs=specs, out_specs=[pl.BlockSpec(memory_space...]
    squeeze x9 -> x7, other arithmetic: 2.88 us -> 9.03 us  [rest(): return self.finish(*marks)[0]]
    ppermute x4, waiting for transfers between devices: 3.18 us -> 9.16 us  [shift(): lax.ppermute(block, axis, [(i, (i + step) % count) for i in range(count)])]
  transfers between devices with their start and end apart: 80 -> 68, of which waited for: 37 -> 20; matrix products, arithmetic and copies ran while one was open for 15% -> 19% of each run, Pallas kernels for 22% -> 30%
where the time goes in v3:
time: 356 us; the launch traced here: 352 us
  Pallas kernels  137 us (38%)
  waiting for transfers between devices  81.4 us (23%)
  starting transfers between devices  59.9 us (17%)
  other arithmetic  40.5 us (11%)
  local copies, waits for them, and re-layouts  31.7 us (9%)
    pallas_call x13, Pallas kernels, run(): pl.pallas_call(body, in_specs=specs, out_specs=[pl.BlockSpec(memory_space...  137 us
    ppermute x64, waiting for transfers between devices, swap(): return lax.ppermute(block, axis, [(i, i ^ step) for i in range(count)])  72.2 us
    ppermute x64, starting transfers between devices, swap(): return lax.ppermute(block, axis, [(i, i ^ step) for i in range(count)])  54.3 us
    convert_element_type x15, other arithmetic, add_low(): return (kept.astype(WIDE) + moved.astype(WIDE)).astype(LOW)  15.2 us
    ppermute x4, waiting for transfers between devices, shift(): lax.ppermute(block, axis, [(i, (i + step) % count) for i in range(count)])  9.16 us
    squeeze x7, other arithmetic, rest(): return self.finish(*marks)[0]  9.03 us
  transfers between devices with their start and end apart: 68, of which 20 were waited for; matrix products, arithmetic and copies ran while one was open for 19% of the time, Pallas kernels for 30%

profile of v3, /device:TPU:0, one launch (start us, length us, event | category | flops | bytes accessed | tf_op | source)
XLA Modules:
  0.0 352.2 jit_solution(14730268767223903262)
XLA Ops:
  2.5 3.1 collective-permute-start.2
  23.2 3.9 %collective-permute-done.5.rest_3_ = bf16[304,384]{1,0:T(8,128)(2,1)S(1)} collective-permute-done((bf16[304,384]{1,0:T(8,128)(2,1)}, bf16[304,384]{1,0:T(8,128)(2,1)S(1)}, u32[]{:S(2)}, u32[]{:S(2)}) %collective-permute-start.5) | collective-permute-done | bytes 233504 | tf_op jit(solution)/shard_map/ppermute | solution.py:28
  29.5 8.3 %collective-permute-done.12 = bf16[2,8,768]{2,1,0:T(8,128)(2,1)S(1)} collective-permute-done((bf16[2,8,768]{2,1,0:T(8,128)(2,1)S(1)}, bf16[2,8,768]{2,1,0:T(8,128)(2,1)S(1)}, u32[]{:S(2)}, u32[]{:S(2)}) %collective-permute-start.12) | collective-permute-done | bytes 24608 | tf_op jit(solution)/shard_map/ppermute | solution.py:33
  44.5 5.1 %shard_map.305 = (bf16[512,384]{1,0:T(8,128)(2,1)}, bf16[512,256]{1,0:T(8,128)(2,1)}, bf16[512,256]{1,0:T(8,128)(2,1)}, bf16[512,256]{1,0:T(8,128)(2,1)}, bf16[3,2,384,384]{3,2,1,0:T(8,128)(2,1)}) custom-call(s32[2]{0:T(128)} %pad_add_fusion.4.here, bf16[256,768]{1,0:T(8,128)(2,1)} %get-tuple-element.305.own, bf16[256,768]{1,0:T(8,128)(2,1)} %copy-done.38, ...), custom_call_target="tpu_custom_call" | custom-call | flops 5000000000 | bytes 18000000 | tf_op jit(solution)/shard_map/pallas_call | solution.py:64
  55.0 5.0 %collective-permute-done.4 = bf16[1,384,384]{2,1,0:T(8,128)(2,1)S(1)} collective-permute-done((bf16[1,384,384]{2,1,0:T(8,128)(2,1)S(1)}, bf16[1,384,384]{2,1,0:T(8,128)(2,1)S(1)}, u32[]{:S(2)}, u32[]{:S(2)}) %collective-permute-start.4) | collective-permute-done | bytes 294944 | tf_op jit(solution)/shard_map/ppermute | solution.py:28
  64.8 10.4 %shard_map.306 = (bf16[512,384]{1,0:T(8,128)(2,1)}, bf16[512,768]{1,0:T(8,128)(2,1)}, f32[2,272,384]{2,1,0:T(8,128)}, f32[512,384]{1,0:T(8,128)}, bf16[512,384]{...) custom-call(s32[2]{0:T(128)} %pad_add_fusion.4.here, bf16[256,768]{1,0:T(8,128)(2,1)} %get-tuple-element.305.own, ...), custom_call_target="tpu_custom_call" | custom-call | flops 11000000512 | bytes 39600000 | tf_op jit(solution)/shard_map/pallas_call | solution.py:64
  77.9 6.6 %collective-permute-done.31 = bf16[2,576,384]{2,1,0:T(8,128)(2,1)S(1)} collective-permute-done((bf16[2,576,384]{2,1,0:T(8,128)(2,1)S(1)}, bf16[2,576,384]{2,1,0:T(8,128)(2,1)S(1)}, u32[]{:S(2)}, u32[]{:S(2)}) %collective-permute-start.31) | collective-permute-done | bytes 884768 | tf_op jit(solution)/shard_map/ppermute | solution.py:28
  88.4 7.5 %shard_map.309 = (bf16[512,128]{1,0:T(8,128)(2,1)}, f32[2,8,256]{2,1,0:T(8,128)}) custom-call(s32[8,2]{1,0:T(8,128)} %pad_add_fusion.bounds, bf16[512,128]{1,0:T(8,128)(2,1)} %get-tuple-element.149.query, s32[2,256]{1,0:T(2,128)} %slice.401.doc_query, s32[8,256,128]{2,1,0:T(8,128)} %broadcast_in_dim.34.doc_key, bf16[512,256]{1,0:T(8,128)(2,1)} %get-tuple-element.123.rest_0_, ...), custom_call_target="tpu_custom_call" | custom-call | flops 8000000000 | bytes 28800000 | tf_op jit(solution)/shard_map/pallas_call | solution.py:64
  95.8 5.6 %collective-permute-done.28 = bf16[2,384,384]{2,1,0:T(8,128)(2,1)S(1)} collective-permute-done((bf16[2,384,384]{2,1,0:T(8,128)(2,1)S(1)}, bf16[2,384,384]{2,1,0:T(8,128)(2,1)S(1)}, u32[]{:S(2)}, u32[]{:S(2)}) %collective-permute-start.28) | collective-permute-done | bytes 589856 | tf_op jit(solution)/shard_map/ppermute | solution.py:28
  102.9 7.2 %shard_map.308 = (bf16[512,128]{1,0:T(8,128)(2,1)}, f32[2,8,256]{2,1,0:T(8,128)}) custom-call(s32[8,2]{1,0:T(8,128)} %pad_add_fusion.bounds, bf16[512,128]{1,0:T(8,128)(2,1)} %get-tuple-element.140.query, s32[2,256]{1,0:T(2,128)} %slice.401.doc_query, s32[8,256,128]{2,1,0:T(8,128)} %broadcast_in_dim.34.doc_key, bf16[512,256]{1,0:T(8,128)(2,1)} %get-tuple-element.121.rest_0_, ...), custom_call_target="tpu_custom_call" | custom-call | flops 8000000000 | bytes 28800000 | tf_op jit(solution)/shard_map/pallas_call | solution.py:64
  110.8 7.1 %shard_map.307 = (bf16[512,128]{1,0:T(8,128)(2,1)}, f32[2,8,256]{2,1,0:T(8,128)}) custom-call(s32[8,2]{1,0:T(8,128)} %pad_add_fusion.bounds, bf16[512,128]{1,0:T(8,128)(2,1)} %get-tuple-element.118.query, s32[2,256]{1,0:T(2,128)} %slice.401.doc_query, s32[8,256,128]{2,1,0:T(8,128)} %broadcast_in_dim.34.doc_key, bf16[512,256]{1,0:T(8,128)(2,1)} %get-tuple-element.119.rest_0_, ...), custom_call_target="tpu_custom_call" | custom-call | flops 8000000000 | bytes 28800000 | tf_op jit(solution)/shard_map/pallas_call | solution.py:64
  119.0 32.4 %shard_map.310 = (bf16[256,768]{1,0:T(8,128)(2,1)}, bf16[256,768]{1,0:T(8,128)(2,1)}, f32[512,768]{1,0:T(8,128)}, bf16[512,128]{1,0:T(8,128)(2,1)}, bf16[512,128...) custom-call(s32[2]{0:T(128)} %pad_add_fusion.4.here, ...), custom_call_target="tpu_custom_call" | custom-call | flops 30000001024 | bytes 108000000 | tf_op jit(solution)/shard_map/pallas_call | solution.py:64
  152.1 11.6 %shard_map.311 = (f32[512,128]{1,0:T(8,128)}, bf16[2,512,256]{2,1,0:T(8,128)(2,1)}, bf16[2,512,256]{2,1,0:T(8,128)(2,1)}) custom-call(s32[8,2]{1,0:T(8,128)} %pad_add_fusion.bounds, bf16[512,128]{1,0:T(8,128)(2,1)} %get-tuple-element.118.query, s32[2,256]{1,0:T(2,128)} %slice.401.doc_query, s32[8,256,128]{2,1,0:T(8,128)} %broadcast_in_dim.34.doc_key, ...), custom_call_target="tpu_custom_call" | custom-call | flops 12999999488 | bytes 46800000 | tf_op jit(solution)/shard_map/pallas_call | solution.py:64
  164.5 6.2 %collective-permute-start.33 = (bf16[256,768]{1,0:T(8,128)(2,1)}, bf16[256,768]{1,0:T(8,128)(2,1)}, u32[]{:S(2)}, u32[]{:S(2)}) collective-permute-start(bf16[256,768]{1,0:T(8,128)(2,1)} %get-tuple-element.129), channel_id=1, source_target_pairs={{0,4},{4,0},{1,5},{5,1},{2,6},{6,2},{3,7},{7,3},{8,12},{12,8},{9,1... | collective-permute-start | bytes 1179656 | tf_op jit(solution)/shard_map/ppermute | solution.py:28
  180.3 11.5 %shard_map.312 = (f32[512,128]{1,0:T(8,128)}, bf16[2,512,256]{2,1,0:T(8,128)(2,1)}, bf16[2,512,256]{2,1,0:T(8,128)(2,1)}) custom-call(s32[8,2]{1,0:T(8,128)} %pad_add_fusion.bounds, bf16[512,128]{1,0:T(8,128)(2,1)} %get-tuple-element.140.query, s32[2,256]{1,0:T(2,128)} %slice.401.doc_query, s32[8,256,128]{2,1,0:T(8,128)} %broadcast_in_dim.34.doc_key, ...), custom_call_target="tpu_custom_call" | custom-call | flops 12999999488 | bytes 46800000 | tf_op jit(solution)/shard_map/pallas_call | solution.py:64
  197.8 3.2 collective-permute-done.37
  202.0 3.2 collective-permute-start.40
  205.2 11.8 %shard_map.313 = (f32[512,128]{1,0:T(8,128)}, bf16[2,512,256]{2,1,0:T(8,128)(2,1)}, bf16[2,512,256]{2,1,0:T(8,128)(2,1)}) custom-call(s32[8,2]{1,0:T(8,128)} %pad_add_fusion.bounds, bf16[512,128]{1,0:T(8,128)(2,1)} %get-tuple-element.149.query, s32[2,256]{1,0:T(2,128)} %slice.401.doc_query, s32[8,256,128]{2,1,0:T(8,128)} %broadcast_in_dim.34.doc_key, ...), custom_call_target="tpu_custom_call" | custom-call | flops 12999999488 | bytes 46800000 | tf_op jit(solution)/shard_map/pallas_call | solution.py:64
  224.4 15.9 %shard_map.314 = (bf16[512,384]{1,0:T(8,128)(2,1)}, f32[512,384]{1,0:T(8,128)}, f32[384,1152]{1,0:T(8,128)}, f32[1,1152]{1,0:T(1,128)}, f32[16,768]{1,0:T(8,128)...) custom-call(bf16[256,768]{1,0:T(8,128)(2,1)} %get-tuple-element.305.own, ...), custom_call_target="tpu_custom_call" | custom-call | flops 16000000000 | bytes 57600000 | tf_op jit(solution)/shard_map/pallas_call | solution.py:64
  255.7 5.2 %shard_map.315 = (bf16[4,288,384]{2,1,0:T(8,128)(2,1)}, bf16[4,288,384]{2,1,0:T(8,128)(2,1)}, bf16[3,512,384]{2,1,0:T(8,128)(2,1)}, f32[8,384]{1,0:T(8,128)}) custom-call(s32[2]{0:T(128)} %pad_add_fusion.4.here, bf16[256,768]{1,0:T(8,128)(2,1)} %get-tuple-element.305.own, bf16[256,768]{1,0:T(8,128)(2,1)} %copy-done.38, ...), custom_call_target="tpu_custom_call" | custom-call | flops 6000000000 | bytes 21600000 | tf_op jit(solution)/shard_map/pallas_call | solution.py:64
  262.7 4.7 %collective-permute-start.47 = (bf16[240,384]{1,0:T(8,128)(2,1)S(1)}, bf16[240,384]{1,0:T(8,128)(2,1)S(1)}, u32[]{:S(2)}, u32[]{:S(2)}) collective-permute-start(bf16[240,384]{1,0:T(8,128)(2,1)S(1)} %dynamic-slice_bitcast_fusion.6), channel_id=1, source_target_pairs={{0,16},{8,24},{16,0},{24,8},{1,17},{9,25},{17,1},{25,9},{2,18},{10... | collective-permute-start | bytes 552968 | tf_op jit(solution)/shard_map/ppermute | solution.py:28
  268.5 7.6 %collective-permute-done.47 = bf16[240,384]{1,0:T(8,128)(2,1)S(1)} collective-permute-done((bf16[240,384]{1,0:T(8,128)(2,1)S(1)}, bf16[240,384]{1,0:T(8,128)(2,1)S(1)}, u32[]{:S(2)}, u32[]{:S(2)}) %collective-permute-start.47) | collective-permute-done | bytes 184352 | tf_op jit(solution)/shard_map/ppermute | solution.py:28
  277.4 4.7 %collective-permute-done.65 = f32[296,128]{1,0:T(8,128)S(1)} collective-permute-done((f32[296,128]{1,0:T(8,128)S(1)}, f32[296,128]{1,0:T(8,128)S(1)}, u32[]{:S(2)}, u32[]{:S(2)}) %collective-permute-start.65) | collective-permute-done | bytes 151584 | tf_op jit(solution)/shard_map/ppermute | solution.py:28
  282.2 6.5 %shard_map.316 = (bf16[4,192,384]{2,1,0:T(8,128)(2,1)}, bf16[4,192,384]{2,1,0:T(8,128)(2,1)}, f32[512,768]{1,0:T(8,128)}) custom-call(s32[2]{0:T(128)} %pad_add_fusion.4.here, bf16[256,768]{1,0:T(8,128)(2,1)} %get-tuple-element.305.own, bf16[256,768]{1,0:T(8,128)(2,1)} %copy-done.38, bf16[2,2,384,384]{3,2,1,0:T(8,128)(2,1)} %get-tuple-element.153.w_full, ...), custom_call_target="tpu_custom_call" | custom-call | flops 6000000000 | bytes 21600000 | tf_op jit(solution)/shard_map/pallas_call | solution.py:64
  295.5 5.3 %collective-permute-done.67 = f32[296,128]{1,0:T(8,128)S(1)} collective-permute-done((f32[296,128]{1,0:T(8,128)S(1)}, f32[296,128]{1,0:T(8,128)S(1)}, u32[]{:S(2)}, u32[]{:S(2)}) %collective-permute-start.67) | collective-permute-done | bytes 151584 | tf_op jit(solution)/shard_map/ppermute | solution.py:28
  304.7 4.6 %shard_map.317 = (f32[256,768]{1,0:T(8,128)}, bf16[256,768]{1,0:T(8,128)(2,1)}) custom-call(bf16[3,2,384,384]{3,2,1,0:T(8,128)(2,1)} %get-tuple-element.130.w_full, bf16[3,512,384]{2,1,0:T(8,128)(2,1)} %get-tuple-element.173.lows, f32[512,768]{1,0:T(8,128)} %get-tuple-element.189.token_in), custom_call_target="tpu_custom_call" | custom-call | flops 6000000000 | bytes 21600000 | tf_op jit(solution)/shard_map/pallas_call | solution.py:64
  309.4 3.4 collective-permute-done.56
  314.7 4.4 %collective-permute-done.57 = bf16[1,192,384]{2,1,0:T(8,128)(2,1)S(1)} collective-permute-done((bf16[1,192,384]{2,1,0:T(8,128)(2,1)S(1)}, bf16[1,192,384]{2,1,0:T(8,128)(2,1)S(1)}, u32[]{:S(2)}, u32[]{:S(2)}) %collective-permute-start.57) | collective-permute-done | bytes 147488 | tf_op jit(solution)/shard_map/ppermute | solution.py:28
  321.9 3.4 collective-permute-done.55
  334.4 4.9 %collective-permute-done.59 = bf16[120,384]{1,0:T(8,128)(2,1)S(1)} collective-permute-done((bf16[120,384]{1,0:T(8,128)(2,1)S(1)}, bf16[120,384]{1,0:T(8,128)(2,1)S(1)}, u32[]{:S(2)}, u32[]{:S(2)}) %collective-permute-start.59) | collective-permute-done | bytes 92192 | tf_op jit(solution)/shard_map/ppermute | solution.py:28
  341.3 4.1 %collective-permute-done.60 = bf16[120,384]{1,0:T(8,128)(2,1)S(1)} collective-permute-done((bf16[120,384]{1,0:T(8,128)(2,1)S(1)}, bf16[120,384]{1,0:T(8,128)(2,1)S(1)}, u32[]{:S(2)}, u32[]{:S(2)}) %collective-permute-start.60) | collective-permute-done | bytes 92192 | tf_op jit(solution)/shard_map/ppermute | solution.py:28
  346.8 4.2 %collective-permute-done.61 = bf16[240,384]{1,0:T(8,128)(2,1)S(1)} collective-permute-done((bf16[240,384]{1,0:T(8,128)(2,1)S(1)}, bf16[240,384]{1,0:T(8,128)(2,1)S(1)}, u32[]{:S(2)}, u32[]{:S(2)}) %collective-permute-start.61) | collective-permute-done | bytes 184352 | tf_op jit(solution)/shard_map/ppermute | solution.py:28
  (365 shorter events, 121.6 us)
Async XLA Ops:
  23.2 37.3 %collective-permute-start.15 = (bf16[192,384]{1,0:T(8,128)(2,1)S(1)}, bf16[192,384]{1,0:T(8,128)(2,1)}, u32[]{:S(2)}, u32[]{:S(2)}) collective-permute-start(bf16[192,384]{1,0:T(8,128)(2,1)S(1)} %bitcast.160), channel_id=1, source_target_pairs={{0,1},{1,0},{2,3},{3,2},{4,5},{5,4},{6,7},{7,6},{8,9},{9,8},{10,11... | collective-permute-start | bytes 442376 | tf_op jit(solution)/shard_map/ppermute | solution.py:28
  27.1 33.5 %collective-permute-start.16 = (bf16[192,384]{1,0:T(8,128)(2,1)}, bf16[192,384]{1,0:T(8,128)(2,1)}, u32[]{:S(2)}, u32[]{:S(2)}) collective-permute-start(bf16[192,384]{1,0:T(8,128)(2,1)} %collective-permute-done.13.rest_1_), channel_id=1, source_target_pairs={{0,1},{1,0},{2,3},{3,2},{4,5},{5,4},{6,7},{7,6},{8,9},{9,8},{10,11... | collective-permute-start | bytes 442376 | tf_op jit(solution)/shard_map/ppermute | solution.py:28
  27.1 27.2 %collective-permute-start.30 = (bf16[1,576,384]{2,1,0:T(8,128)(2,1)S(1)}, bf16[1,576,384]{2,1,0:T(8,128)(2,1)S(1)}, u32[]{:S(2)}, u32[]{:S(2)}) collective-permute-start(bf16[1,576,384]{2,1,0:T(8,128)(2,1)S(1)} %bitcast.137), channel_id=1, source_target_pairs={{0,2},{1,3},{2,0},{3,1},{4,6},{5,7},{6,4},{7,5},{8,10},{9,11},{10,... | collective-permute-start | bytes 1327112 | tf_op jit(solution)/shard_map/ppermute | solution.py:28
  27.5 16.2 %collective-permute-start.9 = (bf16[304,384]{1,0:T(8,128)(2,1)S(1)}, bf16[304,384]{1,0:T(8,128)(2,1)S(1)}, u32[]{:S(2)}, u32[]{:S(2)}) collective-permute-start(bf16[304,384]{1,0:T(8,128)(2,1)S(1)} %collective-permute-done.5.rest_3_), channel_id=1, source_target_pairs={{0,1},{1,0},{2,3},{3,2},{4,5},{5,4},{6,7},{7,6},{8,9},{9,8},{10,11... | collective-permute-start | bytes 700424 | tf_op jit(solution)/shard_map/ppermute | solution.py:28
  60.5 25.1 %collective-permute-start.26 = (bf16[512,256]{1,0:T(8,128)(2,1)S(1)}, bf16[512,256]{1,0:T(8,128)(2,1)S(1)}, u32[]{:S(2)}, u32[]{:S(2)}) collective-permute-start(bf16[512,256]{1,0:T(8,128)(2,1)S(1)} %copy-done.47), channel_id=1, source_target_pairs={{0,1},{1,0},{2,3},{3,2},{4,5},{5,4},{6,7},{7,6},{8,9},{9,8},{10,11... | collective-permute-start | bytes 786440 | tf_op jit(solution)/shard_map/ppermute | solution.py:28
  60.6 15.7 %collective-permute-start.19 = (bf16[512,256]{1,0:T(8,128)(2,1)}, bf16[512,256]{1,0:T(8,128)(2,1)}, u32[]{:S(2)}, u32[]{:S(2)}) collective-permute-start(bf16[512,256]{1,0:T(8,128)(2,1)} %get-tuple-element.119.rest_0_), channel_id=1, source_target_pairs={{0,2},{1,3},{2,0},{3,1},{4,6},{5,7},{6,4},{7,5},{8,10},{9,11},{10,... | collective-permute-start | bytes 786440 | tf_op jit(solution)/shard_map/ppermute | solution.py:28
  62.2 15.7 %collective-permute-start.22 = (bf16[512,256]{1,0:T(8,128)(2,1)S(1)}, bf16[512,256]{1,0:T(8,128)(2,1)}, u32[]{:S(2)}, u32[]{:S(2)}) collective-permute-start(bf16[512,256]{1,0:T(8,128)(2,1)S(1)} %copy-done.48), channel_id=1, source_target_pairs={{0,2},{1,3},{2,0},{3,1},{4,6},{5,7},{6,4},{7,5},{8,10},{9,11},{10,... | collective-permute-start | bytes 786440 | tf_op jit(solution)/shard_map/ppermute | solution.py:28
  62.9 21.7 %collective-permute-start.31 = (bf16[2,576,384]{2,1,0:T(8,128)(2,1)S(1)}, bf16[2,576,384]{2,1,0:T(8,128)(2,1)S(1)}, u32[]{:S(2)}, u32[]{:S(2)}) collective-permute-start(bf16[2,576,384]{2,1,0:T(8,128)(2,1)S(1)} %pad_maximum_fusion), channel_id=1, source_target_pairs={{0,4},{4,0},{1,5},{5,1},{2,6},{6,2},{3,7},{7,3},{8,12},{12,8},{9,1... | collective-permute-start | bytes 2654216 | tf_op jit(solution)/shard_map/ppermute | solution.py:28
  76.3 25.2 %collective-permute-start.23 = (bf16[512,256]{1,0:T(8,128)(2,1)S(1)}, bf16[512,256]{1,0:T(8,128)(2,1)}, u32[]{:S(2)}, u32[]{:S(2)}) collective-permute-start(bf16[512,256]{1,0:T(8,128)(2,1)S(1)} %copy-done.48), channel_id=1, source_target_pairs={{0,1},{1,0},{2,3},{3,2},{4,5},{5,4},{6,7},{7,6},{8,9},{9,8},{10,11... | collective-permute-start | bytes 786440 | tf_op jit(solution)/shard_map/ppermute | solution.py:28
  77.9 32.1 %collective-permute-start.20 = (bf16[512,256]{1,0:T(8,128)(2,1)}, bf16[512,256]{1,0:T(8,128)(2,1)}, u32[]{:S(2)}, u32[]{:S(2)}) collective-permute-start(bf16[512,256]{1,0:T(8,128)(2,1)} %get-tuple-element.119.rest_0_), channel_id=1, source_target_pairs={{0,1},{1,0},{2,3},{3,2},{4,5},{5,4},{6,7},{7,6},{8,9},{9,8},{10,11... | collective-permute-start | bytes 786440 | tf_op jit(solution)/shard_map/ppermute | solution.py:28
  84.6 18.1 %collective-permute-start.24 = (bf16[512,256]{1,0:T(8,128)(2,1)}, bf16[512,256]{1,0:T(8,128)(2,1)}, u32[]{:S(2)}, u32[]{:S(2)}) collective-permute-start(bf16[512,256]{1,0:T(8,128)(2,1)} %collective-permute-done.22.rest_1_), channel_id=1, source_target_pairs={{0,1},{1,0},{2,3},{3,2},{4,5},{5,4},{6,7},{7,6},{8,9},{9,8},{10,11... | collective-permute-start | bytes 786440 | tf_op jit(solution)/shard_map/ppermute | solution.py:28
  85.6 15.7 %collective-permute-start.28 = (bf16[2,384,384]{2,1,0:T(8,128)(2,1)S(1)}, bf16[2,384,384]{2,1,0:T(8,128)(2,1)S(1)}, u32[]{:S(2)}, u32[]{:S(2)}) collective-permute-start(bf16[2,384,384]{2,1,0:T(8,128)(2,1)S(1)} %pad_maximum_fusion.2), channel_id=1, source_target_pairs={{0,2},{1,3},{2,0},{3,1},{4,6},{5,7},{6,4},{7,5},{8,10},{9,11},{10,... | collective-permute-start | bytes 1769480 | tf_op jit(solution)/shard_map/ppermute | solution.py:28
  86.8 31.1 %collective-permute-start.32 = (bf16[4,576,384]{2,1,0:T(8,128)(2,1)}, bf16[4,576,384]{2,1,0:T(8,128)(2,1)}, u32[]{:S(2)}, u32[]{:S(2)}) collective-permute-start(bf16[4,576,384]{2,1,0:T(8,128)(2,1)} %constant_dynamic-update-slice_fusion.2.tail_own), channel_id=1, source_target_pairs={{0,1},{1,0},{2,3},{3,2},{4,5},{5,4},{6,7},{7,6},{8,9},{9,8},{10,11... | collective-permute-start | bytes 5308424 | tf_op jit(solution)/shard_map/ppermute | solution.py:28
  101.5 16.4 %collective-permute-start.10 = (bf16[256,768]{1,0:T(8,128)(2,1)S(1)}, bf16[256,768]{1,0:T(8,128)(2,1)S(1)}, u32[]{:S(2)}, u32[]{:S(2)}) collective-permute-start(bf16[256,768]{1,0:T(8,128)(2,1)S(1)} %get-tuple-element.115), channel_id=1, source_target_pairs={{0,4},{4,0},{1,5},{5,1},{2,6},{6,2},{3,7},{7,3},{8,12},{12,8},{9,1... | collective-permute-start | bytes 1179656 | tf_op jit(solution)/shard_map/ppermute | solution.py:28
  102.6 15.3 %collective-permute-start.29 = (bf16[4,384,384]{2,1,0:T(8,128)(2,1)S(1)}, bf16[4,384,384]{2,1,0:T(8,128)(2,1)S(1)}, u32[]{:S(2)}, u32[]{:S(2)}) collective-permute-start(bf16[4,384,384]{2,1,0:T(8,128)(2,1)S(1)} %constant_dynamic-update-slice_fusion.inner_own), channel_id=1, source_target_pairs={{0,1},{1,0},{2,3},{3,2},{4,5},{5,4},{6,7},{7,6},{8,9},{9,8},{10,11... | collective-permute-start | bytes 3538952 | tf_op jit(solution)/shard_map/ppermute | solution.py:28
  151.5 25.4 %collective-permute-start.35 = (bf16[4,576,384]{2,1,0:T(8,128)(2,1)}, bf16[4,576,384]{2,1,0:T(8,128)(2,1)S(1)}, u32[]{:S(2)}, u32[]{:S(2)}) collective-permute-start(bf16[4,576,384]{2,1,0:T(8,128)(2,1)} %get-tuple-element.138), channel_id=1, source_target_pairs={{0,1},{1,0},{2,3},{3,2},{4,5},{5,4},{6,7},{7,6},{8,9},{9,8},{10,11... | collective-permute-start | bytes 5308424 | tf_op jit(solution)/shard_map/ppermute | solution.py:28
  151.8 19.0 %collective-permute-start.34 = (bf16[4,384,384]{2,1,0:T(8,128)(2,1)}, bf16[4,384,384]{2,1,0:T(8,128)(2,1)S(1)}, u32[]{:S(2)}, u32[]{:S(2)}) collective-permute-start(bf16[4,384,384]{2,1,0:T(8,128)(2,1)} %get-tuple-element.135), channel_id=1, source_target_pairs={{0,1},{1,0},{2,3},{3,2},{4,5},{5,4},{6,7},{7,6},{8,9},{9,8},{10,11... | collective-permute-start | bytes 3538952 | tf_op jit(solution)/shard_map/ppermute | solution.py:28
  163.7 28.1 %collective-permute-start.38 = (bf16[2,512,256]{2,1,0:T(8,128)(2,1)}, bf16[2,512,256]{2,1,0:T(8,128)(2,1)}, u32[]{:S(2)}, u32[]{:S(2)}) collective-permute-start(bf16[2,512,256]{2,1,0:T(8,128)(2,1)} %get-tuple-element.147), channel_id=1, source_target_pairs={{0,1},{1,0},{2,3},{3,2},{4,5},{5,4},{6,7},{7,6},{8,9},{9,8},{10,11... | collective-permute-start | bytes 1572872 | tf_op jit(solution)/shard_map/ppermute | solution.py:28
  164.5 127.0 %collective-permute-start.33 = (bf16[256,768]{1,0:T(8,128)(2,1)}, bf16[256,768]{1,0:T(8,128)(2,1)}, u32[]{:S(2)}, u32[]{:S(2)}) collective-permute-start(bf16[256,768]{1,0:T(8,128)(2,1)} %get-tuple-element.129), channel_id=1, source_target_pairs={{0,4},{4,0},{1,5},{5,1},{2,6},{6,2},{3,7},{7,3},{8,12},{12,8},{9,1... | collective-permute-start | bytes 1179656 | tf_op jit(solution)/shard_map/ppermute | solution.py:28
  174.6 17.2 %collective-permute-start.36 = (bf16[2,384,384]{2,1,0:T(8,128)(2,1)}, bf16[2,384,384]{2,1,0:T(8,128)(2,1)}, u32[]{:S(2)}, u32[]{:S(2)}) collective-permute-start(bf16[2,384,384]{2,1,0:T(8,128)(2,1)} %get-tuple-element.291), channel_id=1, source_target_pairs={{0,2},{1,3},{2,0},{3,1},{4,6},{5,7},{6,4},{7,5},{8,10},{9,11},{10,... | collective-permute-start | bytes 1769480 | tf_op jit(solution)/shard_map/ppermute | solution.py:28
  178.3 22.7 %collective-permute-start.37 = (bf16[2,576,384]{2,1,0:T(8,128)(2,1)}, bf16[2,576,384]{2,1,0:T(8,128)(2,1)S(1)}, u32[]{:S(2)}, u32[]{:S(2)}) collective-permute-start(bf16[2,576,384]{2,1,0:T(8,128)(2,1)} %get-tuple-element.289), channel_id=1, source_target_pairs={{0,4},{4,0},{1,5},{5,1},{2,6},{6,2},{3,7},{7,3},{8,12},{12,8},{9,1... | collective-permute-start | bytes 2654216 | tf_op jit(solution)/shard_map/ppermute | solution.py:28
  191.8 25.2 %collective-permute-start.41 = (bf16[2,512,256]{2,1,0:T(8,128)(2,1)}, bf16[2,512,256]{2,1,0:T(8,128)(2,1)}, u32[]{:S(2)}, u32[]{:S(2)}) collective-permute-start(bf16[2,512,256]{2,1,0:T(8,128)(2,1)} %get-tuple-element.158), channel_id=1, source_target_pairs={{0,1},{1,0},{2,3},{3,2},{4,5},{5,4},{6,7},{7,6},{8,9},{9,8},{10,11... | collective-permute-start | bytes 1572872 | tf_op jit(solution)/shard_map/ppermute | solution.py:28
  192.9 24.2 %collective-permute-start.39 = (bf16[1,384,384]{2,1,0:T(8,128)(2,1)S(1)}, bf16[1,384,384]{2,1,0:T(8,128)(2,1)S(1)}, u32[]{:S(2)}, u32[]{:S(2)}) collective-permute-start(bf16[1,384,384]{2,1,0:T(8,128)(2,1)S(1)} %add_convert_fusion.13), channel_id=1, source_target_pairs={{0,4},{4,0},{1,5},{5,1},{2,6},{6,2},{3,7},{7,3},{8,12},{12,8},{9,1... | collective-permute-start | bytes 884744 | tf_op jit(solution)/shard_map/ppermute | solution.py:28
  197.4 45.0 %collective-permute-start.44 = (bf16[1,512,256]{2,1,0:T(8,128)(2,1)}, bf16[1,512,256]{2,1,0:T(8,128)(2,1)}, u32[]{:S(2)}, u32[]{:S(2)}) collective-permute-start(bf16[1,512,256]{2,1,0:T(8,128)(2,1)} %add_convert_fusion.22), channel_id=1, source_target_pairs={{0,2},{1,3},{2,0},{3,1},{4,6},{5,7},{6,4},{7,5},{8,10},{9,11},{10,... | collective-permute-start | bytes 786440 | tf_op jit(solution)/shard_map/ppermute | solution.py:28
  202.0 19.9 %collective-permute-start.40 = (bf16[1,576,384]{2,1,0:T(8,128)(2,1)}, bf16[1,576,384]{2,1,0:T(8,128)(2,1)}, u32[]{:S(2)}, u32[]{:S(2)}) collective-permute-start(bf16[1,576,384]{2,1,0:T(8,128)(2,1)} %add_convert_fusion.8), channel_id=1, source_target_pairs={{0,2},{1,3},{2,0},{3,1},{4,6},{5,7},{6,4},{7,5},{8,10},{9,11},{10,... | collective-permute-start | bytes 1327112 | tf_op jit(solution)/shard_map/ppermute | solution.py:28
  220.1 20.3 %collective-permute-start.45 = (bf16[1,512,256]{2,1,0:T(8,128)(2,1)}, bf16[1,512,256]{2,1,0:T(8,128)(2,1)}, u32[]{:S(2)}, u32[]{:S(2)}) collective-permute-start(bf16[1,512,256]{2,1,0:T(8,128)(2,1)} %add_convert_fusion.21), channel_id=1, source_target_pairs={{0,2},{1,3},{2,0},{3,1},{4,6},{5,7},{6,4},{7,5},{8,10},{9,11},{10,... | collective-permute-start | bytes 786440 | tf_op jit(solution)/shard_map/ppermute | solution.py:28
  223.2 31.4 %collective-permute-start.43 = (bf16[480,384]{1,0:T(8,128)(2,1)S(1)}, bf16[480,384]{1,0:T(8,128)(2,1)}, u32[]{:S(2)}, u32[]{:S(2)}) collective-permute-start(bf16[480,384]{1,0:T(8,128)(2,1)S(1)} %dynamic-slice_bitcast_fusion.4), channel_id=1, source_target_pairs={{0,8},{8,0},{16,24},{24,16},{1,9},{9,1},{17,25},{25,17},{2,10},{10... | collective-permute-start | bytes 1105928 | tf_op jit(solution)/shard_map/ppermute | solution.py:28
  224.2 28.6 %collective-permute-start.46 = (bf16[1,512,256]{2,1,0:T(8,128)(2,1)}, bf16[1,512,256]{2,1,0:T(8,128)(2,1)}, u32[]{:S(2)}, u32[]{:S(2)}) collective-permute-start(bf16[1,512,256]{2,1,0:T(8,128)(2,1)} %add_convert_fusion.20), channel_id=1, source_target_pairs={{0,2},{1,3},{2,0},{3,1},{4,6},{5,7},{6,4},{7,5},{8,10},{9,11},{10,... | collective-permute-start | bytes 786440 | tf_op jit(solution)/shard_map/ppermute | solution.py:28
  251.1 16.8 %collective-permute-start.48 = (bf16[2,8,1152]{2,1,0:T(8,128)(2,1)S(1)}, bf16[2,8,1152]{2,1,0:T(8,128)(2,1)S(1)}, u32[]{:S(2)}, u32[]{:S(2)}) collective-permute-start(bf16[2,8,1152]{2,1,0:T(8,128)(2,1)S(1)} %pad_maximum_fusion.5), channel_id=1, source_target_pairs={{0,3},{1,0},{2,1},{3,2},{4,7},{5,4},{6,5},{7,6},{8,11},{9,8},{10,9... | collective-permute-start | bytes 110600 | tf_op jit(solution)/shard_map/ppermute | solution.py:33
  268.5 35.1 %collective-permute-start.51 = (bf16[4,288,384]{2,1,0:T(8,128)(2,1)}, bf16[4,288,384]{2,1,0:T(8,128)(2,1)S(1)}, u32[]{:S(2)}, u32[]{:S(2)}) collective-permute-start(bf16[4,288,384]{2,1,0:T(8,128)(2,1)} %get-tuple-element.185), channel_id=1, source_target_pairs={{0,1},{1,0},{2,3},{3,2},{4,5},{5,4},{6,7},{7,6},{8,9},{9,8},{10,11... | collective-permute-start | bytes 2654216 | tf_op jit(solution)/shard_map/ppermute | solution.py:28
  277.3 16.4 %collective-permute-start.50 = (bf16[240,384]{1,0:T(8,128)(2,1)S(1)}, bf16[240,384]{1,0:T(8,128)(2,1)S(1)}, u32[]{:S(2)}, u32[]{:S(2)}) collective-permute-start(bf16[240,384]{1,0:T(8,128)(2,1)S(1)} %fusion.5), channel_id=1, source_target_pairs={{0,16},{8,24},{16,0},{24,8},{1,17},{9,25},{17,1},{25,9},{2,18},{10... | collective-permute-start | bytes 552968 | tf_op jit(solution)/shard_map/ppermute | solution.py:28
  293.8 34.5 %collective-permute-start.62 = (bf16[480,384]{1,0:T(8,128)(2,1)S(1)}, bf16[480,384]{1,0:T(8,128)(2,1)}, u32[]{:S(2)}, u32[]{:S(2)}) collective-permute-start(bf16[480,384]{1,0:T(8,128)(2,1)S(1)} %maximum_select_fusion.3), channel_id=1, source_target_pairs={{0,8},{8,0},{16,24},{24,16},{1,9},{9,1},{17,25},{25,17},{2,10},{10... | collective-permute-start | bytes 1105928 | tf_op jit(solution)/shard_map/ppermute | solution.py:28
  (89 other events, 714.4 us)

commit v4 on v3

--- a/solution.py
+++ b/solution.py
@@ -49,20 +49,25 @@
 NT = (((1,), (1,)), ((), ()))
 NN = (((1,), (0,)), ((), ()))
 TN = (((0,), (0,)), ((), ()))
+NT_ROWS = (((0,), (1,)), ((), ()))
 
 
 def mm(left, right, how):
     return lax.dot_general(left, right, how, preferred_element_type=WIDE)
 
 
-def kernel_call(body, outs, scratch=(), smem=1, cost=5):
+def kernel_call(body, outs, scratch=(), smem=1, cost=5, parts=0, part=0):
     def run(*args):
         specs = [
             pl.BlockSpec(memory_space=pltpu.SMEM if place < smem else pltpu.VMEM)
-            for place in range(len(args))
+            for place in range(len(args) - parts)
+        ]
+        specs += [
+            pl.BlockSpec((arg.shape[0], 2 * LANE), lambda step: (0, part)) for arg in args[len(args) - parts :]
         ]
         return pl.pallas_call(
             body,
+            grid=(1,),
             in_specs=specs,
             out_specs=[pl.BlockSpec(memory_space=pltpu.VMEM)] * len(outs),
             out_shape=[jax.ShapeDtypeStruct(shape, kind) for shape, kind in outs],
@@ -136,17 +141,29 @@
             self.start()
         return self.part
 
-    def rest(self):
+    def rest(self, *marks):
         while self.todo:
-            self.finish()
+            self.finish(*marks)
         return self.part
 
 
-def grid_sum(flat):
-    for axis in ("col", "row", "dp"):
-        for step in steps_of(axis):
-            flat = flat + swap(flat, axis, step)
-    return flat
+class FlatSum:
+    def __init__(self, flat):
+        self.todo = [("col", 1), ("row", 1)] + [("col", step) for step in steps_of("col") if step > 1]
+        self.todo += [("dp", step) for step in steps_of("dp")]
+        self.low = flat
+        self.start()
+
+    def start(self):
+        self.moved = swap(self.low, *self.todo[0])
+
+    def finish(self, *marks):
+        moved = after(self.moved, *marks) if marks else self.moved
+        self.todo.pop(0)
+        self.low = add_low(self.low, moved)
+        if self.todo:
+            self.start()
+        return self.low
 
 
 def assemble_pieces(here, pieces, full, parts, size):
@@ -201,7 +218,7 @@
 
 def project_kernel(keys, here, own, other, bias, *rest):
     weights, rest = rest[: len(keys)], rest[len(keys) :]
-    query, pairs, w_full = rest[0], rest[1 : 1 + PAIRS], rest[1 + PAIRS]
+    query, pairs, w_full = rest
     size = (weights[0].shape[0] - DOC_ROWS) // 3
     block_len = own.shape[0]
     assemble_pieces(here, list(zip(keys, weights)), w_full, 3, size)
@@ -215,9 +232,9 @@
         query[rows, :] = (product(0) + bias[0:1, :]).astype(LOW)
         key_low = product(1).astype(LOW)
         value_low = (product(2) + bias[1:2, :]).astype(LOW)
-        for index, pair in enumerate(pairs):
+        for index in range(PAIRS):
             lanes = slice(index * LANE, (index + 1) * LANE)
-            pair[rows, :] = two(key_low[:, lanes], value_low[:, lanes])
+            pairs[rows, 2 * index * LANE : 2 * (index + 1) * LANE] = two(key_low[:, lanes], value_low[:, lanes])
 
 
 def tile_lanes(mask, times):
@@ -247,12 +264,40 @@
     return jnp.where(lane // HEAD == head, 1.0, 0.0).astype(LOW)
 
 
+def take_rims(keys, here, pieces, start, cols, low_rim, high_rim):
+    for rims, step, edge, first in ((low_rim, -1, 0, 0), (high_rim, 1, cols - 1, 2 * RIM)):
+        source = here[1] ^ ((here[1] + step + cols) % cols)
+        turn = jnp.where(here[1] == edge, 1, 0)
+        for (dr, dc), piece in zip(keys, pieces):
+            if dr == 0 and dc > 0:
+
+                @pl.when(source == dc)
+                def _():
+                    rows = piece[start : start + 8 * RIM, :].astype(WIDE)
+                    for slot in range(2):
+                        place = first + slot * RIM
+                        left = rows[place : place + RIM, :]
+                        right = rows[4 * RIM + place : 4 * RIM + place + RIM, :]
+                        rims[slot ^ turn] = two(left, right).astype(LOW)
+
+
 def branch_kernel(
-    keys, here, own, other, low_rim, high_rim, docs, depth_gain, bias, tap_weight, tap_bias, query, *rest
+    keys, size, cols, here, own, other, docs, depth_gain, bias, tap_weight, tap_bias, query, *rest
 ):
     weights, rest = rest[: len(keys)], rest[len(keys) :]
-    context, depth_low, value_wide, key_conv, conv_attn, conv_weights, w_full, wide = rest
-    size = weights[0].shape[0] // 2
+    (
+        context,
+        depth_low,
+        value_wide,
+        key_conv,
+        conv_attn,
+        conv_weights,
+        w_full,
+        low_rim,
+        high_rim,
+        wide,
+    ) = rest
+    take_rims(keys, here, weights, 2 * size, cols, low_rim, high_rim)
     block_len = own.shape[0]
     start = RIM - KERNEL // 2
     assemble_pieces(here, list(zip(keys, weights)), w_full, 2, size)
@@ -315,15 +360,16 @@
     return (bounds[block, 0] <= bounds[slot, 1]) & (bounds[block, 1] >= bounds[slot, 0])
 
 
-def attend_kernel(count, bounds, query, doc_query, doc_key, *rest):
+def attend_kernel(count, index, bounds, query, doc_query, doc_key, *rest):
     stacks, rest = rest[:count], rest[count:]
     out, stats, scores, top, total, mixed = rest
+    pair_lanes = slice(index * LANE, (index + 1) * LANE)
     tokens_here = query.shape[0]
     block_len = tokens_here // 2
     score_scale = HEAD ** (-0.5)
     for slot in range(2):
         rows = slice(slot * block_len, (slot + 1) * block_len)
-        scaled = query[rows, :] * jnp.asarray(score_scale, LOW)
+        scaled = query[rows, pair_lanes] * jnp.asarray(score_scale, LOW)
         queries = [head_queries(scaled, head) for head in range(2)]
         doc_here = doc_query[slot : slot + 1, :]
         top[...] = jnp.full(top.shape, MASKED, WIDE)
@@ -372,9 +418,10 @@
         out[rows, :] = jnp.concatenate(parts, axis=0).T.astype(LOW)
 
 
-def attend_back_kernel(count, bounds, query, doc_query, doc_key, attended, grad, stats, *rest):
+def attend_back_kernel(count, index, bounds, query, doc_query, doc_key, attended, grad, stats, *rest):
     stacks, rest = rest[:count], rest[count:]
-    grad_query, grad_own, grad_far, delta, grad_kv = rest
+    grad_query, grad_own, grad_far, bias_grad, delta, grad_kv = rest
+    pair_lanes = slice(index * LANE, (index + 1) * LANE)
     tokens_here = query.shape[0]
     block_len = tokens_here // 2
     score_scale = HEAD ** (-0.5)
@@ -387,6 +434,7 @@
         high, low = split_low(both)
         delta[slot] = mm(chosen, high, NT) + mm(chosen, low, NT)
     grad_query[...] = jnp.zeros(grad_query.shape, WIDE)
+    bias_grad[...] = jnp.zeros(bias_grad.shape, WIDE)
 
     for place, stack in enumerate(stacks):
         out = (grad_own, grad_far)[2 * place // count]
@@ -403,7 +451,7 @@
                     rows = slice(slot * block_len, (slot + 1) * block_len)
                     key_rows = stack[keys, :LANE]
                     value_rows = stack[keys, LANE:]
-                    scaled = query[rows, :] * jnp.asarray(score_scale, LOW)
+                    scaled = query[rows, pair_lanes] * jnp.asarray(score_scale, LOW)
                     allowed = tile_lanes(doc_key[block], block_len // LANE) == doc_query[slot : slot + 1, :]
                     for head in range(2):
                         query_here = head_queries(scaled, head)
@@ -419,11 +467,13 @@
                         grad_kv[:, :LANE] += mm(g_score, query_here, NN)
                         grad_kv[:, LANE:] += mm(probs.astype(LOW), grad_here, NN)
 
+            bias_grad[1:2, :] += column_sum(grad_kv[:, LANE:])
             out[entry, keys, :] = grad_kv[...].astype(LOW)
             return carry
 
         lax.fori_loop(0, 2, one, 0)
     grad_query[...] = grad_query[...] * score_scale
+    bias_grad[0:1, :] = column_sum(grad_query[...])
 
 
 def norm_stats(values):
@@ -450,7 +500,7 @@
     here,
     own,
     other,
-    cot_own,
+    cot_pair,
     cot_other,
     att_0,
     att_1,
@@ -499,7 +549,7 @@
     bias_outer, gain_2, shift_2 = vectors[3:4, :], vectors[4:5, :], vectors[5:6, :]
     context[0] = jnp.concatenate([att_0[...], att_1[...], att_2[...]], axis=1)
     context[1] = conv_context[...]
-    sources = ((own, cot_own, out_own), (other, cot_other, out_other))
+    sources = ((own, cot_pair.at[here[0]], out_own), (other, cot_other, out_other))
     for slot, (source, _, _) in enumerate(sources):
         rows = slice(slot * block_len, (slot + 1) * block_len)
         attn = (
@@ -621,15 +671,19 @@
     bias_grad,
     g_ext_value,
     g_ext_tokens,
+    first_rim,
+    last_rim,
     wide,
     weight_grad,
     low_grad,
+    tap_sum,
+    tap_bias_sum,
 ):
     block_len = own.shape[0]
     start = RIM - KERNEL // 2
     spread = spread_heads()
-    d_tap_weight[...] = jnp.zeros(d_tap_weight.shape, WIDE)
-    d_tap_bias[...] = jnp.zeros(d_tap_bias.shape, WIDE)
+    tap_sum[...] = jnp.zeros(tap_sum.shape, WIDE)
+    tap_bias_sum[...] = jnp.zeros(tap_bias_sum.shape, WIDE)
     d_depth[...] = jnp.zeros(d_depth.shape, WIDE)
     bias_grad[...] = jnp.zeros(bias_grad.shape, WIDE)
     g_ext_value[...] = jnp.zeros(g_ext_value.shape, WIDE)
@@ -652,14 +706,15 @@
             weight = conv_weights[rows, lanes]
             low_grad[:, lanes] = (weight * (weight_grad[:, lanes] - mean)).astype(LOW)
             g_ext_value[slot, place, :] += mm(two(*split_low(weight)), spread, NN) * grad
-        d_tap_weight[...] += mm(conv_attn[rows, :], low_grad[...], TN)
-        d_tap_bias[...] += column_sum(low_grad[...].astype(WIDE))
+        tap_sum[...] += mm(conv_attn[rows, :], low_grad[...], TN)
+        tap_bias_sum[0:1, :] += column_sum(low_grad[...].astype(WIDE))
         g_attn = mm(low_grad[...], tap_weight[...], NT)
         g_key = (g_attn * query[rows, :].astype(WIDE)).astype(LOW)
         g_key_conv[rows, :] = g_key
         bias_grad[0:1, :] += column_sum(g_ext_value[slot])
         bias_grad[1:2, :] += column_sum(g_key.astype(WIDE))
         g_query[rows, :] = g_attn * key_conv[rows, :]
+        bias_grad[2:3, :] += column_sum(g_query[rows, :])
         for half in range(2):
             g_depth = mm(g_key, w_full[1, half], NN)
             for block in range(g_depth.shape[1] // LANE):
@@ -671,6 +726,41 @@
                     masked = jnp.where(same_doc(docs, slot, offset, block_len), piece, 0.0)
                     d_depth[offset : offset + 1, lanes] += column_sum(masked * wide[slot, place, lanes])
                     g_ext_tokens[slot, place, lanes] += masked * depth_gain[offset : offset + 1, lanes]
+        for rim, place in ((first_rim, slice(0, RIM)), (last_rim, slice(RIM + block_len, 2 * RIM + block_len))):
+            rim[slot] = two(g_ext_value[slot, place, :], g_ext_tokens[slot, place, :]).astype(LOW)
+    source = lax.broadcasted_iota(jnp.int32, (KERNEL * LANE, LANE), 0)
+    target = lax.broadcasted_iota(jnp.int32, (KERNEL * LANE, LANE), 1)
+    chosen = (source % LANE < HEADS) & (source % LANE * KERNEL + source // LANE == target)
+    chosen = jnp.where(chosen, 1.0, 0.0).astype(LOW)
+    high, low = split_low(tap_sum[...])
+    d_tap_weight[...] = mm(chosen, high, NT_ROWS) + mm(chosen, low, NT_ROWS)
+    high, low = split_low(tap_bias_sum[...])
+    d_tap_bias[...] = mm(high, chosen, NN) + mm(low, chosen, NN)
+
+
+def pack(out, grads):
+    vector_grads, inner_bias_grad, d_depth, d_tap_weight, d_tap_bias, branch_bias, biases = grads
+    width = out.shape[1]
+    out[...] = jnp.zeros(out.shape, WIDE)
+    row = 0
+    for source, count in ((vector_grads, 6), (d_depth, KERNEL)):
+        for index in range(count):
+            for half in range(2):
+                out[row : row + 1, :] = source[index : index + 1, half * width : (half + 1) * width]
+                row += 1
+    taps = HEADS * KERNEL
+    out[row : row + taps, :] = d_tap_weight[0:taps, :]
+    row += taps
+    out[row : row + 1, :LANE] = d_tap_bias[0:1, :]
+    query_bias = jnp.concatenate([grads[0:1, :] for grads in biases], axis=1)
+    value_bias = jnp.concatenate([grads[1:2, :] for grads in biases], axis=1)
+    out[row + 1 : row + 2, :] = query_bias + branch_bias[2:3, :]
+    out[row + 2 : row + 3, :] = value_bias
+    out[row + 3 : row + 5, :] = branch_bias[0:2, :]
+    row += 5
+    for index in range(inner_bias_grad.shape[0]):
+        out[row : row + 1, : inner_bias_grad.shape[2]] = inner_bias_grad[index]
+        row += 1
 
 
 def branch_weights_kernel(
@@ -685,14 +775,30 @@
     after,
     before,
     resid_grad,
+    vector_grads,
+    inner_bias_grad,
+    d_depth,
+    d_tap_weight,
+    d_tap_bias,
+    branch_bias,
+    bias_0,
+    bias_1,
+    bias_2,
     d_own,
     d_far,
     token_grad,
+    packed,
     ext,
     d_full,
     tokens,
     value_grad,
+    rows_wide,
 ):
+    pack(
+        rows_wide,
+        (vector_grads, inner_bias_grad, d_depth, d_tap_weight, d_tap_bias, branch_bias, (bias_0, bias_1, bias_2)),
+    )
+    packed[...] = rows_wide[...].astype(LOW)
     block_len = own.shape[0]
     size = d_own.shape[1] // 2
     for slot, source in enumerate((own, other)):
@@ -724,19 +830,21 @@
     grad_1,
     grad_2,
     g_query,
-    pair_0,
-    pair_1,
-    pair_2,
+    kept_0,
+    moved_0,
+    kept_1,
+    moved_1,
+    kept_2,
+    moved_2,
     d_own,
     d_far,
     lows,
-    bias_grad,
     d_full,
     tokens,
 ):
     block_len = own.shape[0]
     size = d_own.shape[1] // 3
-    pairs = (pair_0, pair_1, pair_2)
+    pairs = ((kept_0, moved_0), (kept_1, moved_1), (kept_2, moved_2))
     for slot, source in enumerate((own, other)):
         tokens[slot * block_len : (slot + 1) * block_len, :] = source[...]
     lows[0] = (
@@ -744,10 +852,12 @@
     ).astype(LOW)
     for part in range(2):
         lows[1 + part] = jnp.concatenate(
-            [pair[:, part * LANE : (part + 1) * LANE] for pair in pairs], axis=1
+            [
+                add_low(kept[0, :, part * LANE : (part + 1) * LANE], moved[0, :, part * LANE : (part + 1) * LANE])
+                for kept, moved in pairs
+            ],
+            axis=1,
         )
-    bias_grad[0:1, :] = column_sum(lows[0].astype(WIDE))
-    bias_grad[1:2, :] = column_sum(lows[2].astype(WIDE))
     for part in range(3):
         for half in range(2):
             lanes = slice(half * d_own.shape[2], (half + 1) * d_own.shape[2])
@@ -809,11 +919,10 @@
         doc_ids[:, 0].astype(LOW), ((0, DOC_ROWS - doc_ids.shape[0]), (0, lanes - block_len))
     )
     first = {(0, 0): jnp.concatenate([proj_t[:3].reshape(-1, lanes), doc_slab], axis=0)}
-    branch = {(0, 0): proj_t[3:].reshape(-1, lanes)}
-
-    def spread_row(held, *marks):
+
+    def spread_row(held):
         for dr, dc in list(held):
-            held[(1, dc)] = swap(after(held[(dr, dc)], *marks), "row", 1)
+            held[(1, dc)] = swap(held[(dr, dc)], "row", 1)
 
     def spread_col(held, step):
         for dr, dc in list(held):
@@ -832,10 +941,20 @@
     own, other = trade(tokens, first_row)
     for dr, dc in list(first):
         first[(dr, dc ^ 1)] = swap(first[(dr, dc)], "col", 1)
-    branch[(0, 0)] = after(branch[(0, 0)], first[(0, far_steps[0])])
+    edges = jnp.concatenate([own[block_len - RIM :], other[block_len - RIM :], own[:RIM], other[:RIM]], axis=0)
+    branch_parts = [proj_t[3:].reshape(-1, lanes), edges[:, :lanes], edges[:, lanes:]]
+    inner = inner_weight[0].T
+    branch_low = after(jnp.concatenate(branch_parts, axis=0), first[(1, far_steps[-1])])
+    branch_rows = branch_low.shape[0]
+    branch = {(0, 0): branch_low}
     for step in far_steps:
         spread_col(branch, step)
-    spread_row(branch, other)
+    sent = {key: value for key, value in branch.items() if key != (0, 0)}
+    branch[(1, 0)] = swap(jnp.concatenate([branch_low, inner], axis=0), "row", 1)
+    spread_row(sent)
+    branch.update(sent)
+    inner_moved = branch[(1, 0)][branch_rows:][None]
+    inner = inner[None]
     for dr, dc in list(branch):
         branch[(dr, dc ^ 1)] = swap(branch[(dr, dc)], "col", 1)
 
@@ -844,14 +963,9 @@
         edge = 0 if step > 0 else col_count - 1
         return jnp.where(col_here == edge, moved[::-1], moved)
 
-    low_rim = wrapped(jnp.stack([own[block_len - RIM :], other[block_len - RIM :]]), 1)
-    high_rim = wrapped(jnp.stack([own[:RIM], other[:RIM]]), -1)
-
-    inner = grow(after(inner_weight[0].T, other, branch[(1, 0)])[None], "row", 1)
-    inner_row = inner
     tail = grow(
         after(
-            jnp.concatenate([outer_weight[0], out_weight.T], axis=0), first[(1, far_steps[-1])]
+            jnp.concatenate([outer_weight[0], out_weight.T], axis=0), branch[(0, far_steps[-1])]
         )[None],
         "col",
         far_steps[0],
@@ -873,32 +987,21 @@
     ).astype(WIDE)
 
     first_keys = sorted(first, key=lambda key: (key[1] & 1, key[1], key[0]))
-    query, *pairs = kernel_call(
+    query, pairs, w_first = kernel_call(
         functools.partial(project_kernel, first_keys),
-        [((tokens_here, ATT), LOW)]
-        + [((tokens_here, 2 * LANE), LOW)] * PAIRS
-        + [((3, row_count, ATT, lanes), LOW)],
+        [
+            ((tokens_here, ATT), LOW),
+            ((tokens_here, 2 * ATT), LOW),
+            ((3, row_count, ATT, lanes), LOW),
+        ],
+        cost=0.05,
     )(here, own, other, wide_bias, *[first[key] for key in first_keys])
-    w_first = pairs.pop()
-
-    gathered = []
-    for pair in pairs:
-        pieces = [pair]
-        for step in far_steps:
-            pieces = pieces + [swap(piece, "col", step) for piece in pieces]
-        gathered.append(pieces)
-    far_pair = gathered[0][1]
-    for pieces in gathered:
-        pieces.extend([swap(piece, "col", 1) for piece in list(pieces)])
-    tail = grow(after(tail, inner_row, query), "row", 1)
-    inner = after(inner, far_pair)
+
+    gathered = [pairs]
     for step in far_steps:
-        inner = grow(inner, "col", step)
-    for step in far_steps[1:]:
-        tail = grow(tail, "col", step)
-    inner_own, inner_far = inner, swap(inner, "col", 1)
-    tail_own, tail_far = tail, swap(tail, "col", 1)
-    cot_own, cot_other = trade(cotangent, inner_row, query)
+        gathered = gathered + [swap(piece, "col", step) for piece in gathered]
+    tail = after(tail, query)
+    tail_moved = swap(tail, "row", 1)
 
     doc_blocks = jnp.stack(
         [
@@ -929,8 +1032,8 @@
 
     ext_len = block_len + 2 * RIM
     branch_keys = list(branch)
-    conv_context, depth_low, value_wide, key_conv, conv_attn, conv_weights, w_branch = kernel_call(
-        functools.partial(branch_kernel, branch_keys),
+    conv_context, depth_low, value_wide, key_conv, conv_attn, conv_weights, w_branch, low_rim, high_rim = kernel_call(
+        functools.partial(branch_kernel, branch_keys, cut_proj, col_count),
         [
             ((tokens_here, ATT), LOW),
             ((tokens_here, model_width), LOW),
@@ -939,6 +1042,8 @@
             ((tokens_here, ATT), LOW),
             ((tokens_here, KERNEL * LANE), WIDE),
             ((2, row_count, ATT, lanes), LOW),
+            ((2, RIM, model_width), LOW),
+            ((2, RIM, model_width), LOW),
         ],
         [((2, ext_len, model_width), WIDE)],
         cost=11,
@@ -946,8 +1051,6 @@
         here,
         own,
         other,
-        low_rim,
-        high_rim,
         doc_rows,
         depth_gain,
         wide_bias,
@@ -957,15 +1060,21 @@
         *[branch[key] for key in branch_keys],
     )
 
+    gathered.append(swap(pairs, "col", 1))
+    for piece in gathered[1 : col_count // 2]:
+        gathered.append(swap(after(piece, conv_context), "col", 1))
+    inner = jnp.concatenate([inner, after(inner_moved, conv_context)], axis=0)
+    for step in far_steps[:-1]:
+        inner = grow(inner, "col", step)
+    inner_far_moved = swap(inner, "col", far_steps[-1])
+    _, cot_other = trade(cotangent, conv_context)
+
     doc_query = doc_blocks[:2]
     attended = []
     stats = []
     for index in range(PAIRS):
-        query_pair = query[:, index * LANE : (index + 1) * LANE]
-        if index == 0:
-            query_pair = after(query_pair, conv_context)
         out, stat = kernel_call(
-            functools.partial(attend_kernel, col_count),
+            functools.partial(attend_kernel, col_count, index),
             [((tokens_here, LANE), LOW), ((2, 8, block_len), WIDE)],
             [
                 ((2 * col_count, 2, block_len, block_len), WIDE),
@@ -974,9 +1083,18 @@
                 ((2, LANE, block_len), WIDE),
             ],
             cost=8,
-        )(bounds, query_pair, doc_query, doc_key, *gathered[index])
+            parts=col_count,
+            part=index,
+        )(bounds, after(query, conv_context), doc_query, doc_key, *gathered)
         attended.append(out)
         stats.append(stat)
+
+    tail = jnp.concatenate([tail, after(tail_moved, conv_context)], axis=0)
+    for step in far_steps[1:]:
+        tail = grow(tail, "col", step)
+    inner = jnp.concatenate([inner, after(inner_far_moved, attended[0])], axis=0)
+    inner_own, inner_far = inner, swap(inner, "col", 1)
+    tail_own, tail_far = tail, swap(tail, "col", 1)
 
     (
         out_own,
@@ -1021,7 +1139,7 @@
         here,
         own,
         other,
-        cot_own,
+        cotangent,
         cot_other,
         *attended,
         conv_context,
@@ -1059,45 +1177,47 @@
                 self.finish(*marks)
             return self.finish(*marks)[0]
 
+        def terms(self, *marks):
+            while self.todo:
+                self.finish(*marks)
+            return self.kept, self.moved
+
     inner_sum = GridSum(d_inner_own, d_inner_far, row_stages)
     tail_sum = GridSum(d_tail_own, d_tail_far, col_stages)
     query_grads = []
+    bias_grads = []
     pair_sums = []
-    marks = []
-    for index in range(PAIRS):
-        query_pair = query[:, index * LANE : (index + 1) * LANE]
-        if marks:
-            query_pair = after(query_pair, *marks)
-        grad_query, grad_own, grad_far = kernel_call(
-            functools.partial(attend_back_kernel, col_count),
+
+    def attend_back(index, *marks):
+        grad_query, grad_own, grad_far, bias_grad = kernel_call(
+            functools.partial(attend_back_kernel, col_count, index),
             [
                 ((tokens_here, LANE), WIDE),
                 ((pair_entries, tokens_here, 2 * LANE), LOW),
                 ((pair_entries, tokens_here, 2 * LANE), LOW),
+                ((8, LANE), WIDE),
             ],
             [((2, 8, block_len), WIDE), ((block_len, 2 * LANE), WIDE)],
             cost=13,
+            parts=col_count,
+            part=index,
         )(
             bounds,
-            query_pair,
+            after(query, *marks) if marks else query,
             doc_query,
             doc_key,
             attended[index],
             g_att[index],
             stats[index],
-            *gathered[index],
+            *gathered,
         )
         query_grads.append(grad_query)
+        bias_grads.append(bias_grad)
         pair_sums.append(GridSum(grad_own, grad_far, [("col", step) for step in reversed(far_steps)]))
-        marks = [grad_query]
-        if len(inner_sum.todo) > 0:
-            marks += [inner_sum.finish(grad_query), tail_sum.finish(grad_query)]
-        if index > 0:
-            marks.append(pair_sums[index - 1].finish(grad_query))
-    marks.append(pair_sums[-1].finish())
-    wide_part = jnp.concatenate([inner_sum.rest(grad_query), tail_sum.rest(grad_query)], axis=0)
-    wide_sum = DataSum(wide_part)
-
+        return grad_query
+
+    done = attend_back(0)
+    marks = [inner_sum.finish(done), tail_sum.finish(done)]
     (
         g_key_conv,
         g_query,
@@ -1107,22 +1227,28 @@
         branch_bias,
         g_ext_value,
         g_ext_tokens,
+        first_rim,
+        last_rim,
     ) = kernel_call(
         branch_back_kernel,
         [
             ((tokens_here, ATT), LOW),
             ((tokens_here, ATT), WIDE),
-            ((ATT, KERNEL * LANE), WIDE),
-            ((1, KERNEL * LANE), WIDE),
+            ((LANE, ATT), WIDE),
+            ((8, LANE), WIDE),
             ((16, model_width), WIDE),
             ((8, ATT), WIDE),
             ((2, ext_len, ATT), WIDE),
             ((2, ext_len, model_width), WIDE),
+            ((2, RIM, ATT + model_width), LOW),
+            ((2, RIM, ATT + model_width), LOW),
         ],
         [
             ((2, ext_len, model_width), WIDE),
             ((block_len, KERNEL * LANE), WIDE),
             ((block_len, KERNEL * LANE), LOW),
+            ((ATT, KERNEL * LANE), WIDE),
+            ((8, KERNEL * LANE), WIDE),
         ],
         smem=0,
         cost=16,
@@ -1136,41 +1262,33 @@
         depth_gain,
         tap_weight,
         query,
-        after(g_conv, wide_part, *marks),
+        after(g_conv, *marks),
         value_wide,
         key_conv,
         conv_attn,
         conv_weights,
     )
-    pair_grads = [part.rest(g_query) for part in pair_sums]
-    wide_stage = wide_sum.finish(g_query)
-
-    def rim_of(start):
-        return jnp.concatenate(
-            [g_ext_value[:, start : start + RIM], g_ext_tokens[:, start : start + RIM]], axis=2
-        ).astype(LOW)
-
-    from_after = wrapped(rim_of(0), -1)
-    from_before = wrapped(rim_of(RIM + block_len), 1)
-
-    d_first_own, d_first_far, lows, first_bias = kernel_call(
-        first_weights_kernel,
-        [((entries, 3 * cut_proj, lanes), LOW)] * 2
-        + [((3, tokens_here, ATT), LOW), ((8, ATT), WIDE)],
-        [((3, row_count, ATT, lanes), LOW), ((tokens_here, model_width), LOW)],
-        cost=6,
-    )(here, own, other, *query_grads, after(g_query, wide_stage), *pair_grads)
-    first_sum = GridSum(d_first_own, d_first_far, row_stages)
-    wide_stage = wide_sum.finish(first_bias)
-
-    d_branch_own, d_branch_far, token_grad = kernel_call(
+    marks = [pair_sums[0].finish(g_query), inner_sum.finish(g_query), tail_sum.finish(g_query)]
+    done = attend_back(1, *marks)
+    from_after = wrapped(after(first_rim, done), -1)
+    from_before = wrapped(after(last_rim, done), 1)
+    wide_part = jnp.concatenate([inner_sum.rest(done), tail_sum.rest(done)], axis=0)
+    wide_sum = DataSum(wide_part)
+    done = attend_back(2, wide_part, pair_sums[1].finish())
+    marks = [pair_sums[2].finish(), wide_sum.finish(done)]
+    inner_rows = inner_bias_grad.shape[0]
+    packed_rows = 2 * (6 + KERNEL) + HEADS * KERNEL + 5 + inner_rows
+    packed_rows += -packed_rows % 16
+    d_branch_own, d_branch_far, token_grad, packed = kernel_call(
         branch_weights_kernel,
-        [((entries, 2 * cut_proj, lanes), LOW)] * 2 + [((tokens_here, model_width), WIDE)],
+        [((entries, 2 * cut_proj, lanes), LOW)] * 2
+        + [((tokens_here, model_width), WIDE), ((packed_rows, lanes), LOW)],
         [
             ((block_len, ATT + model_width), WIDE),
             ((2, row_count, ATT, lanes), LOW),
             ((tokens_here, model_width), LOW),
             ((tokens_here, ATT), LOW),
+            ((packed_rows, lanes), WIDE),
         ],
         cost=6,
     )(
@@ -1179,72 +1297,89 @@
         other,
         w_branch,
         depth_low,
-        after(g_key_conv, lows, wide_stage),
+        after(g_key_conv, done, *marks),
         g_ext_value,
         g_ext_tokens,
         from_after,
         from_before,
         resid_grad,
+        vector_grads,
+        inner_bias_grad,
+        d_depth,
+        d_tap_weight,
+        d_tap_bias,
+        branch_bias,
+        *bias_grads,
     )
+    flat_sum = FlatSum(packed)
     branch_sum = GridSum(d_branch_own, d_branch_far, col_stages)
+    terms = [term for pair in pair_sums for term in pair.terms(token_grad)]
     wide_stage = wide_sum.finish(token_grad)
-    first_stage = first_sum.finish(token_grad)
-    branch_stage = branch_sum.finish()
+    d_first_own, d_first_far, lows = kernel_call(
+        first_weights_kernel,
+        [((entries, 3 * cut_proj, lanes), LOW)] * 2
+        + [((3, tokens_here, ATT), LOW)],
+        [((3, row_count, ATT, lanes), LOW), ((tokens_here, model_width), LOW)],
+        cost=0.05,
+    )(here, own, other, *query_grads, after(g_query, wide_stage), *terms)
+    first_sum = GridSum(d_first_own, d_first_far, row_stages)
+
+    flat_stage = flat_sum.finish(lows)
+    branch_stage = branch_sum.finish(lows)
+    first_stage = first_sum.finish()
     token_own, token_other = kernel_call(
         token_kernel,
         [((block_len, model_width), WIDE), ((block_len, model_width), LOW)],
         smem=0,
-        cost=6,
-    )(w_first, lows, after(token_grad, wide_stage, first_stage, branch_stage))
-    wide_sum.finish(token_own)
-    wide_sum = wide_sum.rest().astype(WIDE)
-    first_part = first_sum.rest(token_own)
-    branch_part = branch_sum.rest(token_own)
-    proj_sum = DataSum(jnp.concatenate([first_part, branch_part], axis=0)).rest().astype(WIDE)
-
-    def tap_layout(grads):
-        return grads.reshape(-1, KERNEL, LANE)[:, :, :HEADS].transpose(0, 2, 1).reshape(-1, HEADS * KERNEL)
-
-    items = [
-        vector_grads[:6],
-        inner_bias_grad,
-        d_depth[:KERNEL],
-        tap_layout(d_tap_weight),
-        tap_layout(d_tap_bias),
-        branch_bias[:2],
-        first_bias[:2],
-    ]
-    flat = jnp.concatenate([item.reshape(-1) for item in items])
-    flat = jnp.pad(flat, (0, -flat.shape[0] % 1024)).reshape(-1, LANE)
-    flat = grid_sum(flat).reshape(-1)
+        cost=0.05,
+    )(w_first, lows, after(token_grad, first_stage, branch_stage, flat_stage))
+    first_stage = first_sum.finish(token_own)
+    branch_stage = branch_sum.finish(token_own)
+    wide_stage = wide_sum.finish(token_own)
+    flat_sum.finish(first_stage, branch_stage, wide_stage)
+    token_other = after(token_other, first_stage)
+    first_part = first_sum.rest()
+    branch_part = branch_sum.rest(first_stage)
+    proj_sum = DataSum(jnp.concatenate([first_part, branch_part], axis=0))
+    while len(flat_sum.todo) > 1:
+        flat_sum.finish(first_part)
+    proj_stage = proj_sum.finish()
+    wide_sum = wide_sum.rest(proj_stage).astype(WIDE)
+    flat_sum.finish(proj_stage)
+    proj_stage = proj_sum.finish()
+    proj_sum = proj_sum.rest().astype(WIDE)
+    flat = flat_sum.low.astype(WIDE)
     finals = []
     start = 0
-    for item in items:
-        finals.append(flat[start : start + item.size].reshape(item.shape))
-        start += item.size
-    vector_sum, inner_bias_sum, depth_sum, tap_weight_sum, tap_bias_sum, branch_bias_sum, first_bias_sum = finals
-
-    def give_back(here_rows, there_rows):
+    for count in (12, 2 * KERNEL, HEADS * KERNEL, 1, 4, inner_rows):
+        finals.append(flat[start : start + count])
+        start += count
+    vector_sum, depth_sum, tap_weight_sum, tap_bias_sum, bias_sum, inner_bias_sum = finals
+    vector_sum = vector_sum.reshape(6, -1)
+
+    def give_back(here_rows, there_rows, *marks):
         moved = swap(there_rows, "row", 1).astype(here_rows.dtype)
+        if marks:
+            moved = after(moved, *marks)
         return jnp.where(
             row_here == 0, jnp.stack([here_rows, moved]), jnp.stack([moved, here_rows])
         )
 
     return (
-        give_back(out_own, out_other),
-        give_back(token_own, token_other),
+        give_back(out_own, out_other, first_stage),
+        give_back(token_own, token_other, proj_stage),
         jnp.transpose(proj_sum.reshape(5, cut_proj, lanes), (0, 2, 1)),
         wide_sum[2 * cut_inner :].T,
         wide_sum[:cut_inner].T[None],
         wide_sum[cut_inner : 2 * cut_inner][None],
-        depth_sum,
-        jnp.concatenate([first_bias_sum, branch_bias_sum], axis=0),
-        tap_weight_sum,
-        tap_bias_sum[0],
+        depth_sum.reshape(KERNEL, -1),
+        bias_sum,
+        tap_weight_sum.T,
+        tap_bias_sum[0, : HEADS * KERNEL],
         vector_sum[5],
         vector_sum[3],
         vector_sum[4],
-        inner_bias_sum.reshape(-1),
+        inner_bias_sum[:, :cut_inner].reshape(-1),
         vector_sum[2],
         vector_sum[0],
         vector_sum[1],

time: 356 us -> 318 us (0.89)
  waiting for transfers between devices: 81.4 us -> 52.6 us
  other arithmetic: 40.5 us -> 29.4 us
  starting transfers between devices: 59.9 us -> 69.2 us
  Pallas kernels: 137 us -> 131 us
  local copies, waits for them, and re-layouts: 31.7 us -> 28 us
    ppermute x64 -> x57, waiting for transfers between devices: 72.2 us -> 52.1 us  [swap(): return lax.ppermute(block, axis, [(i, i ^ step) for i in range(count)])]
    ppermute x64 -> x57, starting transfers between devices: 54.3 us -> 64.4 us  [swap(): return lax.ppermute(block, axis, [(i, i ^ step) for i in range(count)])]
    ppermute x4 -> x2, waiting for transfers between devices: 9.16 us -> 0.5 us  [shift(): lax.ppermute(block, axis, [(i, (i + step) % count) for i in range(count)])]
    squeeze x7 -> x4, other arithmetic: 9.03 us -> 2.4 us  [rest(): return self.finish(*marks)[0]]
    pallas_call x13, Pallas kernels: 137 us -> 131 us  [run(): pl.pallas_call(body, grid=(1,), in_specs=specs, out_specs=[pl.BlockSpec(m...]
    slice x12 -> x8, local copies, waits for them, and re-layouts: 5.4 us -> 1.56 us  [the longest x1 0.92 us: local(): proj_t[3:].reshape(-1, lanes)]
    convert_element_type x15 -> x19, other arithmetic: 15.2 us -> 12 us  [add_low(): return (kept.astype(WIDE) + moved.astype(WIDE)).astype(LOW)]
  transfers between devices with their start and end apart: 68 -> 59, of which waited for: 20 -> 18; matrix products, arithmetic and copies ran while one was open for 19% -> 16% of each run, Pallas kernels for 30% -> 30%
where the time goes in v4:
time: 318 us; the launch traced here: 313 us
  Pallas kernels  131 us (41%)
  starting transfers between devices  69.2 us (22%)
  waiting for transfers between devices  52.6 us (17%)
  other arithmetic  29.4 us (9%)
  local copies, waits for them, and re-layouts  28 us (9%)
    pallas_call x13, Pallas kernels, run(): pl.pallas_call(body, grid=(1,), in_specs=specs, out_specs=[pl.BlockSpec(m...  131 us
    ppermute x57, starting transfers between devices, swap(): return lax.ppermute(block, axis, [(i, i ^ step) for i in range(count)])  64.4 us
    ppermute x57, waiting for transfers between devices, swap(): return lax.ppermute(block, axis, [(i, i ^ step) for i in range(count)])  52.1 us
    convert_element_type x19, other arithmetic, add_low(): return (kept.astype(WIDE) + moved.astype(WIDE)).astype(LOW)  12 us
  transfers between devices with their start and end apart: 59, of which 18 were waited for; matrix products, arithmetic and copies ran while one was open for 16% of the time, Pallas kernels for 30%

profile of v4, /device:TPU:0, one launch (start us, length us, event | category | flops | bytes accessed | tf_op | source)
XLA Modules:
  0.0 312.8 jit_solution(8514723395604424005)
XLA Ops:
  2.4 3.0 collective-permute-start
  23.5 4.0 %collective-permute-done.3.rest_3_ = bf16[304,384]{1,0:T(8,128)(2,1)S(1)} collective-permute-done((bf16[304,384]{1,0:T(8,128)(2,1)S(1)}, bf16[304,384]{1,0:T(8,128)(2,1)S(1)}, u32[]{:S(2)}, u32[]{:S(2)}) %collective-permute-start.3) | collective-permute-done | bytes 233504 | tf_op jit(solution)/shard_map/ppermute | solution.py:28
  30.7 5.9 %collective-permute-done.8.rest_1_ = bf16[256,384]{1,0:T(8,128)(2,1)S(1)} collective-permute-done((bf16[256,384]{1,0:T(8,128)(2,1)S(1)}, bf16[256,384]{1,0:T(8,128)(2,1)S(1)}, u32[]{:S(2)}, u32[]{:S(2)}) %collective-permute-start.8) | collective-permute-done | bytes 196640 | tf_op jit(solution)/shard_map/ppermute | solution.py:28
  37.2 2.8 collective-permute-done.9.rest_2_
  41.9 5.1 %shard_map.305 = (bf16[512,384]{1,0:T(8,128)(2,1)}, bf16[512,768]{1,0:T(8,128)(2,1)}, bf16[3,2,384,384]{3,2,1,0:T(8,128)(2,1)}) custom-call(s32[2]{0:T(128)} %pad_add_fusion.4.here, bf16[256,768]{1,0:T(8,128)(2,1)} %get-tuple-element.259.own, bf16[256,768]{1,0:T(8,128)(2,1)} %copy-done.1, f32[4,384]{1,0:T(4,128)} %convert_element_type.378.bias, ...), custom_call_target="tpu_custom_call" | custom-call | flops 50000000 | bytes 180000 | tf_op jit(solution)/shard_map/pallas_call | solution.py:68
  50.8 10.9 %shard_map.306 = (bf16[512,384]{1,0:T(8,128)(2,1)}, bf16[512,768]{1,0:T(8,128)(2,1)}, f32[2,272,384]{2,1,0:T(8,128)}, f32[512,384]{1,0:T(8,128)}, bf16[512,384]{...) custom-call(s32[2]{0:T(128)} %pad_add_fusion.4.here, ...), custom_call_target="tpu_custom_call" | custom-call | flops 11000000512 | bytes 39600000 | tf_op jit(solution)/shard_map/pallas_call | solution.py:68
  61.7 6.0 %collective-permute-done.16.rest_1_ = bf16[512,768]{1,0:T(8,128)(2,1)} collective-permute-done((bf16[512,768]{1,0:T(8,128)(2,1)}, bf16[512,768]{1,0:T(8,128)(2,1)}, u32[]{:S(2)}, u32[]{:S(2)}) %collective-permute-start.16) | collective-permute-done | bytes 786464 | tf_op jit(solution)/shard_map/ppermute | solution.py:28
  75.7 6.5 %shard_map.307 = (bf16[512,128]{1,0:T(8,128)(2,1)}, f32[2,8,256]{2,1,0:T(8,128)}) custom-call(s32[8,2]{1,0:T(8,128)} %pad_add_fusion.bounds, bf16[512,384]{1,0:T(8,128)(2,1)} %get-tuple-element.170.query, s32[2,256]{1,0:T(2,128)} %slice.353.doc_query, s32[8,256,128]{2,1,0:T(8,128)} %broadcast_in_dim.36.doc_key, bf16[512,768]{1,0:T(8,128)(2,1)} %get-tuple-element.126.rest_0_, ...), custom_call_target="tpu_custom_call" | custom-call | flops 8000000000 | bytes 28800000 | tf_op jit(solution)/shard_map/pallas_call | solution.py:68
  82.2 4.8 %collective-permute-done.19 = bf16[2,384,384]{2,1,0:T(8,128)(2,1)} collective-permute-done((bf16[2,384,384]{2,1,0:T(8,128)(2,1)S(1)}, bf16[2,384,384]{2,1,0:T(8,128)(2,1)}, u32[]{:S(2)}, u32[]{:S(2)}) %collective-permute-start.19) | collective-permute-done | bytes 589856 | tf_op jit(solution)/shard_map/ppermute | solution.py:28
  88.3 6.7 %shard_map.309 = (bf16[512,128]{1,0:T(8,128)(2,1)}, f32[2,8,256]{2,1,0:T(8,128)}) custom-call(s32[8,2]{1,0:T(8,128)} %pad_add_fusion.bounds, bf16[512,384]{1,0:T(8,128)(2,1)} %get-tuple-element.170.query, s32[2,256]{1,0:T(2,128)} %slice.353.doc_query, s32[8,256,128]{2,1,0:T(8,128)} %broadcast_in_dim.36.doc_key, bf16[512,768]{1,0:T(8,128)(2,1)} %get-tuple-element.126.rest_0_, ...), custom_call_target="tpu_custom_call" | custom-call | flops 8000000000 | bytes 28800000 | tf_op jit(solution)/shard_map/pallas_call | solution.py:68
  95.0 6.3 %shard_map.308 = (bf16[512,128]{1,0:T(8,128)(2,1)}, f32[2,8,256]{2,1,0:T(8,128)}) custom-call(s32[8,2]{1,0:T(8,128)} %pad_add_fusion.bounds, bf16[512,384]{1,0:T(8,128)(2,1)} %get-tuple-element.170.query, s32[2,256]{1,0:T(2,128)} %slice.353.doc_query, s32[8,256,128]{2,1,0:T(8,128)} %broadcast_in_dim.36.doc_key, bf16[512,768]{1,0:T(8,128)(2,1)} %get-tuple-element.126.rest_0_, ...), custom_call_target="tpu_custom_call" | custom-call | flops 8000000000 | bytes 28800000 | tf_op jit(solution)/shard_map/pallas_call | solution.py:68
  102.4 32.5 %shard_map.310 = (bf16[256,768]{1,0:T(8,128)(2,1)}, bf16[256,768]{1,0:T(8,128)(2,1)}, f32[512,768]{1,0:T(8,128)}, bf16[512,128]{1,0:T(8,128)(2,1)}, bf16[512,128...) custom-call(s32[2]{0:T(128)} %pad_add_fusion.4.here, ...), custom_call_target="tpu_custom_call" | custom-call | flops 30000001024 | bytes 108000000 | tf_op jit(solution)/shard_map/pallas_call | solution.py:68
  137.1 10.0 %shard_map.311 = (f32[512,128]{1,0:T(8,128)}, bf16[2,512,256]{2,1,0:T(8,128)(2,1)}, bf16[2,512,256]{2,1,0:T(8,128)(2,1)}, f32[8,128]{1,0:T(8,128)}) custom-call(s32[8,2]{1,0:T(8,128)} %pad_add_fusion.bounds, bf16[512,384]{1,0:T(8,128)(2,1)} %get-tuple-element.170.query, s32[2,256]{1,0:T(2,128)} %slice.353.doc_query, ...), custom_call_target="tpu_custom_call" | custom-call | flops 12999999488 | bytes 46800000 | tf_op jit(solution)/shard_map/pallas_call | solution.py:68
  149.2 2.5 add_convert_fusion.2
  151.7 5.8 %collective-permute-start.28 = (bf16[2,384,384]{2,1,0:T(8,128)(2,1)}, bf16[2,384,384]{2,1,0:T(8,128)(2,1)}, u32[]{:S(2)}, u32[]{:S(2)}) collective-permute-start(bf16[2,384,384]{2,1,0:T(8,128)(2,1)} %get-tuple-element.243), channel_id=1, source_target_pairs={{0,2},{1,3},{2,0},{3,1},{4,6},{5,7},{6,4},{7,5},{8,10},{9,11},{10,... | collective-permute-start | bytes 1769480 | tf_op jit(solution)/shard_map/ppermute | solution.py:28
  158.9 3.3 %collective-permute-start.29 = (bf16[2,576,384]{2,1,0:T(8,128)(2,1)}, bf16[2,576,384]{2,1,0:T(8,128)(2,1)S(1)}, u32[]{:S(2)}, u32[]{:S(2)}) collective-permute-start(bf16[2,576,384]{2,1,0:T(8,128)(2,1)} %get-tuple-element.241), channel_id=1, source_target_pairs={{0,4},{4,0},{1,5},{5,1},{2,6},{6,2},{3,7},{7,3},{8,12},{12,8},{9,1... | collective-permute-start | bytes 2654216 | tf_op jit(solution)/shard_map/ppermute | solution.py:28
  162.2 16.8 %shard_map.312 = (bf16[512,384]{1,0:T(8,128)(2,1)}, f32[512,384]{1,0:T(8,128)}, f32[128,384]{1,0:T(8,128)}, f32[8,128]{1,0:T(8,128)}, f32[16,768]{1,0:T(8,128)},...) custom-call(bf16[256,768]{1,0:T(8,128)(2,1)} %get-tuple-element.259., ...), custom_call_target="tpu_custom_call" | custom-call | flops 16000000000 | bytes 57600000 | tf_op jit(solution)/shard_map/pallas_call | solution.py:68
  185.4 9.9 %shard_map.313 = (f32[512,128]{1,0:T(8,128)}, bf16[2,512,256]{2,1,0:T(8,128)(2,1)}, bf16[2,512,256]{2,1,0:T(8,128)(2,1)}, f32[8,128]{1,0:T(8,128)}) custom-call(s32[8,2]{1,0:T(8,128)} %pad_add_fusion.bounds, bf16[512,384]{1,0:T(8,128)(2,1)} %get-tuple-element.170.query, s32[2,256]{1,0:T(2,128)} %slice.353.doc_query, ...), custom_call_target="tpu_custom_call" | custom-call | flops 12999999488 | bytes 46800000 | tf_op jit(solution)/shard_map/pallas_call | solution.py:68
  195.9 4.1 %collective-permute-start.36 = (bf16[2,8,1152]{2,1,0:T(8,128)(2,1)}, bf16[2,8,1152]{2,1,0:T(8,128)(2,1)}, u32[]{:S(2)}, u32[]{:S(2)}) collective-permute-start(bf16[2,8,1152]{2,1,0:T(8,128)(2,1)} %get-tuple-element.183), channel_id=1, source_target_pairs={{0,3},{1,0},{2,1},{3,2},{4,7},{5,4},{6,5},{7,6},{8,11},{9,8},{10,9... | collective-permute-start | bytes 110600 | tf_op jit(solution)/shard_map/ppermute | solution.py:33
  205.3 10.1 %shard_map.314 = (f32[512,128]{1,0:T(8,128)}, bf16[2,512,256]{2,1,0:T(8,128)(2,1)}, bf16[2,512,256]{2,1,0:T(8,128)(2,1)}, f32[8,128]{1,0:T(8,128)}) custom-call(s32[8,2]{1,0:T(8,128)} %pad_add_fusion.bounds, bf16[512,384]{1,0:T(8,128)(2,1)} %get-tuple-element.170.query, s32[2,256]{1,0:T(2,128)} %slice.353.doc_query, ...), custom_call_target="tpu_custom_call" | custom-call | flops 12999999488 | bytes 46800000 | tf_op jit(solution)/shard_map/pallas_call | solution.py:68
  218.8 3.0 collective-permute-start.39
  222.0 7.0 %collective-permute-start.34 = (bf16[240,384]{1,0:T(8,128)(2,1)S(1)}, bf16[240,384]{1,0:T(8,128)(2,1)S(1)}, u32[]{:S(2)}, u32[]{:S(2)}) collective-permute-start(bf16[240,384]{1,0:T(8,128)(2,1)S(1)} %dynamic-slice_bitcast_fusion.5), channel_id=1, source_target_pairs={{0,16},{8,24},{16,0},{24,8},{1,17},{9,25},{17,1},{25,9},{2,18},{10... | collective-permute-start | bytes 552968 | tf_op jit(solution)/shard_map/ppermute | solution.py:28
  231.8 6.6 %shard_map.315 = (bf16[4,192,384]{2,1,0:T(8,128)(2,1)}, bf16[4,192,384]{2,1,0:T(8,128)(2,1)}, f32[512,768]{1,0:T(8,128)}, bf16[112,384]{1,0:T(8,128)(2,1)}) custom-call(s32[2]{0:T(128)} %pad_add_fusion.4.here, bf16[256,768]{1,0:T(8,128)(2,1)} %get-tuple-element.259.own, bf16[256,768]{1,0:T(8,128)(2,1)} %copy-done.1, ...), custom_call_target="tpu_custom_call" | custom-call | flops 6000000000 | bytes 21600000 | tf_op jit(solution)/shard_map/pallas_call | solution.py:68
  239.3 5.5 %shard_map.316 = (bf16[4,288,384]{2,1,0:T(8,128)(2,1)}, bf16[4,288,384]{2,1,0:T(8,128)(2,1)}, bf16[3,512,384]{2,1,0:T(8,128)(2,1)}) custom-call(s32[2]{0:T(128)} %pad_add_fusion.4.here, bf16[256,768]{1,0:T(8,128)(2,1)} %get-tuple-element.259.own, bf16[256,768]{1,0:T(8,128)(2,1)} %copy-done.1, f32[512,128]{1,0:T(8,128)} %get-tuple-element.140.grad_0, ...), custom_call_target="tpu_custom_call" | custom-call | flops 50000000 | bytes 180000 | tf_op jit(solution)/shard_map/pallas_call | solution.py:68
  245.4 4.4 %collective-permute-start.53 = (bf16[240,384]{1,0:T(8,128)(2,1)S(1)}, bf16[240,384]{1,0:T(8,128)(2,1)}, u32[]{:S(2)}, u32[]{:S(2)}) collective-permute-start(bf16[240,384]{1,0:T(8,128)(2,1)S(1)} %fusion.5), channel_id=1, source_target_pairs={{0,16},{8,24},{16,0},{24,8},{1,17},{9,25},{17,1},{25,9},{2,18},{10... | collective-permute-start | bytes 552968 | tf_op jit(solution)/shard_map/ppermute | solution.py:28
  255.6 4.6 %shard_map.317 = (f32[256,768]{1,0:T(8,128)}, bf16[256,768]{1,0:T(8,128)(2,1)}) custom-call(bf16[3,2,384,384]{3,2,1,0:T(8,128)(2,1)} %get-tuple-element.201.w_full, bf16[3,512,384]{2,1,0:T(8,128)(2,1)} %get-tuple-element.202.lows, f32[512,768]{1,0:T(8,128)} %get-tuple-element.208.token_in), custom_call_target="tpu_custom_call" | custom-call | flops 50000000 | bytes 180000 | tf_op jit(solution)/shard_map/pallas_call | solution.py:68
  260.3 3.6 %collective-permute-done.47 = bf16[2,192,384]{2,1,0:T(8,128)(2,1)S(1)} collective-permute-done((bf16[2,192,384]{2,1,0:T(8,128)(2,1)}, bf16[2,192,384]{2,1,0:T(8,128)(2,1)S(1)}, u32[]{:S(2)}, u32[]{:S(2)}) %collective-permute-start.47) | collective-permute-done | bytes 294944 | tf_op jit(solution)/shard_map/ppermute | solution.py:28
  272.9 2.9 collective-permute-done.46
  280.5 3.5 %collective-permute-start.58 = (bf16[112,384]{1,0:T(8,128)(2,1)S(1)}, bf16[112,384]{1,0:T(8,128)(2,1)S(1)}, u32[]{:S(2)}, u32[]{:S(2)}) collective-permute-start(bf16[112,384]{1,0:T(8,128)(2,1)S(1)} %add_convert_fusion.27), channel_id=1, source_target_pairs={{0,16},{8,24},{16,0},{24,8},{1,17},{9,25},{17,1},{25,9},{2,18},{10... | collective-permute-start | bytes 258056 | tf_op jit(solution)/shard_map/ppermute | solution.py:28
  286.0 3.2 %collective-permute-done.58 = bf16[112,384]{1,0:T(8,128)(2,1)S(1)} collective-permute-done((bf16[112,384]{1,0:T(8,128)(2,1)S(1)}, bf16[112,384]{1,0:T(8,128)(2,1)S(1)}, u32[]{:S(2)}, u32[]{:S(2)}) %collective-permute-start.58) | collective-permute-done | bytes 86048 | tf_op jit(solution)/shard_map/ppermute | solution.py:28
  291.1 5.7 %collective-permute-done.50 = bf16[120,384]{1,0:T(8,128)(2,1)S(1)} collective-permute-done((bf16[120,384]{1,0:T(8,128)(2,1)S(1)}, bf16[120,384]{1,0:T(8,128)(2,1)S(1)}, u32[]{:S(2)}, u32[]{:S(2)}) %collective-permute-start.50) | collective-permute-done | bytes 92192 | tf_op jit(solution)/shard_map/ppermute | solution.py:28
  297.0 5.9 %collective-permute-done.51 = bf16[120,384]{1,0:T(8,128)(2,1)S(1)} collective-permute-done((bf16[120,384]{1,0:T(8,128)(2,1)S(1)}, bf16[120,384]{1,0:T(8,128)(2,1)S(1)}, u32[]{:S(2)}, u32[]{:S(2)}) %collective-permute-start.51) | collective-permute-done | bytes 92192 | tf_op jit(solution)/shard_map/ppermute | solution.py:28
  (305 shorter events, 97.6 us)
Async XLA Ops:
  5.5 16.2 %collective-permute-start.2 = (bf16[304,384]{1,0:T(8,128)(2,1)S(1)}, bf16[304,384]{1,0:T(8,128)(2,1)S(1)}, u32[]{:S(2)}, u32[]{:S(2)}) collective-permute-start(bf16[304,384]{1,0:T(8,128)(2,1)S(1)} %fusion.7.rest_0_), channel_id=1, source_target_pairs={{0,2},{1,3},{2,0},{3,1},{4,6},{5,7},{6,4},{7,5},{8,10},{9,11},{10,... | collective-permute-start | bytes 700424 | tf_op jit(solution)/shard_map/ppermute | solution.py:28
  7.0 22.1 %collective-permute-start.4 = (bf16[304,384]{1,0:T(8,128)(2,1)S(1)}, bf16[304,384]{1,0:T(8,128)(2,1)S(1)}, u32[]{:S(2)}, u32[]{:S(2)}) collective-permute-start(bf16[304,384]{1,0:T(8,128)(2,1)S(1)} %fusion.7.rest_0_), channel_id=1, source_target_pairs={{0,1},{1,0},{2,3},{3,2},{4,5},{5,4},{6,7},{7,6},{8,9},{9,8},{10,11... | collective-permute-start | bytes 700424 | tf_op jit(solution)/shard_map/ppermute | solution.py:28
  11.9 11.5 %collective-permute-start.1 = (bf16[256,768]{1,0:T(8,128)(2,1)S(1)}, bf16[256,768]{1,0:T(8,128)(2,1)S(1)}, u32[]{:S(2)}, u32[]{:S(2)}) collective-permute-start(bf16[256,768]{1,0:T(8,128)(2,1)S(1)} %get-tuple-element.120), channel_id=1, source_target_pairs={{0,4},{4,0},{1,5},{5,1},{2,6},{6,2},{3,7},{7,3},{8,12},{12,8},{9,1... | collective-permute-start | bytes 1179656 | tf_op jit(solution)/shard_map/ppermute | solution.py:28
  27.5 12.4 %collective-permute-start.9 = (bf16[640,384]{1,0:T(8,128)(2,1)S(1)}, bf16[640,384]{1,0:T(8,128)(2,1)}, u32[]{:S(2)}, u32[]{:S(2)}) collective-permute-start(bf16[640,384]{1,0:T(8,128)(2,1)S(1)} %pad_maximum_fusion.4), channel_id=1, source_target_pairs={{0,4},{4,0},{1,5},{5,1},{2,6},{6,2},{3,7},{7,3},{8,12},{12,8},{9,1... | collective-permute-start | bytes 1474568 | tf_op jit(solution)/shard_map/ppermute | solution.py:28
  29.8 19.3 %collective-permute-start.11 = (bf16[256,384]{1,0:T(8,128)(2,1)S(1)}, bf16[256,384]{1,0:T(8,128)(2,1)}, u32[]{:S(2)}, u32[]{:S(2)}) collective-permute-start(bf16[256,384]{1,0:T(8,128)(2,1)S(1)} %pad_maximum_fusion.7.rest_0_), channel_id=1, source_target_pairs={{0,1},{1,0},{2,3},{3,2},{4,5},{5,4},{6,7},{7,6},{8,9},{9,8},{10,11... | collective-permute-start | bytes 589832 | tf_op jit(solution)/shard_map/ppermute | solution.py:28
  36.6 11.9 %collective-permute-start.21 = (bf16[1,576,384]{2,1,0:T(8,128)(2,1)S(1)}, bf16[1,576,384]{2,1,0:T(8,128)(2,1)S(1)}, u32[]{:S(2)}, u32[]{:S(2)}) collective-permute-start(bf16[1,576,384]{2,1,0:T(8,128)(2,1)S(1)} %bitcast.107), channel_id=1, source_target_pairs={{0,2},{1,3},{2,0},{3,1},{4,6},{5,7},{6,4},{7,5},{8,10},{9,11},{10,... | collective-permute-start | bytes 1327112 | tf_op jit(solution)/shard_map/ppermute | solution.py:28
  48.5 19.3 %collective-permute-start.16 = (bf16[512,768]{1,0:T(8,128)(2,1)}, bf16[512,768]{1,0:T(8,128)(2,1)}, u32[]{:S(2)}, u32[]{:S(2)}) collective-permute-start(bf16[512,768]{1,0:T(8,128)(2,1)} %get-tuple-element.126.rest_0_), channel_id=1, source_target_pairs={{0,2},{1,3},{2,0},{3,1},{4,6},{5,7},{6,4},{7,5},{8,10},{9,11},{10,... | collective-permute-start | bytes 2359304 | tf_op jit(solution)/shard_map/ppermute | solution.py:28
  49.1 25.2 %collective-permute-start.17 = (bf16[512,768]{1,0:T(8,128)(2,1)}, bf16[512,768]{1,0:T(8,128)(2,1)}, u32[]{:S(2)}, u32[]{:S(2)}) collective-permute-start(bf16[512,768]{1,0:T(8,128)(2,1)} %get-tuple-element.126.rest_0_), channel_id=1, source_target_pairs={{0,1},{1,0},{2,3},{3,2},{4,5},{5,4},{6,7},{7,6},{8,9},{9,8},{10,11... | collective-permute-start | bytes 2359304 | tf_op jit(solution)/shard_map/ppermute | solution.py:28
  49.2 24.0 %collective-permute-start.22 = (bf16[2,576,384]{2,1,0:T(8,128)(2,1)S(1)}, bf16[2,576,384]{2,1,0:T(8,128)(2,1)S(1)}, u32[]{:S(2)}, u32[]{:S(2)}) collective-permute-start(bf16[2,576,384]{2,1,0:T(8,128)(2,1)S(1)} %pad_maximum_fusion.1), channel_id=1, source_target_pairs={{0,4},{4,0},{1,5},{5,1},{2,6},{6,2},{3,7},{7,3},{8,12},{12,8},{9,1... | collective-permute-start | bytes 2654216 | tf_op jit(solution)/shard_map/ppermute | solution.py:28
  71.1 15.9 %collective-permute-start.19 = (bf16[2,384,384]{2,1,0:T(8,128)(2,1)S(1)}, bf16[2,384,384]{2,1,0:T(8,128)(2,1)}, u32[]{:S(2)}, u32[]{:S(2)}) collective-permute-start(bf16[2,384,384]{2,1,0:T(8,128)(2,1)S(1)} %pad_maximum_fusion.3), channel_id=1, source_target_pairs={{0,2},{1,3},{2,0},{3,1},{4,6},{5,7},{6,4},{7,5},{8,10},{9,11},{10,... | collective-permute-start | bytes 1769480 | tf_op jit(solution)/shard_map/ppermute | solution.py:28
  71.5 29.8 %collective-permute-start.15 = (bf16[256,768]{1,0:T(8,128)(2,1)}, bf16[256,768]{1,0:T(8,128)(2,1)}, u32[]{:S(2)}, u32[]{:S(2)}) collective-permute-start(bf16[256,768]{1,0:T(8,128)(2,1)} %dynamic-slice_bitcast_fusion), channel_id=1, source_target_pairs={{0,4},{4,0},{1,5},{5,1},{2,6},{6,2},{3,7},{7,3},{8,12},{12,8},{9,1... | collective-permute-start | bytes 1179656 | tf_op jit(solution)/shard_map/ppermute | solution.py:28
  74.3 27.1 %collective-permute-start.23 = (bf16[4,576,384]{2,1,0:T(8,128)(2,1)}, bf16[4,576,384]{2,1,0:T(8,128)(2,1)}, u32[]{:S(2)}, u32[]{:S(2)}) collective-permute-start(bf16[4,576,384]{2,1,0:T(8,128)(2,1)} %constant_dynamic-update-slice_fusion.tail_own), channel_id=1, source_target_pairs={{0,1},{1,0},{2,3},{3,2},{4,5},{5,4},{6,7},{7,6},{8,9},{9,8},{10,11... | collective-permute-start | bytes 5308424 | tf_op jit(solution)/shard_map/ppermute | solution.py:28
  88.3 13.1 %collective-permute-start.20 = (bf16[4,384,384]{2,1,0:T(8,128)(2,1)S(1)}, bf16[4,384,384]{2,1,0:T(8,128)(2,1)S(1)}, u32[]{:S(2)}, u32[]{:S(2)}) collective-permute-start(bf16[4,384,384]{2,1,0:T(8,128)(2,1)S(1)} %pad_maximum_fusion.inner_own), channel_id=1, source_target_pairs={{0,1},{1,0},{2,3},{3,2},{4,5},{5,4},{6,7},{7,6},{8,9},{9,8},{10,11... | collective-permute-start | bytes 3538952 | tf_op jit(solution)/shard_map/ppermute | solution.py:28
  134.9 22.6 %collective-permute-start.27 = (bf16[4,576,384]{2,1,0:T(8,128)(2,1)}, bf16[4,576,384]{2,1,0:T(8,128)(2,1)S(1)}, u32[]{:S(2)}, u32[]{:S(2)}) collective-permute-start(bf16[4,576,384]{2,1,0:T(8,128)(2,1)} %get-tuple-element.151), channel_id=1, source_target_pairs={{0,1},{1,0},{2,3},{3,2},{4,5},{5,4},{6,7},{7,6},{8,9},{9,8},{10,11... | collective-permute-start | bytes 5308424 | tf_op jit(solution)/shard_map/ppermute | solution.py:28
  136.9 12.3 %collective-permute-start.26 = (bf16[4,384,384]{2,1,0:T(8,128)(2,1)}, bf16[4,384,384]{2,1,0:T(8,128)(2,1)}, u32[]{:S(2)}, u32[]{:S(2)}) collective-permute-start(bf16[4,384,384]{2,1,0:T(8,128)(2,1)} %get-tuple-element.148), channel_id=1, source_target_pairs={{0,1},{1,0},{2,3},{3,2},{4,5},{5,4},{6,7},{7,6},{8,9},{9,8},{10,11... | collective-permute-start | bytes 3538952 | tf_op jit(solution)/shard_map/ppermute | solution.py:28
  147.0 32.0 %collective-permute-start.25 = (bf16[2,512,256]{2,1,0:T(8,128)(2,1)}, bf16[2,512,256]{2,1,0:T(8,128)(2,1)}, u32[]{:S(2)}, u32[]{:S(2)}) collective-permute-start(bf16[2,512,256]{2,1,0:T(8,128)(2,1)} %get-tuple-element.142), channel_id=1, source_target_pairs={{0,1},{1,0},{2,3},{3,2},{4,5},{5,4},{6,7},{7,6},{8,9},{9,8},{10,11... | collective-permute-start | bytes 1572872 | tf_op jit(solution)/shard_map/ppermute | solution.py:28
  151.7 27.3 %collective-permute-start.28 = (bf16[2,384,384]{2,1,0:T(8,128)(2,1)}, bf16[2,384,384]{2,1,0:T(8,128)(2,1)}, u32[]{:S(2)}, u32[]{:S(2)}) collective-permute-start(bf16[2,384,384]{2,1,0:T(8,128)(2,1)} %get-tuple-element.243), channel_id=1, source_target_pairs={{0,2},{1,3},{2,0},{3,1},{4,6},{5,7},{6,4},{7,5},{8,10},{9,11},{10,... | collective-permute-start | bytes 1769480 | tf_op jit(solution)/shard_map/ppermute | solution.py:28
  158.9 25.3 %collective-permute-start.29 = (bf16[2,576,384]{2,1,0:T(8,128)(2,1)}, bf16[2,576,384]{2,1,0:T(8,128)(2,1)S(1)}, u32[]{:S(2)}, u32[]{:S(2)}) collective-permute-start(bf16[2,576,384]{2,1,0:T(8,128)(2,1)} %get-tuple-element.241), channel_id=1, source_target_pairs={{0,4},{4,0},{1,5},{5,1},{2,6},{6,2},{3,7},{7,3},{8,12},{12,8},{9,1... | collective-permute-start | bytes 2654216 | tf_op jit(solution)/shard_map/ppermute | solution.py:28
  180.1 20.0 %collective-permute-start.30 = (bf16[1,384,384]{2,1,0:T(8,128)(2,1)S(1)}, bf16[1,384,384]{2,1,0:T(8,128)(2,1)S(1)}, u32[]{:S(2)}, u32[]{:S(2)}) collective-permute-start(bf16[1,384,384]{2,1,0:T(8,128)(2,1)S(1)} %add_convert_fusion.13), channel_id=1, source_target_pairs={{0,4},{4,0},{1,5},{5,1},{2,6},{6,2},{3,7},{7,3},{8,12},{12,8},{9,1... | collective-permute-start | bytes 884744 | tf_op jit(solution)/shard_map/ppermute | solution.py:28
  182.1 56.4 %collective-permute-start.38 = (bf16[1,512,256]{2,1,0:T(8,128)(2,1)}, bf16[1,512,256]{2,1,0:T(8,128)(2,1)}, u32[]{:S(2)}, u32[]{:S(2)}) collective-permute-start(bf16[1,512,256]{2,1,0:T(8,128)(2,1)} %get-tuple-element.255), channel_id=1, source_target_pairs={{0,2},{1,3},{2,0},{3,1},{4,6},{5,7},{6,4},{7,5},{8,10},{9,11},{10,... | collective-permute-start | bytes 786440 | tf_op jit(solution)/shard_map/ppermute | solution.py:28
  185.0 17.2 %collective-permute-start.31 = (bf16[1,576,384]{2,1,0:T(8,128)(2,1)}, bf16[1,576,384]{2,1,0:T(8,128)(2,1)}, u32[]{:S(2)}, u32[]{:S(2)}) collective-permute-start(bf16[1,576,384]{2,1,0:T(8,128)(2,1)} %add_convert_fusion.8), channel_id=1, source_target_pairs={{0,2},{1,3},{2,0},{3,1},{4,6},{5,7},{6,4},{7,5},{8,10},{9,11},{10,... | collective-permute-start | bytes 1327112 | tf_op jit(solution)/shard_map/ppermute | solution.py:28
  195.9 21.4 %collective-permute-start.36 = (bf16[2,8,1152]{2,1,0:T(8,128)(2,1)}, bf16[2,8,1152]{2,1,0:T(8,128)(2,1)}, u32[]{:S(2)}, u32[]{:S(2)}) collective-permute-start(bf16[2,8,1152]{2,1,0:T(8,128)(2,1)} %get-tuple-element.183), channel_id=1, source_target_pairs={{0,3},{1,0},{2,1},{3,2},{4,7},{5,4},{6,5},{7,6},{8,11},{9,8},{10,9... | collective-permute-start | bytes 110600 | tf_op jit(solution)/shard_map/ppermute | solution.py:33
  203.6 18.3 %collective-permute-start.33 = (bf16[480,384]{1,0:T(8,128)(2,1)S(1)}, bf16[480,384]{1,0:T(8,128)(2,1)S(1)}, u32[]{:S(2)}, u32[]{:S(2)}) collective-permute-start(bf16[480,384]{1,0:T(8,128)(2,1)S(1)} %dynamic-slice_bitcast_fusion.3), channel_id=1, source_target_pairs={{0,8},{8,0},{16,24},{24,16},{1,9},{9,1},{17,25},{25,17},{2,10},{10... | collective-permute-start | bytes 1105928 | tf_op jit(solution)/shard_map/ppermute | solution.py:28
  215.4 13.6 %collective-permute-start.35 = (bf16[2,512,256]{2,1,0:T(8,128)(2,1)}, bf16[2,512,256]{2,1,0:T(8,128)(2,1)S(1)}, u32[]{:S(2)}, u32[]{:S(2)}) collective-permute-start(bf16[2,512,256]{2,1,0:T(8,128)(2,1)} %get-tuple-element.178), channel_id=1, source_target_pairs={{0,1},{1,0},{2,3},{3,2},{4,5},{5,4},{6,7},{7,6},{8,9},{9,8},{10,11... | collective-permute-start | bytes 1572872 | tf_op jit(solution)/shard_map/ppermute | solution.py:28
  218.8 19.8 %collective-permute-start.39 = (bf16[1,512,256]{2,1,0:T(8,128)(2,1)S(1)}, bf16[1,512,256]{2,1,0:T(8,128)(2,1)S(1)}, u32[]{:S(2)}, u32[]{:S(2)}) collective-permute-start(bf16[1,512,256]{2,1,0:T(8,128)(2,1)S(1)} %get-tuple-element.253), channel_id=1, source_target_pairs={{0,2},{1,3},{2,0},{3,1},{4,6},{5,7},{6,4},{7,5},{8,10},{9,11},{10,... | collective-permute-start | bytes 786440 | tf_op jit(solution)/shard_map/ppermute | solution.py:28
  222.0 16.5 %collective-permute-start.34 = (bf16[240,384]{1,0:T(8,128)(2,1)S(1)}, bf16[240,384]{1,0:T(8,128)(2,1)S(1)}, u32[]{:S(2)}, u32[]{:S(2)}) collective-permute-start(bf16[240,384]{1,0:T(8,128)(2,1)S(1)} %dynamic-slice_bitcast_fusion.5), channel_id=1, source_target_pairs={{0,16},{8,24},{16,0},{24,8},{1,17},{9,25},{17,1},{25,9},{2,18},{10... | collective-permute-start | bytes 552968 | tf_op jit(solution)/shard_map/ppermute | solution.py:28
  245.4 25.2 %collective-permute-start.24 = (bf16[256,768]{1,0:T(8,128)(2,1)}, bf16[256,768]{1,0:T(8,128)(2,1)}, u32[]{:S(2)}, u32[]{:S(2)}) collective-permute-start(bf16[256,768]{1,0:T(8,128)(2,1)} %get-tuple-element.137), channel_id=1, source_target_pairs={{0,4},{4,0},{1,5},{5,1},{2,6},{6,2},{3,7},{7,3},{8,12},{12,8},{9,1... | collective-permute-start | bytes 1179656 | tf_op jit(solution)/shard_map/ppermute | solution.py:28
  245.4 14.9 %collective-permute-start.53 = (bf16[240,384]{1,0:T(8,128)(2,1)S(1)}, bf16[240,384]{1,0:T(8,128)(2,1)}, u32[]{:S(2)}, u32[]{:S(2)}) collective-permute-start(bf16[240,384]{1,0:T(8,128)(2,1)S(1)} %fusion.5), channel_id=1, source_target_pairs={{0,16},{8,24},{16,0},{24,8},{1,17},{9,25},{17,1},{25,9},{2,18},{10... | collective-permute-start | bytes 552968 | tf_op jit(solution)/shard_map/ppermute | solution.py:28
  254.9 12.7 %collective-permute-start.42 = (bf16[2,288,384]{2,1,0:T(8,128)(2,1)S(1)}, bf16[2,288,384]{2,1,0:T(8,128)(2,1)S(1)}, u32[]{:S(2)}, u32[]{:S(2)}) collective-permute-start(bf16[2,288,384]{2,1,0:T(8,128)(2,1)S(1)} %get-tuple-element.244), channel_id=1, source_target_pairs={{0,2},{1,3},{2,0},{3,1},{4,6},{5,7},{6,4},{7,5},{8,10},{9,11},{10,... | collective-permute-start | bytes 1327112 | tf_op jit(solution)/shard_map/ppermute | solution.py:28
  255.6 12.4 %collective-permute-start.55 = (bf16[112,384]{1,0:T(8,128)(2,1)S(1)}, bf16[112,384]{1,0:T(8,128)(2,1)S(1)}, u32[]{:S(2)}, u32[]{:S(2)}) collective-permute-start(bf16[112,384]{1,0:T(8,128)(2,1)S(1)} %add_convert_fusion.30), channel_id=1, source_target_pairs={{0,4},{4,0},{1,5},{5,1},{2,6},{6,2},{3,7},{7,3},{8,12},{12,8},{9,1... | collective-permute-start | bytes 258056 | tf_op jit(solution)/shard_map/ppermute | solution.py:28
  266.6 17.5 %collective-permute-start.54 = (bf16[480,384]{1,0:T(8,128)(2,1)S(1)}, bf16[480,384]{1,0:T(8,128)(2,1)S(1)}, u32[]{:S(2)}, u32[]{:S(2)}) collective-permute-start(bf16[480,384]{1,0:T(8,128)(2,1)S(1)} %maximum_select_fusion.4), channel_id=1, source_target_pairs={{0,8},{8,0},{16,24},{24,16},{1,9},{9,1},{17,25},{25,17},{2,10},{10... | collective-permute-start | bytes 1105928 | tf_op jit(solution)/shard_map/ppermute | solution.py:28
  270.6 13.4 %collective-permute-start.45 = (bf16[256,768]{1,0:T(8,128)(2,1)S(1)}, bf16[256,768]{1,0:T(8,128)(2,1)S(1)}, u32[]{:S(2)}, u32[]{:S(2)}) collective-permute-start(bf16[256,768]{1,0:T(8,128)(2,1)S(1)} %copy-done.39), channel_id=1, source_target_pairs={{0,4},{4,0},{1,5},{5,1},{2,6},{6,2},{3,7},{7,3},{8,12},{12,8},{9,1... | collective-permute-start | bytes 1179656 | tf_op jit(solution)/shard_map/ppermute | solution.py:28
  (71 other events, 515.2 us)

commit v5 on v4

--- a/solution.py
+++ b/solution.py
@@ -928,10 +928,8 @@
         for dr, dc in list(held):
             held[(dr, dc ^ step)] = swap(held[(dr, dc)], "col", step)
 
-    def trade(pair, *marks):
-        sent = pick(pair, 1 - row_here)
-        if marks:
-            sent = after(sent, *marks)
+    def trade(pair, mark):
+        sent = after(pick(pair, 1 - row_here), mark)
         return pick(pair, row_here), swap(sent, "row", 1)
 
     spread_row(first)
@@ -1061,13 +1059,14 @@
     )
 
     gathered.append(swap(pairs, "col", 1))
+    inner = jnp.concatenate([inner, after(inner_moved, conv_context)], axis=0)
+    cot_sent = pick(cotangent, 1 - row_here)
     for piece in gathered[1 : col_count // 2]:
-        gathered.append(swap(after(piece, conv_context), "col", 1))
-    inner = jnp.concatenate([inner, after(inner_moved, conv_context)], axis=0)
+        gathered.append(swap(after(piece, conv_context, inner, cot_sent), "col", 1))
     for step in far_steps[:-1]:
         inner = grow(inner, "col", step)
     inner_far_moved = swap(inner, "col", far_steps[-1])
-    _, cot_other = trade(cotangent, conv_context)
+    cot_other = swap(after(cot_sent, conv_context), "row", 1)
 
     doc_query = doc_blocks[:2]
     attended = []
@@ -1346,8 +1345,6 @@
     proj_stage = proj_sum.finish()
     wide_sum = wide_sum.rest(proj_stage).astype(WIDE)
     flat_sum.finish(proj_stage)
-    proj_stage = proj_sum.finish()
-    proj_sum = proj_sum.rest().astype(WIDE)
     flat = flat_sum.low.astype(WIDE)
     finals = []
     start = 0
@@ -1356,6 +1353,16 @@
         start += count
     vector_sum, depth_sum, tap_weight_sum, tap_bias_sum, bias_sum, inner_bias_sum = finals
     vector_sum = vector_sum.reshape(6, -1)
+    vectors_out = [vector_sum[row] for row in (5, 3, 4)]
+    vectors_out.append(inner_bias_sum[:, :cut_inner].reshape(-1))
+    vectors_out += [vector_sum[row] for row in (2, 0, 1)]
+    small_out = [
+        depth_sum.reshape(KERNEL, -1),
+        bias_sum,
+        tap_weight_sum.T,
+        tap_bias_sum[0, : HEADS * KERNEL],
+    ]
+    proj_stage = proj_sum.finish(*small_out)
 
     def give_back(here_rows, there_rows, *marks):
         moved = swap(there_rows, "row", 1).astype(here_rows.dtype)
@@ -1365,24 +1372,23 @@
             row_here == 0, jnp.stack([here_rows, moved]), jnp.stack([moved, here_rows])
         )
 
-    return (
-        give_back(out_own, out_other, first_stage),
-        give_back(token_own, token_other, proj_stage),
-        jnp.transpose(proj_sum.reshape(5, cut_proj, lanes), (0, 2, 1)),
+    token_grad = give_back(token_own, token_other, proj_stage)
+    wide_grads = (
         wide_sum[2 * cut_inner :].T,
         wide_sum[:cut_inner].T[None],
         wide_sum[cut_inner : 2 * cut_inner][None],
-        depth_sum.reshape(KERNEL, -1),
-        bias_sum,
-        tap_weight_sum.T,
-        tap_bias_sum[0, : HEADS * KERNEL],
-        vector_sum[5],
-        vector_sum[3],
-        vector_sum[4],
-        inner_bias_sum[:, :cut_inner].reshape(-1),
-        vector_sum[2],
-        vector_sum[0],
-        vector_sum[1],
+    )
+    while len(proj_sum.todo) > 1:
+        proj_sum.finish(*vectors_out)
+    proj_sum = proj_sum.finish(token_grad, *wide_grads).astype(WIDE)
+
+    return (
+        give_back(out_own, out_other, first_stage),
+        token_grad,
+        jnp.transpose(proj_sum.reshape(5, cut_proj, lanes), (0, 2, 1)),
+        *wide_grads,
+        *small_out,
+        *vectors_out,
     )
 
 

time: 318 us -> 313 us (0.984)
  starting transfers between devices: 69.2 us -> 61.1 us
  waiting for transfers between devices: 52.6 us -> 56.5 us
    ppermute x57, starting transfers between devices: 64.4 us -> 57.9 us  [swap(): return lax.ppermute(block, axis, [(i, i ^ step) for i in range(count)])]
    ppermute x57, waiting for transfers between devices: 52.1 us -> 56 us  [swap(): return lax.ppermute(block, axis, [(i, i ^ step) for i in range(count)])]
  transfers between devices with their start and end apart: 59 -> 59, of which waited for: 18 -> 20; matrix products, arithmetic and copies ran while one was open for 16% -> 16% of each run, Pallas kernels for 30% -> 30%
where the time goes in v5:
time: 313 us; the launch traced here: 308 us
  Pallas kernels  131 us (42%)
  starting transfers between devices  61.1 us (20%)
  waiting for transfers between devices  56.5 us (18%)
  other arithmetic  29.5 us (9%)
  local copies, waits for them, and re-layouts  27.5 us (9%)
    pallas_call x13, Pallas kernels, run(): pl.pallas_call(body, grid=(1,), in_specs=specs, out_specs=[pl.BlockSpec(m...  131 us
    ppermute x57, starting transfers between devices, swap(): return lax.ppermute(block, axis, [(i, i ^ step) for i in range(count)])  57.9 us
    ppermute x57, waiting for transfers between devices, swap(): return lax.ppermute(block, axis, [(i, i ^ step) for i in range(count)])  56 us
    convert_element_type x19, other arithmetic, add_low(): return (kept.astype(WIDE) + moved.astype(WIDE)).astype(LOW)  12 us
  transfers between devices with their start and end apart: 59, of which 20 were waited for; matrix products, arithmetic and copies ran while one was open for 16% of the time, Pallas kernels for 30%

profile of v5, /device:TPU:0, one launch (start us, length us, event | category | flops | bytes accessed | tf_op | source)
XLA Modules:
  0.0 308.2 jit_solution(6165953414861738606)
XLA Ops:
  2.5 3.0 collective-permute-start
  18.3 5.8 %collective-permute-done.3.rest_3_ = bf16[304,384]{1,0:T(8,128)(2,1)S(1)} collective-permute-done((bf16[304,384]{1,0:T(8,128)(2,1)S(1)}, bf16[304,384]{1,0:T(8,128)(2,1)S(1)}, u32[]{:S(2)}, u32[]{:S(2)}) %collective-permute-start.3) | collective-permute-done | bytes 233504 | tf_op jit(solution)/shard_map/ppermute | solution.py:28
  24.1 3.1 %collective-permute-done.1.other = bf16[256,768]{1,0:T(8,128)(2,1)S(1)} collective-permute-done((bf16[256,768]{1,0:T(8,128)(2,1)S(1)}, bf16[256,768]{1,0:T(8,128)(2,1)S(1)}, u32[]{:S(2)}, u32[]{:S(2)}) %collective-permute-start.1) | collective-permute-done | bytes 393248 | tf_op jit(solution)/shard_map/ppermute | solution.py:28
  29.5 4.8 %collective-permute-done.8.rest_1_ = bf16[256,384]{1,0:T(8,128)(2,1)} collective-permute-done((bf16[256,384]{1,0:T(8,128)(2,1)S(1)}, bf16[256,384]{1,0:T(8,128)(2,1)}, u32[]{:S(2)}, u32[]{:S(2)}) %collective-permute-start.8) | collective-permute-done | bytes 196640 | tf_op jit(solution)/shard_map/ppermute | solution.py:28
  36.3 5.3 %collective-permute-done.9.rest_2_ = bf16[640,384]{1,0:T(8,128)(2,1)} collective-permute-done((bf16[640,384]{1,0:T(8,128)(2,1)S(1)}, bf16[640,384]{1,0:T(8,128)(2,1)}, u32[]{:S(2)}, u32[]{:S(2)}) %collective-permute-start.9) | collective-permute-done | bytes 491552 | tf_op jit(solution)/shard_map/ppermute | solution.py:28
  41.7 5.1 %shard_map.305 = (bf16[512,384]{1,0:T(8,128)(2,1)}, bf16[512,768]{1,0:T(8,128)(2,1)}, bf16[3,2,384,384]{3,2,1,0:T(8,128)(2,1)}) custom-call(s32[2]{0:T(128)} %pad_add_fusion.4.here, bf16[256,768]{1,0:T(8,128)(2,1)} %get-tuple-element.265.own, bf16[256,768]{1,0:T(8,128)(2,1)} %copy-done.1, f32[4,384]{1,0:T(4,128)} %convert_element_type.378.bias, ...), custom_call_target="tpu_custom_call" | custom-call | flops 50000000 | bytes 180000 | tf_op jit(solution)/shard_map/pallas_call | solution.py:68
  50.6 10.9 %shard_map.306 = (bf16[512,384]{1,0:T(8,128)(2,1)}, bf16[512,768]{1,0:T(8,128)(2,1)}, f32[2,272,384]{2,1,0:T(8,128)}, f32[512,384]{1,0:T(8,128)}, bf16[512,384]{...) custom-call(s32[2]{0:T(128)} %pad_add_fusion.4.here, ...), custom_call_target="tpu_custom_call" | custom-call | flops 11000000512 | bytes 39600000 | tf_op jit(solution)/shard_map/pallas_call | solution.py:68
  61.6 7.1 %collective-permute-done.16.rest_1_ = bf16[512,768]{1,0:T(8,128)(2,1)} collective-permute-done((bf16[512,768]{1,0:T(8,128)(2,1)}, bf16[512,768]{1,0:T(8,128)(2,1)}, u32[]{:S(2)}, u32[]{:S(2)}) %collective-permute-start.16) | collective-permute-done | bytes 786464 | tf_op jit(solution)/shard_map/ppermute | solution.py:28
  75.7 6.6 %shard_map.307 = (bf16[512,128]{1,0:T(8,128)(2,1)}, f32[2,8,256]{2,1,0:T(8,128)}) custom-call(s32[8,2]{1,0:T(8,128)} %pad_add_fusion.bounds, bf16[512,384]{1,0:T(8,128)(2,1)} %get-tuple-element.173.query, s32[2,256]{1,0:T(2,128)} %slice.353.doc_query, s32[8,256,128]{2,1,0:T(8,128)} %broadcast_in_dim.36.doc_key, bf16[512,768]{1,0:T(8,128)(2,1)} %get-tuple-element.129.rest_0_, ...), custom_call_target="tpu_custom_call" | custom-call | flops 8000000000 | bytes 28800000 | tf_op jit(solution)/shard_map/pallas_call | solution.py:68
  82.2 6.1 %collective-permute-done.19 = bf16[2,384,384]{2,1,0:T(8,128)(2,1)} collective-permute-done((bf16[2,384,384]{2,1,0:T(8,128)(2,1)S(1)}, bf16[2,384,384]{2,1,0:T(8,128)(2,1)}, u32[]{:S(2)}, u32[]{:S(2)}) %collective-permute-start.19) | collective-permute-done | bytes 589856 | tf_op jit(solution)/shard_map/ppermute | solution.py:28
  89.6 6.6 %shard_map.309 = (bf16[512,128]{1,0:T(8,128)(2,1)}, f32[2,8,256]{2,1,0:T(8,128)}) custom-call(s32[8,2]{1,0:T(8,128)} %pad_add_fusion.bounds, bf16[512,384]{1,0:T(8,128)(2,1)} %get-tuple-element.173.query, s32[2,256]{1,0:T(2,128)} %slice.353.doc_query, s32[8,256,128]{2,1,0:T(8,128)} %broadcast_in_dim.36.doc_key, bf16[512,768]{1,0:T(8,128)(2,1)} %get-tuple-element.129.rest_0_, ...), custom_call_target="tpu_custom_call" | custom-call | flops 8000000000 | bytes 28800000 | tf_op jit(solution)/shard_map/pallas_call | solution.py:68
  96.3 6.3 %shard_map.308 = (bf16[512,128]{1,0:T(8,128)(2,1)}, f32[2,8,256]{2,1,0:T(8,128)}) custom-call(s32[8,2]{1,0:T(8,128)} %pad_add_fusion.bounds, bf16[512,384]{1,0:T(8,128)(2,1)} %get-tuple-element.173.query, s32[2,256]{1,0:T(2,128)} %slice.353.doc_query, s32[8,256,128]{2,1,0:T(8,128)} %broadcast_in_dim.36.doc_key, bf16[512,768]{1,0:T(8,128)(2,1)} %get-tuple-element.129.rest_0_, ...), custom_call_target="tpu_custom_call" | custom-call | flops 8000000000 | bytes 28800000 | tf_op jit(solution)/shard_map/pallas_call | solution.py:68
  103.6 32.5 %shard_map.310 = (bf16[256,768]{1,0:T(8,128)(2,1)}, bf16[256,768]{1,0:T(8,128)(2,1)}, f32[512,768]{1,0:T(8,128)}, bf16[512,128]{1,0:T(8,128)(2,1)}, bf16[512,128...) custom-call(s32[2]{0:T(128)} %pad_add_fusion.4.here, ...), custom_call_target="tpu_custom_call" | custom-call | flops 30000001024 | bytes 108000000 | tf_op jit(solution)/shard_map/pallas_call | solution.py:68
  138.3 9.9 %shard_map.311 = (f32[512,128]{1,0:T(8,128)}, bf16[2,512,256]{2,1,0:T(8,128)(2,1)}, bf16[2,512,256]{2,1,0:T(8,128)(2,1)}, f32[8,128]{1,0:T(8,128)}) custom-call(s32[8,2]{1,0:T(8,128)} %pad_add_fusion.bounds, bf16[512,384]{1,0:T(8,128)(2,1)} %get-tuple-element.173.query, s32[2,256]{1,0:T(2,128)} %slice.353.doc_query, ...), custom_call_target="tpu_custom_call" | custom-call | flops 12999999488 | bytes 46800000 | tf_op jit(solution)/shard_map/pallas_call | solution.py:68
  150.5 2.5 add_convert_fusion.2
  153.0 6.1 %collective-permute-start.28 = (bf16[2,384,384]{2,1,0:T(8,128)(2,1)}, bf16[2,384,384]{2,1,0:T(8,128)(2,1)}, u32[]{:S(2)}, u32[]{:S(2)}) collective-permute-start(bf16[2,384,384]{2,1,0:T(8,128)(2,1)} %get-tuple-element.249), channel_id=1, source_target_pairs={{0,2},{1,3},{2,0},{3,1},{4,6},{5,7},{6,4},{7,5},{8,10},{9,11},{10,... | collective-permute-start | bytes 1769480 | tf_op jit(solution)/shard_map/ppermute | solution.py:28
  160.4 16.8 %shard_map.312 = (bf16[512,384]{1,0:T(8,128)(2,1)}, f32[512,384]{1,0:T(8,128)}, f32[128,384]{1,0:T(8,128)}, f32[8,128]{1,0:T(8,128)}, f32[16,768]{1,0:T(8,128)},...) custom-call(bf16[256,768]{1,0:T(8,128)(2,1)} %get-tuple-element.265., ...), custom_call_target="tpu_custom_call" | custom-call | flops 16000000000 | bytes 57600000 | tf_op jit(solution)/shard_map/pallas_call | solution.py:68
  185.2 9.9 %shard_map.313 = (f32[512,128]{1,0:T(8,128)}, bf16[2,512,256]{2,1,0:T(8,128)(2,1)}, bf16[2,512,256]{2,1,0:T(8,128)(2,1)}, f32[8,128]{1,0:T(8,128)}) custom-call(s32[8,2]{1,0:T(8,128)} %pad_add_fusion.bounds, bf16[512,384]{1,0:T(8,128)(2,1)} %get-tuple-element.173.query, s32[2,256]{1,0:T(2,128)} %slice.353.doc_query, ...), custom_call_target="tpu_custom_call" | custom-call | flops 12999999488 | bytes 46800000 | tf_op jit(solution)/shard_map/pallas_call | solution.py:68
  195.6 2.7 collective-permute-start.36
  204.7 10.1 %shard_map.314 = (f32[512,128]{1,0:T(8,128)}, bf16[2,512,256]{2,1,0:T(8,128)(2,1)}, bf16[2,512,256]{2,1,0:T(8,128)(2,1)}, f32[8,128]{1,0:T(8,128)}) custom-call(s32[8,2]{1,0:T(8,128)} %pad_add_fusion.bounds, bf16[512,384]{1,0:T(8,128)(2,1)} %get-tuple-element.173.query, s32[2,256]{1,0:T(2,128)} %slice.353.doc_query, ...), custom_call_target="tpu_custom_call" | custom-call | flops 12999999488 | bytes 46800000 | tf_op jit(solution)/shard_map/pallas_call | solution.py:68
  216.9 3.4 %collective-permute-start.39 = (bf16[1,512,256]{2,1,0:T(8,128)(2,1)S(1)}, bf16[1,512,256]{2,1,0:T(8,128)(2,1)S(1)}, u32[]{:S(2)}, u32[]{:S(2)}) collective-permute-start(bf16[1,512,256]{2,1,0:T(8,128)(2,1)S(1)} %get-tuple-element.259), channel_id=1, source_target_pairs={{0,2},{1,3},{2,0},{3,1},{4,6},{5,7},{6,4},{7,5},{8,10},{9,11},{10,... | collective-permute-start | bytes 786440 | tf_op jit(solution)/shard_map/ppermute | solution.py:28
  221.5 6.6 %shard_map.315 = (bf16[4,192,384]{2,1,0:T(8,128)(2,1)}, bf16[4,192,384]{2,1,0:T(8,128)(2,1)}, f32[512,768]{1,0:T(8,128)}, bf16[112,384]{1,0:T(8,128)(2,1)}) custom-call(s32[2]{0:T(128)} %pad_add_fusion.4.here, bf16[256,768]{1,0:T(8,128)(2,1)} %get-tuple-element.265.own, bf16[256,768]{1,0:T(8,128)(2,1)} %copy-done.1, ...), custom_call_target="tpu_custom_call" | custom-call | flops 6000000000 | bytes 21600000 | tf_op jit(solution)/shard_map/pallas_call | solution.py:68
  228.1 2.3 collective-permute-done.34
  233.1 5.5 %shard_map.316 = (bf16[4,288,384]{2,1,0:T(8,128)(2,1)}, bf16[4,288,384]{2,1,0:T(8,128)(2,1)}, bf16[3,512,384]{2,1,0:T(8,128)(2,1)}) custom-call(s32[2]{0:T(128)} %pad_add_fusion.4.here, bf16[256,768]{1,0:T(8,128)(2,1)} %get-tuple-element.265.own, bf16[256,768]{1,0:T(8,128)(2,1)} %copy-done.1, f32[512,128]{1,0:T(8,128)} %get-tuple-element.143.grad_0, ...), custom_call_target="tpu_custom_call" | custom-call | flops 50000000 | bytes 180000 | tf_op jit(solution)/shard_map/pallas_call | solution.py:68
  239.2 7.2 %collective-permute-start.24 = (bf16[256,768]{1,0:T(8,128)(2,1)}, bf16[256,768]{1,0:T(8,128)(2,1)}, u32[]{:S(2)}, u32[]{:S(2)}) collective-permute-start(bf16[256,768]{1,0:T(8,128)(2,1)} %get-tuple-element.140), channel_id=1, source_target_pairs={{0,4},{4,0},{1,5},{5,1},{2,6},{6,2},{3,7},{7,3},{8,12},{12,8},{9,1... | collective-permute-start | bytes 1179656 | tf_op jit(solution)/shard_map/ppermute | solution.py:28
  246.4 4.4 %collective-permute-start.52 = (bf16[240,384]{1,0:T(8,128)(2,1)S(1)}, bf16[240,384]{1,0:T(8,128)(2,1)}, u32[]{:S(2)}, u32[]{:S(2)}) collective-permute-start(bf16[240,384]{1,0:T(8,128)(2,1)S(1)} %fusion.5), channel_id=1, source_target_pairs={{0,16},{8,24},{16,0},{24,8},{1,17},{9,25},{17,1},{25,9},{2,18},{10... | collective-permute-start | bytes 552968 | tf_op jit(solution)/shard_map/ppermute | solution.py:28
  256.7 4.6 %shard_map.317 = (f32[256,768]{1,0:T(8,128)}, bf16[256,768]{1,0:T(8,128)(2,1)}) custom-call(bf16[3,2,384,384]{3,2,1,0:T(8,128)(2,1)} %get-tuple-element.204.w_full, bf16[3,512,384]{2,1,0:T(8,128)(2,1)} %get-tuple-element.205.lows, f32[512,768]{1,0:T(8,128)} %get-tuple-element.211.token_in), custom_call_target="tpu_custom_call" | custom-call | flops 50000000 | bytes 180000 | tf_op jit(solution)/shard_map/pallas_call | solution.py:68
  264.4 2.6 collective-permute-done.42
  277.5 2.4 collective-permute-done.54
  279.9 2.7 collective-permute-start.55
  290.6 4.7 %collective-permute-done.50 = bf16[120,384]{1,0:T(8,128)(2,1)S(1)} collective-permute-done((bf16[120,384]{1,0:T(8,128)(2,1)S(1)}, bf16[120,384]{1,0:T(8,128)(2,1)S(1)}, u32[]{:S(2)}, u32[]{:S(2)}) %collective-permute-start.50) | collective-permute-done | bytes 92192 | tf_op jit(solution)/shard_map/ppermute | solution.py:28
  304.3 2.4 collective-permute-done.57
  (301 shorter events, 95.8 us)
Async XLA Ops:
  2.5 13.3 %collective-permute-start = (bf16[304,384]{1,0:T(8,128)(2,1)S(1)}, bf16[304,384]{1,0:T(8,128)(2,1)S(1)}, u32[]{:S(2)}, u32[]{:S(2)}) collective-permute-start(bf16[304,384]{1,0:T(8,128)(2,1)S(1)} %fusion.7.rest_0_), channel_id=1, source_target_pairs={{0,4},{4,0},{1,5},{5,1},{2,6},{6,2},{3,7},{7,3},{8,12},{12,8},{9,1... | collective-permute-start | bytes 700424 | tf_op jit(solution)/shard_map/ppermute | solution.py:28
  27.4 14.3 %collective-permute-start.9 = (bf16[640,384]{1,0:T(8,128)(2,1)S(1)}, bf16[640,384]{1,0:T(8,128)(2,1)}, u32[]{:S(2)}, u32[]{:S(2)}) collective-permute-start(bf16[640,384]{1,0:T(8,128)(2,1)S(1)} %pad_maximum_fusion.4), channel_id=1, source_target_pairs={{0,4},{4,0},{1,5},{5,1},{2,6},{6,2},{3,7},{7,3},{8,12},{12,8},{9,1... | collective-permute-start | bytes 1474568 | tf_op jit(solution)/shard_map/ppermute | solution.py:28
  28.3 20.8 %collective-permute-start.11 = (bf16[256,384]{1,0:T(8,128)(2,1)S(1)}, bf16[256,384]{1,0:T(8,128)(2,1)}, u32[]{:S(2)}, u32[]{:S(2)}) collective-permute-start(bf16[256,384]{1,0:T(8,128)(2,1)S(1)} %pad_maximum_fusion.7.rest_0_), channel_id=1, source_target_pairs={{0,1},{1,0},{2,3},{3,2},{4,5},{5,4},{6,7},{7,6},{8,9},{9,8},{10,11... | collective-permute-start | bytes 589832 | tf_op jit(solution)/shard_map/ppermute | solution.py:28
  34.3 14.1 %collective-permute-start.21 = (bf16[1,576,384]{2,1,0:T(8,128)(2,1)S(1)}, bf16[1,576,384]{2,1,0:T(8,128)(2,1)S(1)}, u32[]{:S(2)}, u32[]{:S(2)}) collective-permute-start(bf16[1,576,384]{2,1,0:T(8,128)(2,1)S(1)} %bitcast.107), channel_id=1, source_target_pairs={{0,2},{1,3},{2,0},{3,1},{4,6},{5,7},{6,4},{7,5},{8,10},{9,11},{10,... | collective-permute-start | bytes 1327112 | tf_op jit(solution)/shard_map/ppermute | solution.py:28
  34.8 12.6 %collective-permute-start.10 = (bf16[256,384]{1,0:T(8,128)(2,1)}, bf16[256,384]{1,0:T(8,128)(2,1)}, u32[]{:S(2)}, u32[]{:S(2)}) collective-permute-start(bf16[256,384]{1,0:T(8,128)(2,1)} %collective-permute-done.8.rest_1_), channel_id=1, source_target_pairs={{0,4},{4,0},{1,5},{5,1},{2,6},{6,2},{3,7},{7,3},{8,12},{12,8},{9,1... | collective-permute-start | bytes 589832 | tf_op jit(solution)/shard_map/ppermute | solution.py:28
  48.5 20.3 %collective-permute-start.16 = (bf16[512,768]{1,0:T(8,128)(2,1)}, bf16[512,768]{1,0:T(8,128)(2,1)}, u32[]{:S(2)}, u32[]{:S(2)}) collective-permute-start(bf16[512,768]{1,0:T(8,128)(2,1)} %get-tuple-element.129.rest_0_), channel_id=1, source_target_pairs={{0,2},{1,3},{2,0},{3,1},{4,6},{5,7},{6,4},{7,5},{8,10},{9,11},{10,... | collective-permute-start | bytes 2359304 | tf_op jit(solution)/shard_map/ppermute | solution.py:28
  49.2 25.2 %collective-permute-start.17 = (bf16[512,768]{1,0:T(8,128)(2,1)}, bf16[512,768]{1,0:T(8,128)(2,1)}, u32[]{:S(2)}, u32[]{:S(2)}) collective-permute-start(bf16[512,768]{1,0:T(8,128)(2,1)} %get-tuple-element.129.rest_0_), channel_id=1, source_target_pairs={{0,1},{1,0},{2,3},{3,2},{4,5},{5,4},{6,7},{7,6},{8,9},{9,8},{10,11... | collective-permute-start | bytes 2359304 | tf_op jit(solution)/shard_map/ppermute | solution.py:28
  49.4 23.9 %collective-permute-start.22 = (bf16[2,576,384]{2,1,0:T(8,128)(2,1)S(1)}, bf16[2,576,384]{2,1,0:T(8,128)(2,1)S(1)}, u32[]{:S(2)}, u32[]{:S(2)}) collective-permute-start(bf16[2,576,384]{2,1,0:T(8,128)(2,1)S(1)} %pad_maximum_fusion.1), channel_id=1, source_target_pairs={{0,4},{4,0},{1,5},{5,1},{2,6},{6,2},{3,7},{7,3},{8,12},{12,8},{9,1... | collective-permute-start | bytes 2654216 | tf_op jit(solution)/shard_map/ppermute | solution.py:28
  72.5 15.8 %collective-permute-start.19 = (bf16[2,384,384]{2,1,0:T(8,128)(2,1)S(1)}, bf16[2,384,384]{2,1,0:T(8,128)(2,1)}, u32[]{:S(2)}, u32[]{:S(2)}) collective-permute-start(bf16[2,384,384]{2,1,0:T(8,128)(2,1)S(1)} %pad_maximum_fusion.3), channel_id=1, source_target_pairs={{0,2},{1,3},{2,0},{3,1},{4,6},{5,7},{6,4},{7,5},{8,10},{9,11},{10,... | collective-permute-start | bytes 1769480 | tf_op jit(solution)/shard_map/ppermute | solution.py:28
  73.0 29.6 %collective-permute-start.15 = (bf16[256,768]{1,0:T(8,128)(2,1)S(1)}, bf16[256,768]{1,0:T(8,128)(2,1)}, u32[]{:S(2)}, u32[]{:S(2)}) collective-permute-start(bf16[256,768]{1,0:T(8,128)(2,1)S(1)} %dynamic-slice_bitcast_fusion), channel_id=1, source_target_pairs={{0,4},{4,0},{1,5},{5,1},{2,6},{6,2},{3,7},{7,3},{8,12},{12,8},{9,1... | collective-permute-start | bytes 1179656 | tf_op jit(solution)/shard_map/ppermute | solution.py:28
  74.3 28.2 %collective-permute-start.23 = (bf16[4,576,384]{2,1,0:T(8,128)(2,1)}, bf16[4,576,384]{2,1,0:T(8,128)(2,1)}, u32[]{:S(2)}, u32[]{:S(2)}) collective-permute-start(bf16[4,576,384]{2,1,0:T(8,128)(2,1)} %constant_dynamic-update-slice_fusion.tail_own), channel_id=1, source_target_pairs={{0,1},{1,0},{2,3},{3,2},{4,5},{5,4},{6,7},{7,6},{8,9},{9,8},{10,11... | collective-permute-start | bytes 5308424 | tf_op jit(solution)/shard_map/ppermute | solution.py:28
  89.5 13.0 %collective-permute-start.20 = (bf16[4,384,384]{2,1,0:T(8,128)(2,1)S(1)}, bf16[4,384,384]{2,1,0:T(8,128)(2,1)S(1)}, u32[]{:S(2)}, u32[]{:S(2)}) collective-permute-start(bf16[4,384,384]{2,1,0:T(8,128)(2,1)S(1)} %pad_maximum_fusion.inner_own), channel_id=1, source_target_pairs={{0,1},{1,0},{2,3},{3,2},{4,5},{5,4},{6,7},{7,6},{8,9},{9,8},{10,11... | collective-permute-start | bytes 3538952 | tf_op jit(solution)/shard_map/ppermute | solution.py:28
  136.1 22.9 %collective-permute-start.27 = (bf16[4,576,384]{2,1,0:T(8,128)(2,1)}, bf16[4,576,384]{2,1,0:T(8,128)(2,1)S(1)}, u32[]{:S(2)}, u32[]{:S(2)}) collective-permute-start(bf16[4,576,384]{2,1,0:T(8,128)(2,1)} %get-tuple-element.154), channel_id=1, source_target_pairs={{0,1},{1,0},{2,3},{3,2},{4,5},{5,4},{6,7},{7,6},{8,9},{9,8},{10,11... | collective-permute-start | bytes 5308424 | tf_op jit(solution)/shard_map/ppermute | solution.py:28
  138.2 12.3 %collective-permute-start.26 = (bf16[4,384,384]{2,1,0:T(8,128)(2,1)}, bf16[4,384,384]{2,1,0:T(8,128)(2,1)}, u32[]{:S(2)}, u32[]{:S(2)}) collective-permute-start(bf16[4,384,384]{2,1,0:T(8,128)(2,1)} %get-tuple-element.151), channel_id=1, source_target_pairs={{0,1},{1,0},{2,3},{3,2},{4,5},{5,4},{6,7},{7,6},{8,9},{9,8},{10,11... | collective-permute-start | bytes 3538952 | tf_op jit(solution)/shard_map/ppermute | solution.py:28
  148.3 28.9 %collective-permute-start.25 = (bf16[2,512,256]{2,1,0:T(8,128)(2,1)}, bf16[2,512,256]{2,1,0:T(8,128)(2,1)}, u32[]{:S(2)}, u32[]{:S(2)}) collective-permute-start(bf16[2,512,256]{2,1,0:T(8,128)(2,1)} %get-tuple-element.145), channel_id=1, source_target_pairs={{0,1},{1,0},{2,3},{3,2},{4,5},{5,4},{6,7},{7,6},{8,9},{9,8},{10,11... | collective-permute-start | bytes 1572872 | tf_op jit(solution)/shard_map/ppermute | solution.py:28
  153.0 24.2 %collective-permute-start.28 = (bf16[2,384,384]{2,1,0:T(8,128)(2,1)}, bf16[2,384,384]{2,1,0:T(8,128)(2,1)}, u32[]{:S(2)}, u32[]{:S(2)}) collective-permute-start(bf16[2,384,384]{2,1,0:T(8,128)(2,1)} %get-tuple-element.249), channel_id=1, source_target_pairs={{0,2},{1,3},{2,0},{3,1},{4,6},{5,7},{6,4},{7,5},{8,10},{9,11},{10,... | collective-permute-start | bytes 1769480 | tf_op jit(solution)/shard_map/ppermute | solution.py:28
  160.4 22.7 %collective-permute-start.29 = (bf16[2,576,384]{2,1,0:T(8,128)(2,1)}, bf16[2,576,384]{2,1,0:T(8,128)(2,1)S(1)}, u32[]{:S(2)}, u32[]{:S(2)}) collective-permute-start(bf16[2,576,384]{2,1,0:T(8,128)(2,1)} %get-tuple-element.247), channel_id=1, source_target_pairs={{0,4},{4,0},{1,5},{5,1},{2,6},{6,2},{3,7},{7,3},{8,12},{12,8},{9,1... | collective-permute-start | bytes 2654216 | tf_op jit(solution)/shard_map/ppermute | solution.py:28
  178.3 20.0 %collective-permute-start.30 = (bf16[1,384,384]{2,1,0:T(8,128)(2,1)S(1)}, bf16[1,384,384]{2,1,0:T(8,128)(2,1)S(1)}, u32[]{:S(2)}, u32[]{:S(2)}) collective-permute-start(bf16[1,384,384]{2,1,0:T(8,128)(2,1)S(1)} %add_convert_fusion.13), channel_id=1, source_target_pairs={{0,4},{4,0},{1,5},{5,1},{2,6},{6,2},{3,7},{7,3},{8,12},{12,8},{9,1... | collective-permute-start | bytes 884744 | tf_op jit(solution)/shard_map/ppermute | solution.py:28
  182.3 48.2 %collective-permute-start.38 = (bf16[1,512,256]{2,1,0:T(8,128)(2,1)}, bf16[1,512,256]{2,1,0:T(8,128)(2,1)}, u32[]{:S(2)}, u32[]{:S(2)}) collective-permute-start(bf16[1,512,256]{2,1,0:T(8,128)(2,1)} %get-tuple-element.261), channel_id=1, source_target_pairs={{0,2},{1,3},{2,0},{3,1},{4,6},{5,7},{6,4},{7,5},{8,10},{9,11},{10,... | collective-permute-start | bytes 786440 | tf_op jit(solution)/shard_map/ppermute | solution.py:28
  184.0 16.5 %collective-permute-start.31 = (bf16[1,576,384]{2,1,0:T(8,128)(2,1)}, bf16[1,576,384]{2,1,0:T(8,128)(2,1)}, u32[]{:S(2)}, u32[]{:S(2)}) collective-permute-start(bf16[1,576,384]{2,1,0:T(8,128)(2,1)} %add_convert_fusion.8), channel_id=1, source_target_pairs={{0,2},{1,3},{2,0},{3,1},{4,6},{5,7},{6,4},{7,5},{8,10},{9,11},{10,... | collective-permute-start | bytes 1327112 | tf_op jit(solution)/shard_map/ppermute | solution.py:28
  195.6 19.9 %collective-permute-start.36 = (bf16[2,8,1152]{2,1,0:T(8,128)(2,1)}, bf16[2,8,1152]{2,1,0:T(8,128)(2,1)}, u32[]{:S(2)}, u32[]{:S(2)}) collective-permute-start(bf16[2,8,1152]{2,1,0:T(8,128)(2,1)} %get-tuple-element.186), channel_id=1, source_target_pairs={{0,3},{1,0},{2,1},{3,2},{4,7},{5,4},{6,5},{7,6},{8,11},{9,8},{10,9... | collective-permute-start | bytes 110600 | tf_op jit(solution)/shard_map/ppermute | solution.py:33
  201.8 18.6 %collective-permute-start.33 = (bf16[480,384]{1,0:T(8,128)(2,1)S(1)}, bf16[480,384]{1,0:T(8,128)(2,1)S(1)}, u32[]{:S(2)}, u32[]{:S(2)}) collective-permute-start(bf16[480,384]{1,0:T(8,128)(2,1)S(1)} %dynamic-slice_bitcast_fusion.3), channel_id=1, source_target_pairs={{0,8},{8,0},{16,24},{24,16},{1,9},{9,1},{17,25},{25,17},{2,10},{10... | collective-permute-start | bytes 1105928 | tf_op jit(solution)/shard_map/ppermute | solution.py:28
  216.9 13.5 %collective-permute-start.39 = (bf16[1,512,256]{2,1,0:T(8,128)(2,1)S(1)}, bf16[1,512,256]{2,1,0:T(8,128)(2,1)S(1)}, u32[]{:S(2)}, u32[]{:S(2)}) collective-permute-start(bf16[1,512,256]{2,1,0:T(8,128)(2,1)S(1)} %get-tuple-element.259), channel_id=1, source_target_pairs={{0,2},{1,3},{2,0},{3,1},{4,6},{5,7},{6,4},{7,5},{8,10},{9,11},{10,... | collective-permute-start | bytes 786440 | tf_op jit(solution)/shard_map/ppermute | solution.py:28
  238.6 15.0 %collective-permute-start.41 = (bf16[4,288,384]{2,1,0:T(8,128)(2,1)}, bf16[4,288,384]{2,1,0:T(8,128)(2,1)S(1)}, u32[]{:S(2)}, u32[]{:S(2)}) collective-permute-start(bf16[4,288,384]{2,1,0:T(8,128)(2,1)} %get-tuple-element.203), channel_id=1, source_target_pairs={{0,1},{1,0},{2,3},{3,2},{4,5},{5,4},{6,7},{7,6},{8,9},{9,8},{10,11... | collective-permute-start | bytes 2654216 | tf_op jit(solution)/shard_map/ppermute | solution.py:28
  238.6 12.3 %collective-permute-start.43 = (bf16[4,192,384]{2,1,0:T(8,128)(2,1)}, bf16[4,192,384]{2,1,0:T(8,128)(2,1)S(1)}, u32[]{:S(2)}, u32[]{:S(2)}) collective-permute-start(bf16[4,192,384]{2,1,0:T(8,128)(2,1)} %get-tuple-element.207), channel_id=1, source_target_pairs={{0,1},{1,0},{2,3},{3,2},{4,5},{5,4},{6,7},{7,6},{8,9},{9,8},{10,11... | collective-permute-start | bytes 1769480 | tf_op jit(solution)/shard_map/ppermute | solution.py:28
  239.1 11.8 %collective-permute-start.44 = (bf16[112,384]{1,0:T(8,128)(2,1)S(1)}, bf16[112,384]{1,0:T(8,128)(2,1)S(1)}, u32[]{:S(2)}, u32[]{:S(2)}) collective-permute-start(bf16[112,384]{1,0:T(8,128)(2,1)S(1)} %copy-done.24), channel_id=1, source_target_pairs={{0,1},{1,0},{2,3},{3,2},{4,5},{5,4},{6,7},{7,6},{8,9},{9,8},{10,11... | collective-permute-start | bytes 258056 | tf_op jit(solution)/shard_map/ppermute | solution.py:28
  239.2 32.5 %collective-permute-start.24 = (bf16[256,768]{1,0:T(8,128)(2,1)}, bf16[256,768]{1,0:T(8,128)(2,1)}, u32[]{:S(2)}, u32[]{:S(2)}) collective-permute-start(bf16[256,768]{1,0:T(8,128)(2,1)} %get-tuple-element.140), channel_id=1, source_target_pairs={{0,4},{4,0},{1,5},{5,1},{2,6},{6,2},{3,7},{7,3},{8,12},{12,8},{9,1... | collective-permute-start | bytes 1179656 | tf_op jit(solution)/shard_map/ppermute | solution.py:28
  246.4 14.9 %collective-permute-start.52 = (bf16[240,384]{1,0:T(8,128)(2,1)S(1)}, bf16[240,384]{1,0:T(8,128)(2,1)}, u32[]{:S(2)}, u32[]{:S(2)}) collective-permute-start(bf16[240,384]{1,0:T(8,128)(2,1)S(1)} %fusion.5), channel_id=1, source_target_pairs={{0,16},{8,24},{16,0},{24,8},{1,17},{9,25},{17,1},{25,9},{2,18},{10... | collective-permute-start | bytes 552968 | tf_op jit(solution)/shard_map/ppermute | solution.py:28
  253.9 13.1 %collective-permute-start.42 = (bf16[2,288,384]{2,1,0:T(8,128)(2,1)S(1)}, bf16[2,288,384]{2,1,0:T(8,128)(2,1)S(1)}, u32[]{:S(2)}, u32[]{:S(2)}) collective-permute-start(bf16[2,288,384]{2,1,0:T(8,128)(2,1)S(1)} %get-tuple-element.250), channel_id=1, source_target_pairs={{0,2},{1,3},{2,0},{3,1},{4,6},{5,7},{6,4},{7,5},{8,10},{9,11},{10,... | collective-permute-start | bytes 1327112 | tf_op jit(solution)/shard_map/ppermute | solution.py:28
  254.6 14.5 %collective-permute-start.51 = (bf16[112,384]{1,0:T(8,128)(2,1)S(1)}, bf16[112,384]{1,0:T(8,128)(2,1)S(1)}, u32[]{:S(2)}, u32[]{:S(2)}) collective-permute-start(bf16[112,384]{1,0:T(8,128)(2,1)S(1)} %add_convert_fusion.30), channel_id=1, source_target_pairs={{0,4},{4,0},{1,5},{5,1},{2,6},{6,2},{3,7},{7,3},{8,12},{12,8},{9,1... | collective-permute-start | bytes 258056 | tf_op jit(solution)/shard_map/ppermute | solution.py:28
  262.5 20.5 %collective-permute-start.58 = (bf16[480,384]{1,0:T(8,128)(2,1)S(1)}, bf16[480,384]{1,0:T(8,128)(2,1)S(1)}, u32[]{:S(2)}, u32[]{:S(2)}) collective-permute-start(bf16[480,384]{1,0:T(8,128)(2,1)S(1)} %maximum_select_fusion.3), channel_id=1, source_target_pairs={{0,8},{8,0},{16,24},{24,16},{1,9},{9,1},{17,25},{25,17},{2,10},{10... | collective-permute-start | bytes 1105928 | tf_op jit(solution)/shard_map/ppermute | solution.py:28
  269.8 12.8 %collective-permute-start.45 = (bf16[256,768]{1,0:T(8,128)(2,1)S(1)}, bf16[256,768]{1,0:T(8,128)(2,1)S(1)}, u32[]{:S(2)}, u32[]{:S(2)}) collective-permute-start(bf16[256,768]{1,0:T(8,128)(2,1)S(1)} %copy-done.39), channel_id=1, source_target_pairs={{0,4},{4,0},{1,5},{5,1},{2,6},{6,2},{3,7},{7,3},{8,12},{12,8},{9,1... | collective-permute-start | bytes 1179656 | tf_op jit(solution)/shard_map/ppermute | solution.py:28
  (69 other events, 581.7 us)
